TPU v7x, 1024 devices: a whole 4x8x16 slice. The times are simulated.
1024 devices in a mesh: blk: 32 (over x_hi, y, core), panel: 32 (over z, x_lo).
Axes of the slice: x: 4 (x_hi: 2, x_lo: 2; x = x_hi * 2 + x_lo), y: 8, z: 16, core: 2. Of those that a mesh axis runs over, the one named last changes fastest.
Arguments:
- integrals: bfloat16 [8192, 32768], P('blk', 'panel'), may hold values from -0.09375 to 0.09375
- amplitudes: bfloat16 [1600, 32768], P('blk', 'panel'), may hold values from -6 to 6
- ab_irrep: int32 [128], P('blk'), may hold values from 0 to 7
- cd_irrep: int32 [512], P('panel'), may hold values from 0 to 7
- occ_irrep: int32 [40], replicated, may hold values from 0 to 7
Outputs:
- ladder: float32 [8192, 1600], P(('blk', 'panel'))
Inputs may be any that keep to these rules, and one draw needn't show every extreme that they name: `ab_irrep`: irreps of virtual pair tiles. `cd_irrep`: irreps of virtual pair tiles.
All inputs are finite; a program needn't handle non-finite values.
Results may differ from a plain program's by a relative error of at most 0.0003.
Values may be sent and summed in bfloat16 or wider, within the bound.
No kernel may reach another device: no remote copies, remote signals or barrier semaphores. Data moves between devices by JAX's collectives and lax.ppermute only.
A program may use at most 64 MiB of HBM per device.

v0:
```python
import jax
import jax.numpy as jnp
from jax import lax
from jax.sharding import Mesh
from jax.sharding import PartitionSpec as P

TW = 64
OCC = 40
BLK = ("blk_0", "blk_1", "blk_2")
BLK_PANEL = ("blk_0", "blk_1", "blk_2", "panel")


def joined_along(tiles, dim):
    tiles = jnp.moveaxis(tiles, 0, dim)
    lengths = tiles.shape
    return tiles.reshape(*lengths[:dim], lengths[dim] * lengths[dim + 1], *lengths[dim + 2 :])


def stacked_from(array, axes, turns):
    tiles = array[None]
    for k in turns:
        tiles = lax.all_gather(tiles, axes[k], axis=0, tiled=True)
    carried = [lax.axis_size(axes[k]) for k in reversed(turns)]
    tiles = tiles.reshape(*carried, *array.shape)
    turned = sorted(range(len(turns)), key=lambda place: turns[len(turns) - 1 - place])
    return tiles.transpose(*turned, *range(len(turns), tiles.ndim)).reshape(-1, *array.shape)


def whole_of(array, axes, turns, dim):
    return joined_along(stacked_from(array, axes, turns), dim)


def split_up(array, dim, length):
    lengths = array.shape
    tiles = array.reshape(*lengths[:dim], length, lengths[dim] // length, *lengths[dim + 1 :])
    return jnp.moveaxis(tiles, dim, 0)


def sum_at_owner(array, axis, dim):
    tiles = split_up(array, dim, lax.axis_size(axis))
    arrived = lax.all_to_all(tiles, axis, split_axis=0, concat_axis=0, tiled=True)
    return arrived.sum(axis=0)


def lookup_irrep(position, occ_irrep):
    orbitals = jnp.arange(OCC, dtype=jnp.int32)
    hits = position[:, None] == orbitals[None, :]
    return jnp.sum(jnp.where(hits, occ_irrep[None, :], 0), axis=1)


def contract(left, right):
    return lax.dot_general(
        left, right, (((1,), (1,)), ((), ())), preferred_element_type=jnp.float32
    )


def body(integrals, amplitudes, ab_irrep, cd_irrep, occ_irrep):
    pair_count = amplitudes.shape[0]
    row_irrep = jnp.repeat(ab_irrep, TW)
    col_irrep = jnp.repeat(cd_irrep, TW)
    pair_index = lax.axis_index(BLK) * pair_count + jnp.arange(pair_count, dtype=jnp.int32)
    pair_irrep = jnp.bitwise_xor(
        lookup_irrep(pair_index // OCC, occ_irrep), lookup_irrep(pair_index % OCC, occ_irrep)
    )
    masked = jnp.where(
        pair_irrep[:, None] == col_irrep[None, :], amplitudes, jnp.zeros((), amplitudes.dtype)
    )
    tpiece = whole_of(masked, BLK, (0, 1, 2), 0)
    piece_irreps = whole_of(pair_irrep, BLK, (0, 1, 2), 0)
    product = contract(integrals, tpiece)
    product = jnp.where(row_irrep[:, None] == piece_irreps[None, :], product, 0.0)
    return sum_at_owner(product, "panel", 0)


def solution(mesh):
    split = Mesh(
        mesh.devices.reshape(2, 8, 2, mesh.shape["panel"]), ("blk_0", "blk_1", "blk_2", "panel")
    )
    return jax.shard_map(
        body,
        mesh=split,
        in_specs=(P(BLK, "panel"), P(BLK, "panel"), P(BLK), P("panel"), P()),
        out_specs=P(BLK_PANEL, None),
        check_vma=False,
    )
```

profile of v0, /device:TPU:2, one launch (start us, length us, event | category | flops | bytes accessed | tf_op | source)
XLA Modules:
  0.0 233.9 jit_solution(16954615058495775572)
XLA Ops:
  6.6 0.8 broadcast_in_dim.44
  7.3 0.1 eq.72
  7.4 1.3 dynamic-slice
  9.3 0.7 select_reduce_fusion
  10.1 0.1 fusion.3
  10.2 1.0 fusion.1
  11.2 7.2 %all-gather.3 = bf16[2,50,1024]{2,1,0:T(8,128)(2,1)} all-gather(bf16[1,50,1024]{2,1,0:T(8,128)(2,1)S(1)} %fusion.1), channel_id=3, replica_groups=mesh['blk_0'=2,'blk_1'=8,'blk_2'=2,'panel'=32] {'blk_0'}, dimensions={0}, use_global_device_ids=true | all-gather | bytes 307200 | tf_op jit(solution)/shard_map/all_gather | solution.py:22
  18.4 56.0 %all-gather.7.cloned.1.call-done = bf16[16,50,1024]{2,1,0:T(8,128)(2,1)} async-done(((bf16[2,50,1024]{2,1,0:T(8,128)(2,1)}), bf16[16,50,1024]{2,1,0:T(8,128)(2,1)}) %all-gather.7.cloned.1.call-update) | async-done | bytes 1638416 | tf_op jit(solution)/shard_map/all_gather | solution.py:22
  74.5 3.6 %copy.16 = bf16[16,50,1024]{2,0,1:T(8,128)(2,1)} copy(bf16[16,50,1024]{2,1,0:T(8,128)(2,1)} %all-gather.7.cloned.1.call-done) | data formatting | bytes 3276800 | tf_op jit(solution)/shard_map/all_gather | solution.py:22
  78.1 5.8 %all-reduce = s32[100]{0:T(128)S(1)} all-reduce(s32[100]{0:T(128)S(1)} %get-tuple-element.7), channel_id=2, replica_groups=mesh['blk_0'=2,'blk_1'=8,'blk_2'=2,'panel'=32] {'blk_0'}, use_global_device_ids=true, to_apply=%add | all-reduce | flops 100 | bytes 800
  83.8 0.1 reshape.56
  83.9 15.3 %all-gather.2 = s32[8,2,50]{2,1,0:T(2,128)S(1)} all-gather(s32[1,2,50]{2,1,0:T(2,128)S(1)} %reshape.56), channel_id=1, replica_groups=mesh['blk_0'=2,'blk_1'=8,'blk_2'=2,'panel'=32] {'blk_1'}, dimensions={0}, use_global_device_ids=true | all-gather | bytes 3600 | tf_op jit(solution)/shard_map/all_gather | solution.py:22
  99.2 1.8 all_gather.20
  101.0 0.1 eq.68
  101.1 0.1 broadcast_in_dim.41
  101.2 0.1 eq.60
  101.3 1.7 all-gather.9.cloned.1.call-done
  103.0 7.5 %reshape.49 = bf16[2,8,2,50,1024]{4,2,1,0,3:T(2,128)(2,1)} reshape(bf16[32,50,1024]{2,0,1:T(8,128)(2,1)} %all-gather.9.cloned.1.call-done) | data formatting | bytes 6553600 | tf_op jit(solution)/shard_map/reshape | solution.py:24
  110.6 5.6 %copy.20 = bf16[2,8,2,50,1024]{4,3,0,1,2:T(8,128)(2,1)} copy(bf16[2,8,2,50,1024]{4,2,1,0,3:T(2,128)(2,1)} %reshape.49) | data formatting | bytes 6553600 | tf_op jit(solution)/shard_map/reshape | solution.py:24
  116.1 4.7 %reshape_reshape.3 = bf16[1600,1024]{1,0:T(8,128)(2,1)} reshape(bf16[2,8,2,50,1024]{4,3,2,1,0:T(8,128)(2,1)} %bitcast.19) | data formatting | bytes 6553600 | tf_op jit(solution)/shard_map/reshape;reshape | solution.py:16
  120.8 4.2 %fusion = f32[256,1600]{0,1:T(8,128)} fusion(bf16[1600,1024]{1,0:T(8,128)(2,1)} %reshape_reshape.3, bf16[256,1024]{1,0:T(8,128)(2,1)S(1)} %copy-done, s32[256]{0:T(256)S(1)} %eq.60, s32[1600]{0:T(1024)S(1)} %eq.68), kind=kOutput, calls=%fused_computation.2 | convolution fusion | flops 839680000 | bytes 5446912 | tf_op jit(solution)/shard_map/dot_general | solution.py:52
  125.0 1.8 copy.18
  126.8 98.1 %all_to_all.5 = f32[32,8,1600]{2,1,0:T(8,128)} all-to-all(f32[32,8,1600]{2,1,0:T(8,128)S(1)} %bitcast.20), channel_id=1, replica_groups=mesh['blk_0'=2,'blk_1'=8,'blk_2'=2,'panel'=32] {'panel'}, dimensions={0} | all-to-all | bytes 3276800 | tf_op jit(solution)/shard_map/all_to_all | solution.py:41
  224.9 2.2 reduce_sum.29
  (11 shorter events, 0.1 us)
Async XLA Ops:
  6.5 114.3 %copy-start = (bf16[256,1024]{1,0:T(8,128)(2,1)S(1)}, bf16[256,1024]{1,0:T(8,128)(2,1)}, u32[]{:S(2)}) copy-start(bf16[256,1024]{1,0:T(8,128)(2,1)} %param.5) | copy-start | bytes 1572868
  6.5 67.9 %all-gather.7.cloned.1.call-start = ((), (), s32[]{:S(2)}) async-start(), calls=%async_computation.1 | async-start | bytes 2064384 | tf_op jit(solution)/shard_map/all_gather | solution.py:22
  18.4 84.7 %all-gather.9.cloned.1.call-start = ((), (), s32[]{:S(2)}) async-start(), calls=%async_computation.2 | async-start | bytes 4915200 | tf_op jit(solution)/shard_map/all_gather | solution.py:22
  78.0 23.1 %copy-start.1 = (s32[4]{0:T(128)S(1)}, s32[4]{0:T(128)}, u32[]{:S(2)}) copy-start(s32[4]{0:T(128)} %param.7) | copy-start | bytes 52
Sparse Core Ops, SparseCore 0:
  18.5 55.9 all-gather.6
  78.2 24.8 all-gather.8
where the time goes:
time: 235 us; the launch traced here: 234 us
  blocking collectives  128 us (54%)
  waiting for transfers between devices  57.8 us (25%)
  local copies, waits for them, and re-layouts  25.6 us (11%)
  between operations  14.1 us (6%)
  matrix products  4.17 us (2%)
  other arithmetic  4.02 us (2%)
    all_to_all x1, blocking collectives, sum_at_owner(): lax.all_to_all(tiles, axis, split_axis=0, concat_axis=0, tiled=True)  98.1 us
    all_gather x2, waiting for transfers between devices, stacked_from(): tiles = lax.all_gather(tiles, axes[k], axis=0, tiled=True)  57.8 us
    all_gather x3, blocking collectives, stacked_from(): tiles = lax.all_gather(tiles, axes[k], axis=0, tiled=True)  24.2 us
    reshape x2, local copies, waits for them, and re-layouts, stacked_from(): tiles = tiles.reshape(*carried, *array.shape)  13.1 us
    unnamed x1, blocking collectives  5.78 us
  transfers between devices with their start and end apart: 2, of which 2 were waited for; matrix products, arithmetic and copies ran while one was open for 0% of the time, Pallas kernels for 0%

commit v1 on v0

v1 whole, which is shorter than its diff:
```python
import functools

import jax
import jax.numpy as jnp
from jax import lax
from jax.experimental import pallas as pl
from jax.experimental.pallas import tpu as pltpu
from jax.sharding import Mesh
from jax.sharding import PartitionSpec as P


TW = 64
IRREPS = 8
OCC = 40
IJ = 1600
BLK = ("blk_0", "blk_1", "blk_2")
BLK_PANEL = ("blk_0", "blk_1", "blk_2", "panel")
CHIPS = ("blk_0", "blk_1")

PAIRS = 50
ROWS = 56
SOURCES = 16
HALF = SOURCES * ROWS
WIDE = 8
COLS = 640
LIST = 2304
KEPT = 16

SMEM = pl.BlockSpec(memory_space=pltpu.SMEM)
VMEM = pl.BlockSpec(memory_space=pltpu.VMEM)
NT = (((1,), (1,)), ((), ()))


def places(cd_ref):
    irreps = [cd_ref[t] for t in range(16)]
    ranks = []
    for t in range(16):
        rank = jnp.int32(0)
        for earlier in range(t):
            rank += jnp.where(irreps[earlier] == irreps[t], 1, 0)
        ranks.append(rank)
    return irreps, ranks


def fill_chooser(choose, ranks, turn):
    width = WIDE * TW
    row = lax.broadcasted_iota(jnp.int32, (TW, width), 0)
    col = lax.broadcasted_iota(jnp.int32, (TW, width), 1)
    place = jnp.where(col % TW == row, col // TW + turn * WIDE, -1)
    for t in range(16):
        hit = jnp.where(place == ranks[t], 1.0, 0.0)
        choose[t * TW : (t + 1) * TW, :] = hit.astype(jnp.bfloat16)


def column_irreps(irreps):
    lane = lax.broadcasted_iota(jnp.int32, (1, 16 * TW), 1) // TW
    found = jnp.zeros((1, 16 * TW), jnp.int32)
    for t in range(16):
        found = jnp.where(lane == t, irreps[t], found)
    return found


def pack(values, row_irrep, col_irrep, choose):
    kept = jnp.where(row_irrep == col_irrep, values.astype(jnp.float32), 0.0)
    return jnp.dot(
        kept.astype(jnp.bfloat16), choose[...], preferred_element_type=jnp.float32
    ).astype(jnp.bfloat16)


def send_kernel(turn, t_ref, cd_ref, occ_ref, out_ref, choose):
    blk = lax.axis_index("blk_0") * 16 + lax.axis_index("blk_1") * 2 + lax.axis_index("blk_2")
    irreps, ranks = places(cd_ref)
    fill_chooser(choose, ranks, turn)
    first = blk * PAIRS
    row = lax.broadcasted_iota(jnp.int32, (PAIRS, 1), 0)
    row_irrep = jnp.zeros((PAIRS, 1), jnp.int32)
    for m in range(PAIRS):
        pair = first + m
        left = pair // OCC
        irrep = jnp.bitwise_xor(occ_ref[left], occ_ref[pair - left * OCC])
        row_irrep = jnp.where(row == m, irrep, row_irrep)
    packed = pack(t_ref[...], row_irrep, column_irreps(irreps), choose)
    for s in range(SOURCES):
        out_ref[s, :PAIRS, :] = packed
        out_ref[s, PAIRS:, :] = jnp.zeros((ROWS - PAIRS, WIDE * TW), jnp.bfloat16)


def pack_rows_kernel(turn, v_ref, ab_ref, cd_ref, out_ref, choose):
    irreps, ranks = places(cd_ref)
    fill_chooser(choose, ranks, turn)
    row = lax.broadcasted_iota(jnp.int32, (4 * TW, 1), 0) // TW
    row_irrep = jnp.zeros((4 * TW, 1), jnp.int32)
    for i in range(4):
        row_irrep = jnp.where(row == i, ab_ref[i], row_irrep)
    out_ref[...] = pack(v_ref[...], row_irrep, column_irreps(irreps), choose)


def tables_kernel(cd_ref, occ_ref, list_ref, code_ref, kept_ref, orbitals, count):
    core = lax.axis_index("blk_2")
    for g in range(IRREPS):
        orbitals[g] = 0

    @pl.loop(0, OCC)
    def _(i):
        g = occ_ref[i]
        orbitals[g] = orbitals[g] + 1

    start = jnp.int32(0)
    most = jnp.int32(0)
    for g in range(IRREPS):
        pairs = jnp.int32(0)
        for h in range(IRREPS):
            pairs += orbitals[h] * orbitals[g ^ h]
        kept_ref[g] = start
        count[g] = start
        start += pairs
        most = jnp.maximum(most, pairs)
    _, ranks = places(cd_ref)
    widest = ranks[0]
    for rank in ranks[1:]:
        widest = jnp.maximum(widest, rank)
    kept_ref[8] = start
    kept_ref[9] = widest + 1
    kept_ref[10] = most
    for k in range(11, KEPT):
        kept_ref[k] = 0

    @pl.loop(0, OCC)
    def _(i):
        left = occ_ref[i]

        @pl.loop(0, OCC)
        def _(j):
            pair = i * OCC + j
            irrep = jnp.bitwise_xor(left, occ_ref[j])
            at = count[irrep]
            count[irrep] = at + 1
            source = pair // PAIRS
            other = jnp.bitwise_xor(source & 1, core)
            list_ref[at] = (other * SOURCES + (source >> 1)) * ROWS + pair - source * PAIRS
            code_ref[pair] = (at - kept_ref[irrep]) * IRREPS + irrep

    @pl.loop(IJ, LIST)
    def _(k):
        list_ref[k] = 0


def product_kernel(turns, round_ref, *refs):
    halves, weights = refs[: 2 * turns], refs[2 * turns : 3 * turns]
    ab_ref, list_ref, kept_ref, out_ref, left_product, right_product, dense = refs[3 * turns :]
    products = (left_product, right_product)
    for half in range(2):
        total = None
        for turn in range(turns):
            part = lax.dot_general(
                halves[2 * turn + half][...], weights[turn][...], NT,
                preferred_element_type=jnp.float32,
            )
            total = part if total is None else total + part
        for q in range(2):
            products[q][half * HALF : (half + 1) * HALF, :] = total[:, q * 128 : (q + 1) * 128]
    lower = lax.broadcasted_iota(jnp.int32, (1, 128), 1) < TW
    skip = round_ref[0] * COLS
    for q in range(2):
        product = products[q]
        dense[...] = jnp.zeros_like(dense)
        irreps = [ab_ref[2 * q + i] for i in range(2)]
        starts = [jnp.minimum(kept_ref[g] + skip, IJ) for g in irreps]
        counts = [kept_ref[g + 1] - kept_ref[g] - skip for g in irreps]
        most = jnp.clip(jnp.maximum(counts[0], counts[1]), 0, COLS)

        @pl.loop(0, (most + 7) // 8)
        def _(block):
            base = block * 8
            for u in range(8):
                at = [list_ref[start + base + u] for start in starts]
                rows = [product[pl.ds(a, 1), :] for a in at]
                dense[pl.ds(base + u, 1), :] = jnp.where(lower, rows[0], rows[1])

        out_ref[q * 16 : (q + 1) * 16] = dense[...].T.reshape(16, 8, COLS)


def finish_kernel(round_ref, got_ref, ab_ref, code_ref, out_ref):
    irrep = ab_ref[lax.axis_index("panel") // 8]
    total = got_ref[0]
    for s in range(1, 32):
        total = total + got_ref[s]
    high = total.astype(jnp.bfloat16)
    rest = total - high.astype(jnp.float32)
    middle = rest.astype(jnp.bfloat16)
    low = (rest - middle.astype(jnp.float32)).astype(jnp.bfloat16)
    code = code_ref[...]
    place = jnp.where(code % IRREPS == irrep, code // IRREPS - round_ref[0] * COLS, -1)
    row = lax.broadcasted_iota(jnp.int32, (COLS, IJ), 0)
    spread = jnp.where(row == place, 1.0, 0.0).astype(jnp.bfloat16)
    parts = [jnp.dot(p, spread, preferred_element_type=jnp.float32) for p in (low, middle, high)]
    out_ref[...] = parts[0] + parts[1] + parts[2]


def shaped(shape, dtype):
    return jax.ShapeDtypeStruct(shape, dtype)


def body(integrals, amplitudes, ab_irrep, cd_irrep, occ_irrep):
    bf16, f32, i32 = jnp.bfloat16, jnp.float32, jnp.int32
    width = WIDE * TW
    chooser = pltpu.VMEM((16 * TW, width), bf16)

    def gathered(turn):
        sent = pl.pallas_call(
            functools.partial(send_kernel, turn),
            out_shape=shaped((SOURCES, ROWS, width), bf16),
            in_specs=[VMEM, SMEM, SMEM],
            out_specs=VMEM,
            scratch_shapes=[chooser],
        )(amplitudes, cd_irrep, occ_irrep)
        mine = lax.all_to_all(sent, CHIPS, split_axis=0, concat_axis=0, tiled=True)
        mine = mine.reshape(HALF, width)
        return [mine, lax.ppermute(mine, "blk_2", [(0, 1), (1, 0)])]

    def weights(turn):
        return pl.pallas_call(
            functools.partial(pack_rows_kernel, turn),
            out_shape=shaped((4 * TW, width), bf16),
            in_specs=[VMEM, SMEM, SMEM],
            out_specs=VMEM,
            scratch_shapes=[chooser],
        )(integrals, ab_irrep, cd_irrep)

    pair_list, code, kept = pl.pallas_call(
        tables_kernel,
        out_shape=[shaped((LIST,), i32), shaped((IJ,), i32), shaped((KEPT,), i32)],
        in_specs=[SMEM, SMEM],
        out_specs=[SMEM] * 3,
        scratch_shapes=[pltpu.SMEM((IRREPS,), i32), pltpu.SMEM((IRREPS,), i32)],
        name="tables",
    )(cd_irrep, occ_irrep)
    code = code.reshape(1, IJ)

    first, first_weights = gathered(0), weights(0)

    def products(which, turns, operands):
        return pl.pallas_call(
            functools.partial(product_kernel, turns),
            out_shape=shaped((32, 8, COLS), f32),
            in_specs=[SMEM] + [VMEM] * (3 * turns) + [SMEM] * 3,
            out_specs=VMEM,
            scratch_shapes=[
                pltpu.VMEM((2 * HALF, 128), f32),
                pltpu.VMEM((2 * HALF, 128), f32),
                pltpu.VMEM((COLS, 128), f32),
            ],
        )(which, *operands, ab_irrep, pair_list, kept)

    def partial_of(which):
        return lax.cond(
            kept[9] > WIDE,
            lambda: products(which, 2, [*first, *gathered(1), first_weights, weights(1)]),
            lambda: products(which, 1, [*first, first_weights]),
        )

    def reduced(number):
        which = jnp.full((1,), number, i32)
        arrived = lax.all_to_all(partial_of(which), "panel", split_axis=0, concat_axis=0, tiled=True)
        return pl.pallas_call(
            finish_kernel,
            out_shape=shaped((8, IJ), f32),
            in_specs=[SMEM, VMEM, SMEM, VMEM],
            out_specs=VMEM,
            name="finish",
        )(which, arrived, ab_irrep, code)

    def all_rounds():
        rounds = (kept[10] + COLS - 1) // COLS
        return lax.fori_loop(
            0, rounds, lambda number, total: total + reduced(number), jnp.zeros((8, IJ), f32)
        )

    return lax.cond(kept[10] > COLS, all_rounds, lambda: reduced(0))


def solution(mesh):
    split = Mesh(
        mesh.devices.reshape(2, 8, 2, mesh.shape["panel"]), ("blk_0", "blk_1", "blk_2", "panel")
    )
    return jax.shard_map(
        body,
        mesh=split,
        in_specs=(P(BLK, "panel"), P(BLK, "panel"), P(BLK), P("panel"), P()),
        out_specs=P(BLK_PANEL, None),
        check_vma=False,
    )
```

time: 235 us -> 146 us (0.62)
  the two profiles are of different devices: /device:TPU:2 before, /device:TPU:1 now
where the time goes in v1:
time: 146 us; the launch traced here: 145 us
  blocking collectives  84 us (58%)
  Pallas kernels  45 us (31%)
  starting transfers between devices  11.7 us (8%)
  local copies, waits for them, and re-layouts  3.12 us (2%)
    all_to_all x1, blocking collectives, reduced(): lax.all_to_all(partial_of(which), 'panel', split_axis=0, concat_axis=0, t...  56.7 us
    pallas_call x1, Pallas kernels, body(): pl.pallas_call(tables_kernel, out_shape=[shaped((LIST,), i32), shaped((IJ...  33.5 us
    all_to_all x1, blocking collectives, gathered(): mine = lax.all_to_all(sent, CHIPS, split_axis=0, concat_axis=0, tiled=True)  27.2 us
    ppermute x1, starting transfers between devices, gathered(): return [mine, lax.ppermute(mine, 'blk_2', [(0, 1), (1, 0)])]  11.7 us
    pallas_call x1, Pallas kernels, products(): pl.pallas_call(functools.partial(product_kernel, turns), out_shape=shaped...  5.12 us
  transfers between devices with their start and end apart: 1, of which 0 were waited for; matrix products, arithmetic and copies ran while one was open for 1% of the time, Pallas kernels for 24%

profile of v1, /device:TPU:1, one launch (start us, length us, event | category | flops | bytes accessed | tf_op | source)
XLA Modules:
  0.0 145.2 jit_solution(10172119319092538979)
XLA Ops:
  0.0 2.5 %shard_map.57 = bf16[16,56,512]{2,1,0:T(8,128)(2,1)} custom-call(bf16[50,1024]{1,0:T(8,128)(2,1)} %t_ref.1, s32[16]{0:T(128)} %cd_ref.5, s32[40]{0:T(128)} %occ_ref.3), custom_call_target="tpu_custom_call" | custom-call | tf_op jit(solution)/shard_map/pallas_call | solution.py:210
  2.5 0.0 copy-start.2
  2.5 27.2 %all_to_all.26 = bf16[16,56,512]{2,1,0:T(8,128)(2,1)S(1)} all-to-all(bf16[16,56,512]{2,1,0:T(8,128)(2,1)} %shard_map.57), channel_id=1, replica_groups=mesh['blk_0'=2,'blk_1'=8,'blk_2'=2,'panel'=32] {'blk_0','blk_1'}, dimensions={0} | all-to-all | bytes 1835008 | tf_op jit(solution)/shard_map/all_to_all | solution.py:217
  29.8 0.0 copy-start.10
  29.8 0.0 copy-start.20
  29.8 11.7 %collective-permute-start.2 = (bf16[896,512]{1,0:T(8,128)(2,1)S(1)}, bf16[896,512]{1,0:T(8,128)(2,1)S(1)}, u32[]{:S(2)}, u32[]{:S(2)}) collective-permute-start(bf16[896,512]{1,0:T(8,128)(2,1)S(1)} %bitcast.11), channel_id=1, source_target_pairs={{0,32},{32,0},{1,33},{33,1},{2,34},{34,2},{3,35},{35,3},{4,36},{36... | collective-permute-start | bytes 2752520 | tf_op jit(solution)/shard_map/ppermute | solution.py:219
  41.5 0.0 copy-done.10
  41.5 0.0 copy-done.20
  41.5 33.5 %tables.1 = (s32[2304]{0:T(1024)S(1)}, s32[1600]{0:T(1024)}, s32[16]{0:T(128)S(1)}) custom-call(s32[16]{0:T(128)S(1)} %copy-done.10, s32[40]{0:T(128)S(1)} %copy-done.20), custom_call_target="tpu_custom_call" | custom-call | tf_op jit(solution)/shard_map/tables/pallas_call | solution.py:230
  75.0 1.3 reshape.35
  76.3 0.6 slice.14
  77.5 0.0 copy-start.9
  77.5 0.0 copy-done.2
  77.5 0.6 copy-done.9
  78.2 1.0 shard_map.58
  79.2 0.0 collective-permute-done.2
  79.2 0.0 copy-done.3
  79.2 66.0 %conditional.3 = (f32[8,1600]{1,0:T(8,128)}) conditional(s32[]{:T(128)} %bitcast.7, (s32[16]{0:T(128)S(1)}, bf16[896,512]{1,0:T(8,128)(2,1)S(1)}, bf16[896,512]{1,0:T(8,128)(2,1)S(1)}, bf16[256,512]{1,0:T(8,128)(2,1)S(1)}, s32[4]{0:T(128)S(1)}, /*index=5*/s32[2304]{0:T(1024)S(1)}, bf16[50,1024]{1,0:T(8,128)(2,1)S(1)}, s32[16]{0:T(128)S(1)}, ...), branch_computations={%region_0.0_spmd, %region_3.8_spmd} | conditional | flops 12813 | bytes 14815989 | solution.py:279
  79.2 0.6 slice.10
  80.4 5.1 %conditional = (f32[32,8,640]{2,1,0:T(8,128)}) conditional(s32[]{:T(128)} %bitcast.1, (bf16[896,512]{1,0:T(8,128)(2,1)S(1)}, bf16[896,512]{1,0:T(8,128)(2,1)S(1)}, bf16[256,512]{1,0:T(8,128)(2,1)S(1)}, s32[4]{0:T(128)S(1)}, s32[2304]{0:T(1024)S(1)}, /*index=5*/s32[16]{0:T(128)S(1)}) %tuple.23, (bf16[50,1024]{1,0:T(8,128)(2,1)S(1)}, s32[16]{0:T(128)S(1)}, ...), branch_computations={%region_1.0_spmd, %region_2.0_spmd} | conditional | bytes 9175968 | solution.py:256
  80.4 5.1 %branch_0_fun.2 = f32[32,8,640]{2,1,0:T(8,128)} custom-call(s32[1]{0:T(128)} %constant.31.clone.round_ref, bf16[896,512]{1,0:T(8,128)(2,1)S(1)} %get-tuple-element.242.refs_0_, bf16[896,512]{1,0:T(8,128)(2,1)S(1)} %get-tuple-element.243.refs_1_, bf16[256,512]{1,0:T(8,128)(2,1)S(1)} %get-tuple-element.244.refs_2_, s32[4]{0:T(128)S(1)} %get-tuple-element.245.refs_3_, ...), custom_call_target="tpu_custom_call" | custom-call | tf_op jit(solution)/shard_map/cond/branch_0_fun/cond/branch_0_fun/pallas_call | solution.py:243
  85.6 56.7 %all_to_all.24.got_ref = f32[32,8,640]{2,1,0:T(8,128)} all-to-all(f32[32,8,640]{2,1,0:T(8,128)} %get-tuple-element.497), channel_id=1, replica_groups=mesh['blk_0'=2,'blk_1'=8,'blk_2'=2,'panel'=32] {'panel'}, dimensions={0} | all-to-all | bytes 1310720 | tf_op jit(solution)/shard_map/cond/branch_0_fun/all_to_all | solution.py:264
  142.3 0.0 copy-done.7
  142.3 2.8 %finish.3 = f32[8,1600]{1,0:T(8,128)} custom-call(s32[1]{0:T(128)} %constant.33.clone.round_ref, f32[32,8,640]{2,1,0:T(8,128)} %all_to_all.24.got_ref, s32[4]{0:T(128)S(1)} %get-tuple-element.262.ab_ref, s32[1,1600]{1,0:T(1,128)S(1)} %copy-done.7), custom_call_target="tpu_custom_call" | custom-call | tf_op jit(solution)/shard_map/cond/branch_0_fun/finish/pallas_call | solution.py:265
  (2 shorter events, 0.0 us)
Async XLA Ops:
  2.5 75.0 %copy-start.2 = (bf16[256,1024]{1,0:T(8,128)(2,1)S(1)}, bf16[256,1024]{1,0:T(8,128)(2,1)}, u32[]{:S(2)}) copy-start(bf16[256,1024]{1,0:T(8,128)(2,1)} %v_ref.1) | copy-start | bytes 1572868
  29.8 11.7 %copy-start.10 = (s32[16]{0:T(128)S(1)}, s32[16]{0:T(128)}, u32[]{:S(2)}) copy-start(s32[16]{0:T(128)} %cd_ref.5) | copy-start | bytes 196
  29.8 11.7 %copy-start.20 = (s32[40]{0:T(128)S(1)}, s32[40]{0:T(128)}, u32[]{:S(2)}) copy-start(s32[40]{0:T(128)} %occ_ref.3) | copy-start | bytes 484
  29.8 49.4 %collective-permute-start.2 = (bf16[896,512]{1,0:T(8,128)(2,1)S(1)}, bf16[896,512]{1,0:T(8,128)(2,1)S(1)}, u32[]{:S(2)}, u32[]{:S(2)}) collective-permute-start(bf16[896,512]{1,0:T(8,128)(2,1)S(1)} %bitcast.11), channel_id=1, source_target_pairs={{0,32},{32,0},{1,33},{33,1},{2,34},{34,2},{3,35},{35,3},{4,36},{36... | collective-permute-start | bytes 2752520 | tf_op jit(solution)/shard_map/ppermute | solution.py:219
  77.5 0.7 copy-start.9
  78.2 1.0 copy-start.3
  85.6 56.8 %copy-start.7 = (s32[1,1600]{1,0:T(1,128)S(1)}, s32[1,1600]{1,0:T(1,128)}, u32[]{:S(2)}) copy-start(s32[1,1600]{1,0:T(1,128)} %get-tuple-element.268.code_ref) | copy-start | bytes 19204 | tf_op jit(solution)/shard_map/cond

commit v2 on v1

--- a/solution.py
+++ b/solution.py
@@ -22,7 +22,8 @@
 SOURCES = 16
 HALF = SOURCES * ROWS
 WIDE = 8
-COLS = 640
+WIRE = 640
+COLS = WIRE - 1
 LIST = 2304
 KEPT = 16
 
@@ -71,13 +72,15 @@
     blk = lax.axis_index("blk_0") * 16 + lax.axis_index("blk_1") * 2 + lax.axis_index("blk_2")
     irreps, ranks = places(cd_ref)
     fill_chooser(choose, ranks, turn)
-    first = blk * PAIRS
+    upper = blk * 5 // 4
+    at = blk % 4 * 10
+    left = [occ_ref[upper], occ_ref[jnp.minimum(upper + 1, OCC - 1)]]
     row = lax.broadcasted_iota(jnp.int32, (PAIRS, 1), 0)
     row_irrep = jnp.zeros((PAIRS, 1), jnp.int32)
     for m in range(PAIRS):
-        pair = first + m
-        left = pair // OCC
-        irrep = jnp.bitwise_xor(occ_ref[left], occ_ref[pair - left * OCC])
+        later = at + m >= OCC
+        right = occ_ref[at + m - jnp.where(later, OCC, 0)]
+        irrep = jnp.bitwise_xor(jnp.where(later, left[1], left[0]), right)
         row_irrep = jnp.where(row == m, irrep, row_irrep)
     packed = pack(t_ref[...], row_irrep, column_irreps(irreps), choose)
     for s in range(SOURCES):
@@ -125,29 +128,29 @@
     for k in range(11, KEPT):
         kept_ref[k] = 0
 
-    @pl.loop(0, OCC)
-    def _(i):
-        left = occ_ref[i]
-
-        @pl.loop(0, OCC)
-        def _(j):
-            pair = i * OCC + j
-            irrep = jnp.bitwise_xor(left, occ_ref[j])
-            at = count[irrep]
-            count[irrep] = at + 1
-            source = pair // PAIRS
-            other = jnp.bitwise_xor(source & 1, core)
-            list_ref[at] = (other * SOURCES + (source >> 1)) * ROWS + pair - source * PAIRS
-            code_ref[pair] = (at - kept_ref[irrep]) * IRREPS + irrep
-
-    @pl.loop(IJ, LIST)
+    @pl.loop(0, 8)
+    def _(part):
+        base = [part * 2 * ROWS + jnp.bitwise_xor(other, core) * HALF for other in range(2)]
+        for i in range(5):
+            left = occ_ref[part * 5 + i]
+            for j in range(OCC):
+                pair = i * OCC + j
+                source, m = divmod(pair, PAIRS)
+                irrep = jnp.bitwise_xor(left, occ_ref[j])
+                at = count[irrep]
+                count[irrep] = at + 1
+                list_ref[at] = base[source % 2] + source // 2 * ROWS + m
+                code_ref[part * 200 + pair] = at * IRREPS + irrep
+
+    @pl.loop(0, (LIST - IJ) // 16)
     def _(k):
-        list_ref[k] = 0
+        for u in range(16):
+            list_ref[IJ + k * 16 + u] = 0
 
 
 def product_kernel(turns, round_ref, *refs):
     halves, weights = refs[: 2 * turns], refs[2 * turns : 3 * turns]
-    ab_ref, list_ref, kept_ref, out_ref, left_product, right_product, dense = refs[3 * turns :]
+    ab_ref, list_ref, kept_ref, out_ref, left_product, right_product, dense, both = refs[3 * turns :]
     products = (left_product, right_product)
     for half in range(2):
         total = None
@@ -177,21 +180,26 @@
                 rows = [product[pl.ds(a, 1), :] for a in at]
                 dense[pl.ds(base + u, 1), :] = jnp.where(lower, rows[0], rows[1])
 
-        out_ref[q * 16 : (q + 1) * 16] = dense[...].T.reshape(16, 8, COLS)
-
-
-def finish_kernel(round_ref, got_ref, ab_ref, code_ref, out_ref):
+        both[q * 128 : (q + 1) * 128, :] = dense[...].T
+    largest = jnp.max(jnp.max(jnp.abs(both[...]), axis=1, keepdims=True), axis=0, keepdims=True)
+    power = 14.0 - jnp.floor(jnp.log2(jnp.maximum(largest, 1e-30)))
+    scaled = both[...] * jnp.exp2(power)
+    lane = lax.broadcasted_iota(jnp.int32, (4 * TW, WIRE), 1)
+    out_ref[...] = jnp.where(lane == COLS, power, scaled).reshape(32, 8, WIRE)
+
+
+def finish_kernel(round_ref, sum_ref, ab_ref, kept_ref, code_ref, out_ref):
     irrep = ab_ref[lax.axis_index("panel") // 8]
-    total = got_ref[0]
-    for s in range(1, 32):
-        total = total + got_ref[s]
+    total = sum_ref[...]
     high = total.astype(jnp.bfloat16)
     rest = total - high.astype(jnp.float32)
     middle = rest.astype(jnp.bfloat16)
     low = (rest - middle.astype(jnp.float32)).astype(jnp.bfloat16)
     code = code_ref[...]
-    place = jnp.where(code % IRREPS == irrep, code // IRREPS - round_ref[0] * COLS, -1)
-    row = lax.broadcasted_iota(jnp.int32, (COLS, IJ), 0)
+    first = kept_ref[irrep] + round_ref[0] * COLS
+    place = jnp.where(code % IRREPS == irrep, code // IRREPS - first, -1)
+    place = jnp.where(place < COLS, place, -1)
+    row = lax.broadcasted_iota(jnp.int32, (WIRE, IJ), 0)
     spread = jnp.where(row == place, 1.0, 0.0).astype(jnp.bfloat16)
     parts = [jnp.dot(p, spread, preferred_element_type=jnp.float32) for p in (low, middle, high)]
     out_ref[...] = parts[0] + parts[1] + parts[2]
@@ -242,33 +250,39 @@
     def products(which, turns, operands):
         return pl.pallas_call(
             functools.partial(product_kernel, turns),
-            out_shape=shaped((32, 8, COLS), f32),
+            out_shape=shaped((32, 8, WIRE), f32),
             in_specs=[SMEM] + [VMEM] * (3 * turns) + [SMEM] * 3,
             out_specs=VMEM,
             scratch_shapes=[
                 pltpu.VMEM((2 * HALF, 128), f32),
                 pltpu.VMEM((2 * HALF, 128), f32),
-                pltpu.VMEM((COLS, 128), f32),
+                pltpu.VMEM((WIRE, 128), f32),
+                pltpu.VMEM((4 * TW, WIRE), f32),
             ],
         )(which, *operands, ab_irrep, pair_list, kept)
 
+    more_tiles, more_pairs = kept[9] > WIDE, kept[10] > COLS
+
     def partial_of(which):
         return lax.cond(
-            kept[9] > WIDE,
+            more_tiles,
             lambda: products(which, 2, [*first, *gathered(1), first_weights, weights(1)]),
             lambda: products(which, 1, [*first, first_weights]),
         )
 
     def reduced(number):
         which = jnp.full((1,), number, i32)
-        arrived = lax.all_to_all(partial_of(which), "panel", split_axis=0, concat_axis=0, tiled=True)
+        sent = partial_of(which).astype(jnp.float16)
+        arrived = lax.all_to_all(sent, "panel", split_axis=0, concat_axis=0, tiled=True)
+        arrived = arrived.astype(f32)
+        total = jnp.sum(arrived * jnp.exp2(-arrived[:, :, COLS:]), axis=0)
         return pl.pallas_call(
             finish_kernel,
             out_shape=shaped((8, IJ), f32),
-            in_specs=[SMEM, VMEM, SMEM, VMEM],
+            in_specs=[SMEM, VMEM, SMEM, SMEM, VMEM],
             out_specs=VMEM,
             name="finish",
-        )(which, arrived, ab_irrep, code)
+        )(which, total, ab_irrep, kept, code)
 
     def all_rounds():
         rounds = (kept[10] + COLS - 1) // COLS
@@ -276,7 +290,7 @@
             0, rounds, lambda number, total: total + reduced(number), jnp.zeros((8, IJ), f32)
         )
 
-    return lax.cond(kept[10] > COLS, all_rounds, lambda: reduced(0))
+    return lax.cond(more_pairs, all_rounds, lambda: reduced(0))
 
 
 def solution(mesh):

time: 146 us -> 110 us (0.75)
  the two profiles are of different devices: /device:TPU:1 before, /device:TPU:2 now
where the time goes in v2:
time: 110 us
  blocking collectives  79.2 us (72%)
  Pallas kernels  22.8 us (21%)
  local copies, waits for them, and re-layouts  3.65 us (3%)
  starting transfers between devices  1.91 us (2%)
  between operations  1.34 us (1%)
    all_to_all x1, blocking collectives, reduced(): lax.all_to_all(sent, 'panel', split_axis=0, concat_axis=0, tiled=True)  45.2 us
    all_to_all x1, blocking collectives, gathered(): mine = lax.all_to_all(sent, CHIPS, split_axis=0, concat_axis=0, tiled=True)  34.1 us
    pallas_call x1, Pallas kernels, body(): pl.pallas_call(tables_kernel, out_shape=[shaped((LIST,), i32), shaped((IJ...  11 us
    pallas_call x1, Pallas kernels, products(): pl.pallas_call(functools.partial(product_kernel, turns), out_shape=shaped...  4.66 us
    pallas_call x1, Pallas kernels, reduced(): pl.pallas_call(finish_kernel, out_shape=shaped((8, IJ), f32), in_specs=[S...  2.48 us
    pallas_call x1, Pallas kernels, gathered(): pl.pallas_call(functools.partial(send_kernel, turn), out_shape=shaped((SO...  2.37 us
    pallas_call x1, Pallas kernels, weights(): pl.pallas_call(functools.partial(pack_rows_kernel, turn), out_shape=shape...  2.25 us
  transfers between devices with their start and end apart: 1, of which 0 were waited for; matrix products, arithmetic and copies ran while one was open for 1% of the time, Pallas kernels for 12%

profile of v2, /device:TPU:2, one launch (start us, length us, event | category | flops | bytes accessed | tf_op | source)
XLA Modules:
  0.0 110.0 jit_solution(5495089761400684992)
XLA Ops:
  0.0 0.0 copy-start.3
  0.0 0.0 copy-start.4
  0.0 0.0 copy-start.2
  0.0 2.4 %shard_map.57 = bf16[16,56,512]{2,1,0:T(8,128)(2,1)} custom-call(bf16[50,1024]{1,0:T(8,128)(2,1)} %t_ref.1, s32[16]{0:T(128)} %cd_ref.5, s32[40]{0:T(128)} %occ_ref.3), custom_call_target="tpu_custom_call" | custom-call | tf_op jit(solution)/shard_map/pallas_call | solution.py:218
  2.4 34.1 %all_to_all.26 = bf16[16,56,512]{2,1,0:T(8,128)(2,1)S(1)} all-to-all(bf16[16,56,512]{2,1,0:T(8,128)(2,1)} %shard_map.57), channel_id=1, replica_groups=mesh['blk_0'=2,'blk_1'=8,'blk_2'=2,'panel'=32] {'blk_0','blk_1'}, dimensions={0} | all-to-all | bytes 1835008 | tf_op jit(solution)/shard_map/all_to_all | solution.py:225
  36.4 1.9 %collective-permute-start.2 = (bf16[896,512]{1,0:T(8,128)(2,1)S(1)}, bf16[896,512]{1,0:T(8,128)(2,1)S(1)}, u32[]{:S(2)}, u32[]{:S(2)}) collective-permute-start(bf16[896,512]{1,0:T(8,128)(2,1)S(1)} %bitcast.16), channel_id=1, source_target_pairs={{0,32},{32,0},{1,33},{33,1},{2,34},{34,2},{3,35},{35,3},{4,36},{36... | collective-permute-start | bytes 2752520 | tf_op jit(solution)/shard_map/ppermute | solution.py:227
  38.4 0.0 copy-done.3
  38.4 0.0 copy-done.4
  38.4 11.0 %tables.1 = (s32[2304]{0:T(1024)S(1)}, s32[1600]{0:T(1024)}, s32[16]{0:T(128)S(1)}) custom-call(s32[16]{0:T(128)S(1)} %copy-done.3, s32[40]{0:T(128)S(1)} %copy-done.4), custom_call_target="tpu_custom_call" | custom-call | tf_op jit(solution)/shard_map/tables/pallas_call | solution.py:238
  49.4 0.7 reshape.31
  50.1 0.6 fusion.6
  52.0 0.0 copy-done.2
  52.0 2.2 %shard_map.58 = bf16[256,512]{1,0:T(8,128)(2,1)} custom-call(bf16[256,1024]{1,0:T(8,128)(2,1)} %v_ref.1, s32[4]{0:T(128)S(1)} %copy-done.2, s32[16]{0:T(128)S(1)} %copy-done.3), custom_call_target="tpu_custom_call" | custom-call | tf_op jit(solution)/shard_map/pallas_call | solution.py:230
  54.3 0.0 collective-permute-done.2
  54.3 55.7 %conditional.3 = (f32[8,1600]{1,0:T(8,128)}) conditional(s32[]{:T(128)} %bitcast.7, (pred[]{:T(512)}, bf16[896,512]{1,0:T(8,128)(2,1)S(1)}, bf16[896,512]{1,0:T(8,128)(2,1)S(1)}, bf16[256,512]{1,0:T(8,128)(2,1)}, s32[4]{0:T(128)S(1)}, /*index=5*/s32[2304]{0:T(1024)S(1)}, s32[16]{0:T(128)S(1)}, bf16[50,1024]{1,0:T(8,128)(2,1)}, s32[16]{0:T(128)S(1)}, ...), branch_computations={%region_0.0_spmd, %region_4.10_spmd} | conditional | flops 827404 | bytes 13377172 | solution.py:293
  54.3 4.7 %conditional = (f32[32,8,640]{2,1,0:T(8,128)S(1)}) conditional(s32[]{:T(128)} %convert_element_type.16, (bf16[896,512]{1,0:T(8,128)(2,1)S(1)}, bf16[896,512]{1,0:T(8,128)(2,1)S(1)}, bf16[256,512]{1,0:T(8,128)(2,1)}, s32[4]{0:T(128)S(1)}, s32[2304]{0:T(1024)S(1)}, /*index=5*/s32[16]{0:T(128)S(1)}) %tuple.19, (bf16[50,1024]{1,0:T(8,128)(2,1)}, ...), branch_computations={%region_1.0_spmd, %region_2.0_spmd} | conditional | bytes 9175116 | solution.py:267
  54.3 4.7 %branch_0_fun.2 = f32[32,8,640]{2,1,0:T(8,128)S(1)} custom-call(s32[1]{0:T(128)} %constant.20.clone.round_ref, bf16[896,512]{1,0:T(8,128)(2,1)S(1)} %get-tuple-element.188.refs_0_, bf16[896,512]{1,0:T(8,128)(2,1)S(1)} %get-tuple-element.190.refs_1_, bf16[256,512]{1,0:T(8,128)(2,1)} %get-tuple-element.192.refs_2_, s32[4]{0:T(128)S(1)} %get-tuple-element.193.refs_3_, ...), custom_call_target="tpu_custom_call" | custom-call | tf_op jit(solution)/shard_map/cond/branch_0_fun/cond/branch_0_fun/pallas_call | solution.py:251
  59.0 45.2 %all_to_all.24 = f16[32,8,640]{2,1,0:T(8,128)(2,1)S(1)} all-to-all(f16[32,8,640]{2,1,0:T(8,128)(2,1)S(1)} %convert_element_type.17), channel_id=1, replica_groups=mesh['blk_0'=2,'blk_1'=8,'blk_2'=2,'panel'=32] {'panel'}, dimensions={0} | all-to-all | bytes 655360 | tf_op jit(solution)/shard_map/cond/branch_0_fun/all_to_all | solution.py:276
  104.2 1.6 %copy.10 = f16[32,8,640]{0,1,2:T(8,128)(2,1)S(1)} copy(f16[32,8,640]{2,1,0:T(8,128)(2,1)S(1)} %all_to_all.24) | data formatting | bytes 655360 | tf_op jit(solution)/shard_map/cond/branch_0_fun/all_to_all | solution.py:276
  105.8 0.2 convert_element_type.18
  106.0 0.8 multiply_reduce_fusion
  106.7 0.7 copy.11.sum_ref
  107.5 2.5 %finish.2 = f32[8,1600]{1,0:T(8,128)} custom-call(s32[1]{0:T(128)} %constant.22.clone.round_ref, f32[8,640]{1,0:T(8,128)} %copy.11.sum_ref, s32[4]{0:T(128)S(1)} %get-tuple-element.210.ab_ref, s32[16]{0:T(128)S(1)} %get-tuple-element.212.kept_ref, s32[1,1600]{1,0:T(1,128)S(1)} %get-tuple-element.217.code_ref), custom_call_target="tpu_custom_call" | custom-call | tf_op jit(solution)/shard_map/cond/branch_0_fun/finish/pallas_call | solution.py:279
  (2 shorter events, 0.0 us)
Async XLA Ops:
  0.0 38.4 %copy-start.3 = (s32[16]{0:T(128)S(1)}, s32[16]{0:T(128)}, u32[]{:S(2)}) copy-start(s32[16]{0:T(128)} %cd_ref.5) | copy-start | bytes 196
  0.0 38.4 %copy-start.4 = (s32[40]{0:T(128)S(1)}, s32[40]{0:T(128)}, u32[]{:S(2)}) copy-start(s32[40]{0:T(128)} %occ_ref.3) | copy-start | bytes 484
  0.0 52.0 %copy-start.2 = (s32[4]{0:T(128)S(1)}, s32[4]{0:T(128)}, u32[]{:S(2)}) copy-start(s32[4]{0:T(128)} %ab_ref.1) | copy-start | bytes 52
  36.4 17.8 %collective-permute-start.2 = (bf16[896,512]{1,0:T(8,128)(2,1)S(1)}, bf16[896,512]{1,0:T(8,128)(2,1)S(1)}, u32[]{:S(2)}, u32[]{:S(2)}) collective-permute-start(bf16[896,512]{1,0:T(8,128)(2,1)S(1)} %bitcast.16), channel_id=1, source_target_pairs={{0,32},{32,0},{1,33},{33,1},{2,34},{34,2},{3,35},{35,3},{4,36},{36... | collective-permute-start | bytes 2752520 | tf_op jit(solution)/shard_map/ppermute | solution.py:227

commit v3 on v2

v3 whole, which is shorter than its diff:
```python
import functools

import jax
import jax.numpy as jnp
from jax import lax
from jax.experimental import pallas as pl
from jax.experimental.pallas import tpu as pltpu
from jax.sharding import Mesh
from jax.sharding import PartitionSpec as P


TW = 64
IRREPS = 8
OCC = 40
IJ = 1600
BLK = ("blk_0", "blk_1", "blk_2")
BLK_PANEL = ("blk_0", "blk_1", "blk_2", "panel")
CHIPS = ("blk_0", "blk_1")

PAIRS = 50
SOURCES = 16
WIDE = 8
NARROW = 4
ROWS = 88
FULL = 56
WIRES = (512, 640)
LIST = 2304
KEPT = 16

SMEM = pl.BlockSpec(memory_space=pltpu.SMEM)
VMEM = pl.BlockSpec(memory_space=pltpu.VMEM)
NT = (((1,), (1,)), ((), ()))


def places(cd_ref):
    irreps = [cd_ref[t] for t in range(16)]
    ranks = []
    for t in range(16):
        rank = jnp.int32(0)
        for earlier in range(t):
            rank += jnp.where(irreps[earlier] == irreps[t], 1, 0)
        ranks.append(rank)
    return irreps, ranks


def fill_chooser(choose, ranks, turn):
    width = WIDE * TW
    row = lax.broadcasted_iota(jnp.int32, (TW, width), 0)
    col = lax.broadcasted_iota(jnp.int32, (TW, width), 1)
    place = jnp.where(col % TW == row, col // TW + turn * WIDE, -1)
    for t in range(16):
        hit = jnp.where(place == ranks[t], 1.0, 0.0)
        choose[t * TW : (t + 1) * TW, :] = hit.astype(jnp.bfloat16)


def column_irreps(irreps):
    lane = lax.broadcasted_iota(jnp.int32, (1, 16 * TW), 1) // TW
    found = jnp.zeros((1, 16 * TW), jnp.int32)
    for t in range(16):
        found = jnp.where(lane == t, irreps[t], found)
    return found


def pack(values, row_irrep, col_irrep, choose):
    kept = jnp.where(row_irrep == col_irrep, values.astype(jnp.float32), 0.0)
    return jnp.dot(
        kept.astype(jnp.bfloat16), choose[...], preferred_element_type=jnp.float32
    ).astype(jnp.bfloat16)


def my_pairs(occ_ref):
    blk = lax.axis_index("blk_0") * 16 + lax.axis_index("blk_1") * 2 + lax.axis_index("blk_2")
    upper = blk * 5 // 4
    at = blk % 4 * 10
    left = [occ_ref[upper], occ_ref[jnp.minimum(upper + 1, OCC - 1)]]
    row = lax.broadcasted_iota(jnp.int32, (PAIRS, 1), 0)
    column = jnp.zeros((PAIRS, 1), jnp.int32)
    irreps = []
    for m in range(PAIRS):
        later = at + m >= OCC
        right = occ_ref[at + m - jnp.where(later, OCC, 0)]
        irreps.append(jnp.bitwise_xor(jnp.where(later, left[1], left[0]), right))
        column = jnp.where(row == m, irreps[m], column)
    return irreps, column


def count_rows(irreps, need):
    for g in range(IRREPS):
        tiles = jnp.int32(0)
        for irrep in irreps:
            tiles += jnp.where(irrep == g, 1, 0)
        need[g] = (tiles + NARROW - 1) // NARROW


def send_kernel(t_ref, cd_ref, occ_ref, out_ref, choose, need):
    irreps, ranks = places(cd_ref)
    fill_chooser(choose, ranks, 0)
    count_rows(irreps, need)
    pairs, row_irrep = my_pairs(occ_ref)
    packed = pack(t_ref[...], row_irrep, column_irreps(irreps), choose)
    lane = lax.broadcasted_iota(jnp.int32, (1, PAIRS), 1)
    first = jnp.zeros((1, PAIRS), jnp.int32)
    last = jnp.zeros((1, PAIRS), jnp.int32)
    row = jnp.int32(0)
    for m in range(PAIRS):
        rows = need[pairs[m]]
        first = jnp.where(lane == m, jnp.where(rows > 0, row, -1), first)
        last = jnp.where(lane == m, jnp.where(rows > 1, row + 1, -1), last)
        row += rows
    place = lax.broadcasted_iota(jnp.int32, (ROWS, PAIRS), 0)
    width = NARROW * TW
    spread = None
    for part, at in enumerate((first, last)):
        move = jnp.where(place == at, 1.0, 0.0).astype(jnp.bfloat16)
        moved = jnp.dot(
            move, packed[:, part * width : (part + 1) * width], preferred_element_type=jnp.float32
        )
        spread = moved if spread is None else spread + moved
    spread = spread.astype(jnp.bfloat16)
    for s in range(SOURCES):
        out_ref[s] = spread


def send_full_kernel(turn, t_ref, cd_ref, occ_ref, out_ref, choose):
    irreps, ranks = places(cd_ref)
    fill_chooser(choose, ranks, turn)
    _, row_irrep = my_pairs(occ_ref)
    packed = pack(t_ref[...], row_irrep, column_irreps(irreps), choose)
    for s in range(SOURCES):
        out_ref[s, :PAIRS, :] = packed
        out_ref[s, PAIRS:, :] = jnp.zeros((FULL - PAIRS, WIDE * TW), jnp.bfloat16)


def pack_rows_kernel(turn, v_ref, ab_ref, cd_ref, out_ref, choose):
    irreps, ranks = places(cd_ref)
    fill_chooser(choose, ranks, turn)
    row = lax.broadcasted_iota(jnp.int32, (4 * TW, 1), 0) // TW
    row_irrep = jnp.zeros((4 * TW, 1), jnp.int32)
    for i in range(4):
        row_irrep = jnp.where(row == i, ab_ref[i], row_irrep)
    out_ref[...] = pack(v_ref[...], row_irrep, column_irreps(irreps), choose)


def tables_kernel(cd_ref, occ_ref, list_ref, code_ref, kept_ref, orbitals, count, need):
    core = lax.axis_index("blk_2")
    for g in range(IRREPS):
        orbitals[g] = 0

    @pl.loop(0, OCC)
    def _(i):
        g = occ_ref[i]
        orbitals[g] = orbitals[g] + 1

    start = jnp.int32(0)
    most = jnp.int32(0)
    for g in range(IRREPS):
        pairs = jnp.int32(0)
        for h in range(IRREPS):
            pairs += orbitals[h] * orbitals[g ^ h]
        kept_ref[g] = start
        count[g] = start
        start += pairs
        most = jnp.maximum(most, pairs)
    irreps, ranks = places(cd_ref)
    widest = ranks[0]
    for rank in ranks[1:]:
        widest = jnp.maximum(widest, rank)
    count_rows(irreps, need)
    kept_ref[8] = start
    kept_ref[9] = jnp.where(widest < WIDE, 0, 1)
    kept_ref[10] = most
    for k in range(11, KEPT):
        kept_ref[k] = 0

    @pl.loop(0, 8)
    def _(part):
        half = SOURCES * ROWS
        base = [part * 2 * ROWS + jnp.bitwise_xor(other, core) * half for other in range(2)]
        longest = jnp.int32(0)
        row = None
        for i in range(5):
            left = occ_ref[part * 5 + i]
            for j in range(OCC):
                pair = i * OCC + j
                source, m = divmod(pair, PAIRS)
                if m == 0:
                    row = base[source % 2] + source // 2 * ROWS
                    end = row + ROWS
                irrep = jnp.bitwise_xor(left, occ_ref[j])
                at = count[irrep]
                count[irrep] = at + 1
                list_ref[at] = jnp.minimum(row, end - 1)
                code_ref[part * 200 + pair] = at * IRREPS + irrep
                row += need[irrep]
                if m == PAIRS - 1:
                    longest = jnp.maximum(longest, row - end)
        kept_ref[9] = jnp.where(longest > 0, 1, kept_ref[9])

    @pl.loop(0, (LIST - IJ) // 16)
    def _(k):
        for u in range(16):
            list_ref[IJ + k * 16 + u] = 0


def full_list_kernel(occ_ref, kept_ref, list_ref, count):
    core = lax.axis_index("blk_2")
    for g in range(IRREPS):
        count[g] = kept_ref[g]

    @pl.loop(0, OCC)
    def _(i):
        left = occ_ref[i]

        @pl.loop(0, OCC)
        def _(j):
            pair = i * OCC + j
            irrep = jnp.bitwise_xor(left, occ_ref[j])
            at = count[irrep]
            count[irrep] = at + 1
            source = pair // PAIRS
            chip = jnp.bitwise_xor(source & 1, core) * SOURCES + (source >> 1)
            list_ref[at] = chip * FULL + pair - source * PAIRS

    @pl.loop(IJ, LIST)
    def _(k):
        list_ref[k] = 0


def product_kernel(full, round_ref, *refs):
    turns = 2 if full else 1
    half_rows = SOURCES * (FULL if full else ROWS)
    halves, weights = refs[: 2 * turns], refs[2 * turns : 3 * turns]
    ab_ref, list_ref, kept_ref, out_ref, left_product, right_product, dense, both = refs[3 * turns :]
    products = (left_product, right_product)
    wire = dense.shape[0]
    cols = wire - 1
    width = NARROW * TW

    def times(held, weight):
        return lax.dot_general(held, weight, NT, preferred_element_type=jnp.float32)

    for half in range(2):
        if full:
            total = times(halves[half][...], weights[0][...])
            total += times(halves[2 + half][...], weights[1][...])
        else:
            held = halves[half][...]
            total = times(held, weights[0][:, :width])
            following = times(held, weights[0][:, width:])
            total += pltpu.roll(following, half_rows - 1, 0)
        for q in range(2):
            at = slice(half * half_rows, (half + 1) * half_rows)
            products[q][at, :] = total[:, q * 128 : (q + 1) * 128]
    lower = lax.broadcasted_iota(jnp.int32, (1, 128), 1) < TW
    skip = round_ref[0] * cols
    for q in range(2):
        product = products[q]
        dense[...] = jnp.zeros_like(dense)
        irreps = [ab_ref[2 * q + i] for i in range(2)]
        starts = [jnp.minimum(kept_ref[g] + skip, IJ) for g in irreps]
        counts = [kept_ref[g + 1] - kept_ref[g] - skip for g in irreps]
        most = jnp.clip(jnp.maximum(counts[0], counts[1]), 0, cols)

        @pl.loop(0, (most + 7) // 8)
        def _(block):
            base = block * 8
            for u in range(8):
                at = [list_ref[start + base + u] for start in starts]
                rows = [product[pl.ds(a, 1), :] for a in at]
                dense[pl.ds(base + u, 1), :] = jnp.where(lower, rows[0], rows[1])

        both[q * 128 : (q + 1) * 128, :] = dense[...].T
    largest = jnp.max(jnp.max(jnp.abs(both[...]), axis=1, keepdims=True), axis=0, keepdims=True)
    power = 14.0 - jnp.floor(jnp.log2(jnp.maximum(largest, 1e-30)))
    scaled = both[...] * jnp.exp2(power)
    lane = lax.broadcasted_iota(jnp.int32, (4 * TW, wire), 1)
    out_ref[...] = jnp.where(lane == cols, power, scaled).reshape(32, 8, wire)


def spread_kernel(round_ref, ab_ref, kept_ref, code_ref, out_ref):
    irrep = ab_ref[lax.axis_index("panel") // 8]
    cols = WIRES[-1] - 1
    code = code_ref[...]
    first = kept_ref[irrep] + round_ref[0] * cols
    place = jnp.where(code % IRREPS == irrep, code // IRREPS - first, -1)
    place = jnp.where(place < cols, place, -1)
    row = lax.broadcasted_iota(jnp.int32, (WIRES[-1], IJ), 0)
    out_ref[...] = jnp.where(row == place, 1.0, 0.0).astype(jnp.bfloat16)


def finish_kernel(got_ref, spread_ref, out_ref):
    wire = got_ref.shape[2]
    total = None
    for s in range(32):
        got = got_ref[s]
        got = got * jnp.exp2(-got[:, wire - 1 :])
        total = got if total is None else total + got
    high = total.astype(jnp.bfloat16)
    rest = total - high.astype(jnp.float32)
    middle = rest.astype(jnp.bfloat16)
    low = (rest - middle.astype(jnp.float32)).astype(jnp.bfloat16)
    spread = spread_ref[:wire, :]
    parts = [jnp.dot(p, spread, preferred_element_type=jnp.float32) for p in (low, middle, high)]
    out_ref[...] = parts[0] + parts[1] + parts[2]


def shaped(shape, dtype):
    return jax.ShapeDtypeStruct(shape, dtype)


def body(integrals, amplitudes, ab_irrep, cd_irrep, occ_irrep):
    bf16, f32, i32 = jnp.bfloat16, jnp.float32, jnp.int32
    width = WIDE * TW
    chooser = pltpu.VMEM((16 * TW, width), bf16)
    numbers = pltpu.SMEM((IRREPS,), i32)

    def both_cores(sent):
        mine = lax.all_to_all(sent, CHIPS, split_axis=0, concat_axis=0, tiled=True)
        mine = mine.reshape(sent.shape[0] * sent.shape[1], sent.shape[2])
        return [mine, lax.ppermute(mine, "blk_2", [(0, 1), (1, 0)])]

    def gathered_full(turn):
        sent = pl.pallas_call(
            functools.partial(send_full_kernel, turn),
            out_shape=shaped((SOURCES, FULL, width), bf16),
            in_specs=[VMEM, SMEM, SMEM],
            out_specs=VMEM,
            scratch_shapes=[chooser],
        )(amplitudes, cd_irrep, occ_irrep)
        return both_cores(sent)

    def weights(turn):
        return pl.pallas_call(
            functools.partial(pack_rows_kernel, turn),
            out_shape=shaped((4 * TW, width), bf16),
            in_specs=[VMEM, SMEM, SMEM],
            out_specs=VMEM,
            scratch_shapes=[chooser],
        )(integrals, ab_irrep, cd_irrep)

    def spread_of(which):
        return pl.pallas_call(
            spread_kernel,
            out_shape=shaped((WIRES[-1], IJ), bf16),
            in_specs=[SMEM] * 3 + [VMEM],
            out_specs=VMEM,
            name="spread",
        )(which, ab_irrep, kept, code)

    sent = pl.pallas_call(
        send_kernel,
        out_shape=shaped((SOURCES, ROWS, NARROW * TW), bf16),
        in_specs=[VMEM, SMEM, SMEM],
        out_specs=VMEM,
        scratch_shapes=[chooser, numbers],
        name="send",
    )(amplitudes, cd_irrep, occ_irrep)
    halves = both_cores(sent)

    pair_list, code, kept = pl.pallas_call(
        tables_kernel,
        out_shape=[shaped((LIST,), i32), shaped((IJ,), i32), shaped((KEPT,), i32)],
        in_specs=[SMEM, SMEM],
        out_specs=[SMEM] * 3,
        scratch_shapes=[numbers] * 3,
        name="tables",
    )(cd_irrep, occ_irrep)
    code = code.reshape(1, IJ)
    zero = jnp.zeros((1,), i32)
    first_weights, first_spread = weights(0), spread_of(zero)

    def products(full, wire, which, operands, pairs):
        rows = 2 * SOURCES * (FULL if full else ROWS)
        return pl.pallas_call(
            functools.partial(product_kernel, full),
            out_shape=shaped((32, 8, wire), f32),
            in_specs=[SMEM] + [VMEM] * len(operands) + [SMEM] * 3,
            out_specs=VMEM,
            scratch_shapes=[
                pltpu.VMEM((rows, 128), f32),
                pltpu.VMEM((rows, 128), f32),
                pltpu.VMEM((wire, 128), f32),
                pltpu.VMEM((4 * TW, wire), f32),
            ],
        )(which, *operands, ab_irrep, pairs, kept)

    def full_products(wire, which):
        pairs = pl.pallas_call(
            full_list_kernel,
            out_shape=shaped((LIST,), i32),
            in_specs=[SMEM] * 2,
            out_specs=SMEM,
            scratch_shapes=[numbers],
            name="full_list",
        )(occ_irrep, kept)
        operands = [*gathered_full(0), *gathered_full(1), first_weights, weights(1)]
        return products(True, wire, which, operands, pairs)

    general, most = kept[9] > 0, kept[10]

    def reduced(wire, which, spread):
        partial = lax.cond(
            general,
            lambda: full_products(wire, which),
            lambda: products(False, wire, which, [*halves, first_weights], pair_list),
        ).astype(jnp.float16)
        arrived = lax.all_to_all(partial, "panel", split_axis=0, concat_axis=0, tiled=True)
        return pl.pallas_call(
            finish_kernel,
            out_shape=shaped((8, IJ), f32),
            in_specs=[VMEM, VMEM],
            out_specs=VMEM,
            name="finish",
        )(arrived.astype(f32), spread)

    def all_rounds():
        cols = WIRES[-1] - 1

        def add_round(number, total):
            which = jnp.full((1,), number, i32)
            return total + reduced(WIRES[-1], which, spread_of(which))

        return lax.fori_loop(0, (most + cols - 1) // cols, add_round, jnp.zeros((8, IJ), f32))

    branches = [functools.partial(reduced, wire, zero, first_spread) for wire in WIRES]
    chosen = sum((most >= wire).astype(i32) for wire in WIRES)
    return lax.switch(chosen, [*branches, all_rounds])


def solution(mesh):
    split = Mesh(
        mesh.devices.reshape(2, 8, 2, mesh.shape["panel"]), ("blk_0", "blk_1", "blk_2", "panel")
    )
    return jax.shard_map(
        body,
        mesh=split,
        in_specs=(P(BLK, "panel"), P(BLK, "panel"), P(BLK), P("panel"), P()),
        out_specs=P(BLK_PANEL, None),
        check_vma=False,
    )
```

time: 110 us -> 108 us (0.982)
  blocking collectives: 79.2 us -> 75.6 us
  local copies, waits for them, and re-layouts: 3.65 us -> 1.31 us
  Pallas kernels: 22.8 us -> 25 us
    all_to_all x2, blocking collectives: 79.2 us -> 75.6 us  [the longest x1 45.2 us: reduced(): lax.all_to_all(partial, 'panel', split_axis=0, concat_axis=0, tiled=True)]
    pallas_call x3 -> x4, Pallas kernels: 9.51 us -> 12.3 us  [the longest x1 5.97 us: products(): pl.pallas_call(functools.partial(product_kernel, full), out_shape=shaped(...]
    convert_element_type x2, other arithmetic: 0.21 us -> 2.02 us  [the longest x1 1.13 us: reduced(): partial = lax.cond(general, lambda: full_products(wire, which), lambda: p...]
    all_to_all x1 -> x0, local copies, waits for them, and re-layouts: 1.6 us -> none  [reduced(): lax.all_to_all(sent, 'panel', split_axis=0, concat_axis=0, tiled=True)]
  transfers between devices with their start and end apart: 1 -> 1, of which waited for: 0 -> 0; matrix products, arithmetic and copies ran while one was open for 1% -> 1% of each run, Pallas kernels for 12% -> 13%
where the time goes in v3:
time: 108 us
  blocking collectives  75.6 us (70%)
  Pallas kernels  25 us (23%)
  other arithmetic  2.02 us (2%)
  between operations  1.96 us (2%)
  starting transfers between devices  1.91 us (2%)
  local copies, waits for them, and re-layouts  1.31 us (1%)
    all_to_all x1, blocking collectives, reduced(): lax.all_to_all(partial, 'panel', split_axis=0, concat_axis=0, tiled=True)  45.2 us
    all_to_all x1, blocking collectives, both_cores(): mine = lax.all_to_all(sent, CHIPS, split_axis=0, concat_axis=0, tiled=True)  30.5 us
    pallas_call x1, Pallas kernels, body(): pl.pallas_call(tables_kernel, out_shape=[shaped((LIST,), i32), shaped((IJ...  11.2 us
    pallas_call x1, Pallas kernels, products(): pl.pallas_call(functools.partial(product_kernel, full), out_shape=shaped(...  5.97 us
    pallas_call x1, Pallas kernels, reduced(): pl.pallas_call(finish_kernel, out_shape=shaped((8, IJ), f32), in_specs=[V...  2.76 us
    pallas_call x1, Pallas kernels, body(): pl.pallas_call(send_kernel, out_shape=shaped((SOURCES, ROWS, NARROW * TW)...  2.67 us
  transfers between devices with their start and end apart: 1, of which 0 were waited for; matrix products, arithmetic and copies ran while one was open for 1% of the time, Pallas kernels for 13%

profile of v3, /device:TPU:2, one launch (start us, length us, event | category | flops | bytes accessed | tf_op | source)
XLA Modules:
  0.0 107.9 jit_solution(14141375074685536679)
XLA Ops:
  0.0 0.0 copy-start.3
  0.0 0.0 copy-start.4
  0.0 0.0 copy-start.2
  0.0 2.7 %send.1 = bf16[16,88,256]{2,1,0:T(8,128)(2,1)} custom-call(bf16[50,1024]{1,0:T(8,128)(2,1)} %t_ref.1, s32[16]{0:T(128)} %cd_ref.5, s32[40]{0:T(128)} %occ_ref.3), custom_call_target="tpu_custom_call" | custom-call | tf_op jit(solution)/shard_map/send/pallas_call | solution.py:350
  2.7 30.5 %all_to_all.45 = bf16[16,88,256]{2,1,0:T(8,128)(2,1)S(1)} all-to-all(bf16[16,88,256]{2,1,0:T(8,128)(2,1)} %send.1), channel_id=1, replica_groups=mesh['blk_0'=2,'blk_1'=8,'blk_2'=2,'panel'=32] {'blk_0','blk_1'}, dimensions={0} | all-to-all | bytes 1441792 | tf_op jit(solution)/shard_map/all_to_all | solution.py:318
  33.2 1.9 %collective-permute-start.6 = (bf16[1408,256]{1,0:T(8,128)(2,1)S(1)}, bf16[1408,256]{1,0:T(8,128)(2,1)}, u32[]{:S(2)}, u32[]{:S(2)}) collective-permute-start(bf16[1408,256]{1,0:T(8,128)(2,1)S(1)} %bitcast.16), channel_id=1, source_target_pairs={{0,32},{32,0},{1,33},{33,1},{2,34},{34,2},{3,35},{35,3},{4,36},{36... | collective-permute-start | bytes 2162696 | tf_op jit(solution)/shard_map/ppermute | solution.py:320
  35.1 0.0 copy-done.3
  35.1 0.0 copy-done.4
  35.1 11.2 %tables.1 = (s32[2304]{0:T(1024)S(1)}, s32[1600]{0:T(1024)}, s32[16]{0:T(128)S(1)}) custom-call(s32[16]{0:T(128)S(1)} %copy-done.3, s32[40]{0:T(128)S(1)} %copy-done.4), custom_call_target="tpu_custom_call" | custom-call | tf_op jit(solution)/shard_map/tables/pallas_call | solution.py:360
  46.3 0.7 reshape.27.code_ref
  47.0 0.6 fusion
  48.3 0.0 copy-done.2
  48.3 1.5 %shard_map.58 = bf16[256,512]{1,0:T(8,128)(2,1)S(1)} custom-call(bf16[256,1024]{1,0:T(8,128)(2,1)} %v_ref.1, s32[4]{0:T(128)S(1)} %copy-done.2, s32[16]{0:T(128)S(1)} %copy-done.3), custom_call_target="tpu_custom_call" | custom-call | tf_op jit(solution)/shard_map/pallas_call | solution.py:333
  49.8 0.9 spread.2
  52.0 0.0 collective-permute-done.6
  52.0 56.0 %conditional.4 = (f32[8,1600]{1,0:T(8,128)}) conditional(s32[]{:T(128)} %clamp.3, (pred[]{:T(512)}, bf16[1408,256]{1,0:T(8,128)(2,1)S(1)}, bf16[1408,256]{1,0:T(8,128)(2,1)}, bf16[256,512]{1,0:T(8,128)(2,1)S(1)}, s32[4]{0:T(128)S(1)}, /*index=5*/s32[2304]{0:T(1024)S(1)}, s32[16]{0:T(128)S(1)}, bf16[50,1024]{1,0:T(8,128)(2,1)}, ...), branch_computations={%region_0.0_spmd, %region_3.0_spmd, %region_6.11_spmd} | conditional | flops 340492 | bytes 23339758 | solution.py:427
  52.0 6.0 %conditional.1 = (f32[32,8,640]{2,1,0:T(8,128)}) conditional(s32[]{:T(128)} %convert_element_type.25, (bf16[1408,256]{1,0:T(8,128)(2,1)S(1)}, bf16[1408,256]{1,0:T(8,128)(2,1)}, bf16[256,512]{1,0:T(8,128)(2,1)S(1)}, s32[4]{0:T(128)S(1)}, s32[2304]{0:T(1024)S(1)}, /*index=5*/s32[16]{0:T(128)S(1)}) %tuple.27, (bf16[50,1024]{1,0:T(8,128)(2,1)}, ...), branch_computations={%region_4.0_spmd, %region_5.0_spmd} | conditional | bytes 12845208 | solution.py:402
  52.0 6.0 %branch_0_fun.4 = f32[32,8,640]{2,1,0:T(8,128)} custom-call(s32[1]{0:T(128)} %constant.13.clone.round_ref, bf16[1408,256]{1,0:T(8,128)(2,1)S(1)} %get-tuple-element.259.refs_0_, bf16[1408,256]{1,0:T(8,128)(2,1)} %get-tuple-element.260.refs_1_, bf16[256,512]{1,0:T(8,128)(2,1)S(1)} %get-tuple-element.261.refs_2_, s32[4]{0:T(128)S(1)} %get-tuple-element.262.refs_3_, ...), custom_call_target="tpu_custom_call" | custom-call | tf_op jit(solution)/shard_map/cond/branch_1_fun/cond/branch_0_fun/pallas_call | solution.py:374
  58.0 1.1 %convert_element_type.26 = f16[32,8,640]{2,1,0:T(8,128)(2,1)S(1)} convert(f32[32,8,640]{2,1,0:T(8,128)} %get-tuple-element.513) | non-fusion elementwise | flops 163840 | bytes 983040 | tf_op jit(solution)/shard_map/cond/branch_1_fun/convert_element_type | solution.py:406
  59.1 45.2 %all_to_all.44 = f16[32,8,640]{2,1,0:T(8,128)(2,1)S(1)} all-to-all(f16[32,8,640]{2,1,0:T(8,128)(2,1)S(1)} %convert_element_type.26), channel_id=1, replica_groups=mesh['blk_0'=2,'blk_1'=8,'blk_2'=2,'panel'=32] {'panel'}, dimensions={0} | all-to-all | bytes 655360 | tf_op jit(solution)/shard_map/cond/branch_1_fun/all_to_all | solution.py:407
  104.3 0.9 convert_element_type.27.got_ref
  105.2 2.8 %finish.4 = f32[8,1600]{1,0:T(8,128)} custom-call(f32[32,8,640]{2,1,0:T(8,128)} %convert_element_type.27.got_ref, bf16[640,1600]{1,0:T(8,128)(2,1)S(1)} %get-tuple-element.283.spread_ref), custom_call_target="tpu_custom_call" | custom-call | tf_op jit(solution)/shard_map/cond/branch_1_fun/finish/pallas_call | solution.py:408
Async XLA Ops:
  0.0 35.1 %copy-start.3 = (s32[16]{0:T(128)S(1)}, s32[16]{0:T(128)}, u32[]{:S(2)}) copy-start(s32[16]{0:T(128)} %cd_ref.5) | copy-start | bytes 196
  0.0 35.1 %copy-start.4 = (s32[40]{0:T(128)S(1)}, s32[40]{0:T(128)}, u32[]{:S(2)}) copy-start(s32[40]{0:T(128)} %occ_ref.3) | copy-start | bytes 484
  0.0 48.3 %copy-start.2 = (s32[4]{0:T(128)S(1)}, s32[4]{0:T(128)}, u32[]{:S(2)}) copy-start(s32[4]{0:T(128)} %ab_ref.3) | copy-start | bytes 52
  33.2 18.8 %collective-permute-start.6 = (bf16[1408,256]{1,0:T(8,128)(2,1)S(1)}, bf16[1408,256]{1,0:T(8,128)(2,1)}, u32[]{:S(2)}, u32[]{:S(2)}) collective-permute-start(bf16[1408,256]{1,0:T(8,128)(2,1)S(1)} %bitcast.16), channel_id=1, source_target_pairs={{0,32},{32,0},{1,33},{33,1},{2,34},{34,2},{3,35},{35,3},{4,36},{36... | collective-permute-start | bytes 2162696 | tf_op jit(solution)/shard_map/ppermute | solution.py:320

commit v4 on v3

--- a/solution.py
+++ b/solution.py
@@ -20,16 +20,21 @@
 PAIRS = 50
 SOURCES = 16
 WIDE = 8
-NARROW = 4
-ROWS = 88
+NARROW = 2
+PARTS = WIDE // NARROW
+ROWS = 136
 FULL = 56
 WIRES = (512, 640)
+CODES = 1664
+NOWHERE = 1 << 24
 LIST = 2304
 KEPT = 16
 
 SMEM = pl.BlockSpec(memory_space=pltpu.SMEM)
 VMEM = pl.BlockSpec(memory_space=pltpu.VMEM)
 NT = (((1,), (1,)), ((), ()))
+GRANT = pltpu.CompilerParams(vmem_limit_bytes=24 << 20)
+LARGE = pltpu.CompilerParams(vmem_limit_bytes=40 << 20)
 
 
 def places(cd_ref):
@@ -100,17 +105,18 @@
     packed = pack(t_ref[...], row_irrep, column_irreps(irreps), choose)
     lane = lax.broadcasted_iota(jnp.int32, (1, PAIRS), 1)
     first = jnp.zeros((1, PAIRS), jnp.int32)
-    last = jnp.zeros((1, PAIRS), jnp.int32)
+    count = jnp.zeros((1, PAIRS), jnp.int32)
     row = jnp.int32(0)
     for m in range(PAIRS):
         rows = need[pairs[m]]
-        first = jnp.where(lane == m, jnp.where(rows > 0, row, -1), first)
-        last = jnp.where(lane == m, jnp.where(rows > 1, row + 1, -1), last)
+        first = jnp.where(lane == m, row, first)
+        count = jnp.where(lane == m, rows, count)
         row += rows
     place = lax.broadcasted_iota(jnp.int32, (ROWS, PAIRS), 0)
     width = NARROW * TW
     spread = None
-    for part, at in enumerate((first, last)):
+    for part in range(PARTS):
+        at = jnp.where(count > part, first + part, -1)
         move = jnp.where(place == at, 1.0, 0.0).astype(jnp.bfloat16)
         moved = jnp.dot(
             move, packed[:, part * width : (part + 1) * width], preferred_element_type=jnp.float32
@@ -196,6 +202,9 @@
                     longest = jnp.maximum(longest, row - end)
         kept_ref[9] = jnp.where(longest > 0, 1, kept_ref[9])
 
+    for k in range(IJ, CODES):
+        code_ref[k] = NOWHERE
+
     @pl.loop(0, (LIST - IJ) // 16)
     def _(k):
         for u in range(16):
@@ -234,7 +243,6 @@
     products = (left_product, right_product)
     wire = dense.shape[0]
     cols = wire - 1
-    width = NARROW * TW
 
     def times(held, weight):
         return lax.dot_general(held, weight, NT, preferred_element_type=jnp.float32)
@@ -244,10 +252,10 @@
             total = times(halves[half][...], weights[0][...])
             total += times(halves[2 + half][...], weights[1][...])
         else:
-            held = halves[half][...]
-            total = times(held, weights[0][:, :width])
-            following = times(held, weights[0][:, width:])
-            total += pltpu.roll(following, half_rows - 1, 0)
+            held = halves[half][...].astype(jnp.float32)
+            rows = [held] + [pltpu.roll(held, half_rows - part, 0) for part in range(1, PARTS)]
+            joined = jnp.concatenate([r.astype(jnp.bfloat16) for r in rows], axis=1)
+            total = times(joined, weights[0][...])
         for q in range(2):
             at = slice(half * half_rows, (half + 1) * half_rows)
             products[q][at, :] = total[:, q * 128 : (q + 1) * 128]
@@ -277,31 +285,27 @@
     out_ref[...] = jnp.where(lane == cols, power, scaled).reshape(32, 8, wire)
 
 
-def spread_kernel(round_ref, ab_ref, kept_ref, code_ref, out_ref):
+def finish_kernel(round_ref, got_ref, ab_ref, kept_ref, code_ref, out_ref):
     irrep = ab_ref[lax.axis_index("panel") // 8]
-    cols = WIRES[-1] - 1
-    code = code_ref[...]
-    first = kept_ref[irrep] + round_ref[0] * cols
-    place = jnp.where(code % IRREPS == irrep, code // IRREPS - first, -1)
-    place = jnp.where(place < cols, place, -1)
-    row = lax.broadcasted_iota(jnp.int32, (WIRES[-1], IJ), 0)
-    out_ref[...] = jnp.where(row == place, 1.0, 0.0).astype(jnp.bfloat16)
-
-
-def finish_kernel(got_ref, spread_ref, out_ref):
     wire = got_ref.shape[2]
+    cols = wire - 1
     total = None
     for s in range(32):
         got = got_ref[s]
-        got = got * jnp.exp2(-got[:, wire - 1 :])
+        got = got * jnp.exp2(-got[:, cols:])
         total = got if total is None else total + got
-    high = total.astype(jnp.bfloat16)
-    rest = total - high.astype(jnp.float32)
-    middle = rest.astype(jnp.bfloat16)
-    low = (rest - middle.astype(jnp.float32)).astype(jnp.bfloat16)
-    spread = spread_ref[:wire, :]
-    parts = [jnp.dot(p, spread, preferred_element_type=jnp.float32) for p in (low, middle, high)]
-    out_ref[...] = parts[0] + parts[1] + parts[2]
+    first = kept_ref[irrep] + round_ref[0] * cols
+    for block in range(CODES // 128):
+        code = jnp.broadcast_to(code_ref[:, block * 128 : (block + 1) * 128], (8, 128))
+        place = jnp.where(code % IRREPS == irrep, code // IRREPS - first, -1)
+        place = jnp.where(place < cols, place, -1)
+        lane = place & 127
+        found = jnp.zeros((8, 128), jnp.float32)
+        for k in range(wire // 128):
+            moved = jnp.take_along_axis(total[:, k * 128 : (k + 1) * 128], lane, axis=1)
+            found = jnp.where(place >> 7 == k, moved, found)
+        held = min(128, IJ - block * 128)
+        out_ref[:, block * 128 : block * 128 + held] = found[:, :held]
 
 
 def shaped(shape, dtype):
@@ -326,6 +330,7 @@
             in_specs=[VMEM, SMEM, SMEM],
             out_specs=VMEM,
             scratch_shapes=[chooser],
+            compiler_params=GRANT,
         )(amplitudes, cd_irrep, occ_irrep)
         return both_cores(sent)
 
@@ -336,16 +341,8 @@
             in_specs=[VMEM, SMEM, SMEM],
             out_specs=VMEM,
             scratch_shapes=[chooser],
+            compiler_params=GRANT,
         )(integrals, ab_irrep, cd_irrep)
-
-    def spread_of(which):
-        return pl.pallas_call(
-            spread_kernel,
-            out_shape=shaped((WIRES[-1], IJ), bf16),
-            in_specs=[SMEM] * 3 + [VMEM],
-            out_specs=VMEM,
-            name="spread",
-        )(which, ab_irrep, kept, code)
 
     sent = pl.pallas_call(
         send_kernel,
@@ -353,21 +350,23 @@
         in_specs=[VMEM, SMEM, SMEM],
         out_specs=VMEM,
         scratch_shapes=[chooser, numbers],
+        compiler_params=GRANT,
         name="send",
     )(amplitudes, cd_irrep, occ_irrep)
     halves = both_cores(sent)
 
     pair_list, code, kept = pl.pallas_call(
         tables_kernel,
-        out_shape=[shaped((LIST,), i32), shaped((IJ,), i32), shaped((KEPT,), i32)],
+        out_shape=[shaped((LIST,), i32), shaped((CODES,), i32), shaped((KEPT,), i32)],
         in_specs=[SMEM, SMEM],
         out_specs=[SMEM] * 3,
         scratch_shapes=[numbers] * 3,
+        compiler_params=GRANT,
         name="tables",
     )(cd_irrep, occ_irrep)
-    code = code.reshape(1, IJ)
+    code = code.reshape(1, CODES)
     zero = jnp.zeros((1,), i32)
-    first_weights, first_spread = weights(0), spread_of(zero)
+    first_weights = weights(0)
 
     def products(full, wire, which, operands, pairs):
         rows = 2 * SOURCES * (FULL if full else ROWS)
@@ -382,6 +381,7 @@
                 pltpu.VMEM((wire, 128), f32),
                 pltpu.VMEM((4 * TW, wire), f32),
             ],
+            compiler_params=LARGE,
         )(which, *operands, ab_irrep, pairs, kept)
 
     def full_products(wire, which):
@@ -391,6 +391,7 @@
             in_specs=[SMEM] * 2,
             out_specs=SMEM,
             scratch_shapes=[numbers],
+            compiler_params=GRANT,
             name="full_list",
         )(occ_irrep, kept)
         operands = [*gathered_full(0), *gathered_full(1), first_weights, weights(1)]
@@ -398,7 +399,7 @@
 
     general, most = kept[9] > 0, kept[10]
 
-    def reduced(wire, which, spread):
+    def reduced(wire, which):
         partial = lax.cond(
             general,
             lambda: full_products(wire, which),
@@ -408,21 +409,22 @@
         return pl.pallas_call(
             finish_kernel,
             out_shape=shaped((8, IJ), f32),
-            in_specs=[VMEM, VMEM],
+            in_specs=[SMEM, VMEM, SMEM, SMEM, VMEM],
             out_specs=VMEM,
+            compiler_params=GRANT,
             name="finish",
-        )(arrived.astype(f32), spread)
+        )(which, arrived.astype(f32), ab_irrep, kept, code)
 
     def all_rounds():
         cols = WIRES[-1] - 1
 
         def add_round(number, total):
             which = jnp.full((1,), number, i32)
-            return total + reduced(WIRES[-1], which, spread_of(which))
+            return total + reduced(WIRES[-1], which)
 
         return lax.fori_loop(0, (most + cols - 1) // cols, add_round, jnp.zeros((8, IJ), f32))
 
-    branches = [functools.partial(reduced, wire, zero, first_spread) for wire in WIRES]
+    branches = [functools.partial(reduced, wire, zero) for wire in WIRES]
     chosen = sum((most >= wire).astype(i32) for wire in WIRES)
     return lax.switch(chosen, [*branches, all_rounds])
 

time: 108 us -> 103 us (0.954)
  Pallas kernels: 25 us -> 22.7 us
  blocking collectives: 75.6 us -> 74.2 us
    pallas_call x3 -> x2, Pallas kernels: 14.9 us -> 12.7 us  [the longest x1 11.2 us: body(): pl.pallas_call(tables_kernel, out_shape=[shaped((LIST,), i32), shaped((CO...]
    all_to_all x1, blocking collectives: 30.5 us -> 29 us  [both_cores(): mine = lax.all_to_all(sent, CHIPS, split_axis=0, concat_axis=0, tiled=True)]
where the time goes in v4:
time: 103 us
  blocking collectives  74.2 us (72%)
  Pallas kernels  22.7 us (22%)
  starting transfers between devices  2.04 us (2%)
  between operations  2.02 us (2%)
  other arithmetic  1.17 us (1%)
    all_to_all x1, blocking collectives, reduced(): lax.all_to_all(partial, 'panel', split_axis=0, concat_axis=0, tiled=True)  45.2 us
    all_to_all x1, blocking collectives, both_cores(): mine = lax.all_to_all(sent, CHIPS, split_axis=0, concat_axis=0, tiled=True)  29 us
    pallas_call x1, Pallas kernels, body(): pl.pallas_call(tables_kernel, out_shape=[shaped((LIST,), i32), shaped((CO...  11.2 us
    pallas_call x1, Pallas kernels, products(): pl.pallas_call(functools.partial(product_kernel, full), out_shape=shaped(...  6.53 us
  transfers between devices with their start and end apart: 1, of which 0 were waited for; matrix products, arithmetic and copies ran while one was open for 1% of the time, Pallas kernels for 13%

profile of v4, /device:TPU:2, one launch (start us, length us, event | category | flops | bytes accessed | tf_op | source)
XLA Modules:
  0.0 102.8 jit_solution(15406909860819585744)
XLA Ops:
  0.0 1.7 %send.1 = bf16[16,136,128]{2,1,0:T(8,128)(2,1)S(1)} custom-call(bf16[50,1024]{1,0:T(8,128)(2,1)} %t_ref.1, s32[16]{0:T(128)} %cd_ref.5, s32[40]{0:T(128)} %occ_ref.3), custom_call_target="tpu_custom_call" | custom-call | tf_op jit(solution)/shard_map/send/pallas_call | solution.py:347
  1.8 0.0 copy-start
  1.8 29.0 %all_to_all.45 = bf16[16,136,128]{2,1,0:T(8,128)(2,1)} all-to-all(bf16[16,136,128]{2,1,0:T(8,128)(2,1)S(1)} %send.1), channel_id=1, replica_groups=mesh['blk_0'=2,'blk_1'=8,'blk_2'=2,'panel'=32] {'blk_0','blk_1'}, dimensions={0} | all-to-all | bytes 1114112 | tf_op jit(solution)/shard_map/all_to_all | solution.py:322
  30.8 0.0 copy-start.5
  30.8 0.0 copy-start.6
  30.8 2.0 %collective-permute-start.6 = (bf16[2176,128]{1,0:T(8,128)(2,1)}, bf16[2176,128]{1,0:T(8,128)(2,1)}, u32[]{:S(2)}, u32[]{:S(2)}) collective-permute-start(bf16[2176,128]{1,0:T(8,128)(2,1)} %bitcast.9), channel_id=1, source_target_pairs={{0,32},{32,0},{1,33},{33,1},{2,34},{34,2},{3,35},{35,3},{4,36},{36... | collective-permute-start | bytes 1671176 | tf_op jit(solution)/shard_map/ppermute | solution.py:324
  32.8 0.0 copy-done.5
  32.9 0.0 copy-done.6
  32.9 11.2 %tables.1 = (s32[2304]{0:T(1024)S(1)}, s32[1664]{0:T(1024)S(1)}, s32[16]{0:T(128)S(1)}) custom-call(s32[16]{0:T(128)S(1)} %copy-done.5, s32[40]{0:T(128)S(1)} %copy-done.6), custom_call_target="tpu_custom_call" | custom-call | tf_op jit(solution)/shard_map/tables/pallas_call | solution.py:358
  44.1 0.6 fusion
  46.0 0.0 copy-start.4
  46.7 0.0 copy-done
  46.7 0.0 copy-done.4
  46.7 0.0 copy-start.3
  46.7 1.7 %shard_map.58 = bf16[256,512]{1,0:T(8,128)(2,1)} custom-call(bf16[256,1024]{1,0:T(8,128)(2,1)S(1)} %copy-done, s32[4]{0:T(128)S(1)} %copy-done.4, s32[16]{0:T(128)S(1)} %copy-done.5), custom_call_target="tpu_custom_call" | custom-call | tf_op jit(solution)/shard_map/pallas_call | solution.py:338
  48.4 0.0 collective-permute-done.6
  48.4 0.0 copy-done.3
  48.4 54.4 %conditional.4 = (f32[8,1600]{1,0:T(8,128)}) conditional(s32[]{:T(128)} %clamp.3, (pred[]{:T(512)}, bf16[2176,128]{1,0:T(8,128)(2,1)}, bf16[2176,128]{1,0:T(8,128)(2,1)}, bf16[256,512]{1,0:T(8,128)(2,1)}, s32[4]{0:T(128)S(1)}, /*index=5*/s32[2304]{0:T(1024)S(1)}, s32[16]{0:T(128)S(1)}, bf16[50,1024]{1,0:T(8,128)(2,1)S(1)}, ...), branch_computations={%region_0.0_spmd, %region_3.0_spmd, %region_6.11_spmd} | conditional | flops 340492 | bytes 20195374 | solution.py:429
  48.4 6.5 %conditional.1 = (f32[32,8,640]{2,1,0:T(8,128)}) conditional(s32[]{:T(128)} %convert_element_type.25, (bf16[2176,128]{1,0:T(8,128)(2,1)}, bf16[2176,128]{1,0:T(8,128)(2,1)}, bf16[256,512]{1,0:T(8,128)(2,1)}, s32[4]{0:T(128)S(1)}, s32[2304]{0:T(1024)S(1)}, /*index=5*/s32[16]{0:T(128)S(1)}) %tuple.27, (bf16[50,1024]{1,0:T(8,128)(2,1)S(1)}, ...), branch_computations={%region_4.0_spmd, %region_5.0_spmd} | conditional | bytes 12845208 | solution.py:403
  48.4 6.5 %branch_0_fun.4 = f32[32,8,640]{2,1,0:T(8,128)} custom-call(s32[1]{0:T(128)} %constant.16.clone.round_ref, bf16[2176,128]{1,0:T(8,128)(2,1)} %get-tuple-element.259.refs_0_, bf16[2176,128]{1,0:T(8,128)(2,1)} %get-tuple-element.260.refs_1_, bf16[256,512]{1,0:T(8,128)(2,1)} %get-tuple-element.261.refs_2_, s32[4]{0:T(128)S(1)} %get-tuple-element.262.refs_3_, ...), custom_call_target="tpu_custom_call" | custom-call | tf_op jit(solution)/shard_map/cond/branch_1_fun/cond/branch_0_fun/pallas_call | solution.py:373
  55.0 1.1 %convert_element_type.26 = f16[32,8,640]{2,1,0:T(8,128)(2,1)S(1)} convert(f32[32,8,640]{2,1,0:T(8,128)} %get-tuple-element.513) | non-fusion elementwise | flops 163840 | bytes 983040 | tf_op jit(solution)/shard_map/cond/branch_1_fun/convert_element_type | solution.py:407
  56.1 45.2 %all_to_all.44 = f16[32,8,640]{2,1,0:T(8,128)(2,1)S(1)} all-to-all(f16[32,8,640]{2,1,0:T(8,128)(2,1)S(1)} %convert_element_type.26), channel_id=1, replica_groups=mesh['blk_0'=2,'blk_1'=8,'blk_2'=2,'panel'=32] {'panel'}, dimensions={0} | all-to-all | bytes 655360 | tf_op jit(solution)/shard_map/cond/branch_1_fun/all_to_all | solution.py:408
  101.3 1.5 %finish.4 = f32[8,1600]{1,0:T(8,128)} custom-call(s32[1]{0:T(128)} %constant.18.clone.round_ref, f32[32,8,640]{2,1,0:T(8,128)S(1)} %convert_element_type.27.got_ref, s32[4]{0:T(128)S(1)} %get-tuple-element.276.ab_ref, s32[16]{0:T(128)S(1)} %get-tuple-element.278.kept_ref, s32[1,1664]{1,0:T(1,128)S(1)} %get-tuple-element.283.code_ref), custom_call_target="tpu_custom_call" | custom-call | tf_op jit(solution)/shard_map/cond/branch_1_fun/finish/pallas_call | solution.py:409
  (2 shorter events, 0.1 us)
Async XLA Ops:
  1.8 44.9 %copy-start = (bf16[256,1024]{1,0:T(8,128)(2,1)S(1)}, bf16[256,1024]{1,0:T(8,128)(2,1)}, u32[]{:S(2)}) copy-start(bf16[256,1024]{1,0:T(8,128)(2,1)} %v_ref.1) | copy-start | bytes 1572868
  30.8 2.1 %copy-start.5 = (s32[16]{0:T(128)S(1)}, s32[16]{0:T(128)}, u32[]{:S(2)}) copy-start(s32[16]{0:T(128)} %cd_ref.5) | copy-start | bytes 196
  30.8 2.1 %copy-start.6 = (s32[40]{0:T(128)S(1)}, s32[40]{0:T(128)}, u32[]{:S(2)}) copy-start(s32[40]{0:T(128)} %occ_ref.3) | copy-start | bytes 484
  30.8 17.6 %collective-permute-start.6 = (bf16[2176,128]{1,0:T(8,128)(2,1)}, bf16[2176,128]{1,0:T(8,128)(2,1)}, u32[]{:S(2)}, u32[]{:S(2)}) collective-permute-start(bf16[2176,128]{1,0:T(8,128)(2,1)} %bitcast.9), channel_id=1, source_target_pairs={{0,32},{32,0},{1,33},{33,1},{2,34},{34,2},{3,35},{35,3},{4,36},{36... | collective-permute-start | bytes 1671176 | tf_op jit(solution)/shard_map/ppermute | solution.py:324
  46.0 0.7 copy-start.4
  46.7 1.7 %copy-start.3 = (bf16[50,1024]{1,0:T(8,128)(2,1)S(1)}, bf16[50,1024]{1,0:T(8,128)(2,1)}, u32[]{:S(2)}) copy-start(bf16[50,1024]{1,0:T(8,128)(2,1)} %t_ref.1) | copy-start | bytes 307204

commit v5 on v4

--- a/solution.py
+++ b/solution.py
@@ -32,6 +32,7 @@
 
 SMEM = pl.BlockSpec(memory_space=pltpu.SMEM)
 VMEM = pl.BlockSpec(memory_space=pltpu.VMEM)
+ANY = pl.BlockSpec(memory_space=pl.ANY)
 NT = (((1,), (1,)), ((), ()))
 GRANT = pltpu.CompilerParams(vmem_limit_bytes=24 << 20)
 LARGE = pltpu.CompilerParams(vmem_limit_bytes=40 << 20)
@@ -235,30 +236,54 @@
         list_ref[k] = 0
 
 
+def times(held, weight):
+    return lax.dot_general(held, weight, NT, preferred_element_type=jnp.float32)
+
+
+def joined_product(held_ref, weight_ref):
+    held = held_ref[...].astype(jnp.float32)
+    count = held.shape[0]
+    rows = [held] + [pltpu.roll(held, count - part, 0) for part in range(1, PARTS)]
+    joined = jnp.concatenate([r.astype(jnp.bfloat16) for r in rows], axis=1)
+    return times(joined, weight_ref[...])
+
+
+def own_product_kernel(held_ref, weight_ref, left_ref, right_ref):
+    total = joined_product(held_ref, weight_ref)
+    left_ref[...] = total[:, :128]
+    right_ref[...] = total[:, 128:]
+
+
 def product_kernel(full, round_ref, *refs):
-    turns = 2 if full else 1
-    half_rows = SOURCES * (FULL if full else ROWS)
-    halves, weights = refs[: 2 * turns], refs[2 * turns : 3 * turns]
-    ab_ref, list_ref, kept_ref, out_ref, left_product, right_product, dense, both = refs[3 * turns :]
+    if full:
+        halves, weights, refs = refs[:4], refs[4:6], refs[6:]
+    else:
+        (*own, other, weight), refs = refs[:4], refs[4:]
+    ab_ref, list_ref, kept_ref, out_ref, left_product, right_product, dense, both, sems = refs
     products = (left_product, right_product)
     wire = dense.shape[0]
     cols = wire - 1
-
-    def times(held, weight):
-        return lax.dot_general(held, weight, NT, preferred_element_type=jnp.float32)
-
-    for half in range(2):
-        if full:
+    half_rows = SOURCES * (FULL if full else ROWS)
+
+    def keep(half, total):
+        at = slice(half * half_rows, (half + 1) * half_rows)
+        for q in range(2):
+            products[q][at, :] = total[:, q * 128 : (q + 1) * 128]
+
+    if full:
+        for half in range(2):
             total = times(halves[half][...], weights[0][...])
-            total += times(halves[2 + half][...], weights[1][...])
-        else:
-            held = halves[half][...].astype(jnp.float32)
-            rows = [held] + [pltpu.roll(held, half_rows - part, 0) for part in range(1, PARTS)]
-            joined = jnp.concatenate([r.astype(jnp.bfloat16) for r in rows], axis=1)
-            total = times(joined, weights[0][...])
-        for q in range(2):
-            at = slice(half * half_rows, (half + 1) * half_rows)
-            products[q][at, :] = total[:, q * 128 : (q + 1) * 128]
+            keep(half, total + times(halves[2 + half][...], weights[1][...]))
+    else:
+        copies = [
+            pltpu.make_async_copy(own[q], products[q].at[pl.ds(0, half_rows)], sems.at[q])
+            for q in range(2)
+        ]
+        for copy in copies:
+            copy.start()
+        keep(1, joined_product(other, weight))
+        for copy in copies:
+            copy.wait()
     lower = lax.broadcasted_iota(jnp.int32, (1, 128), 1) < TW
     skip = round_ref[0] * cols
     for q in range(2):
@@ -368,18 +393,30 @@
     zero = jnp.zeros((1,), i32)
     first_weights = weights(0)
 
+    half_rows = SOURCES * ROWS
+    own = pl.pallas_call(
+        own_product_kernel,
+        out_shape=[shaped((half_rows, 128), f32)] * 2,
+        in_specs=[VMEM, VMEM],
+        out_specs=[VMEM] * 2,
+        compiler_params=GRANT,
+        name="own_product",
+    )(halves[0], first_weights)
+
     def products(full, wire, which, operands, pairs):
         rows = 2 * SOURCES * (FULL if full else ROWS)
+        specs = [VMEM] * 6 if full else [ANY, ANY, VMEM, VMEM]
         return pl.pallas_call(
             functools.partial(product_kernel, full),
-            out_shape=shaped((32, 8, wire), f32),
-            in_specs=[SMEM] + [VMEM] * len(operands) + [SMEM] * 3,
+            out_shape=pltpu.VMEM((32, 8, wire), f32),
+            in_specs=[SMEM] + specs + [SMEM] * 3,
             out_specs=VMEM,
             scratch_shapes=[
                 pltpu.VMEM((rows, 128), f32),
                 pltpu.VMEM((rows, 128), f32),
                 pltpu.VMEM((wire, 128), f32),
                 pltpu.VMEM((4 * TW, wire), f32),
+                pltpu.SemaphoreType.DMA((2,)),
             ],
             compiler_params=LARGE,
         )(which, *operands, ab_irrep, pairs, kept)
@@ -403,7 +440,7 @@
         partial = lax.cond(
             general,
             lambda: full_products(wire, which),
-            lambda: products(False, wire, which, [*halves, first_weights], pair_list),
+            lambda: products(False, wire, which, [*own, halves[1], first_weights], pair_list),
         ).astype(jnp.float16)
         arrived = lax.all_to_all(partial, "panel", split_axis=0, concat_axis=0, tiled=True)
         return pl.pallas_call(

time: 103 us -> 105 us (1.019)
  Pallas kernels: 22.7 us -> 25.7 us
  other arithmetic: 1.17 us -> 0.08 us
    pallas_call x1 -> x2, Pallas kernels: 6.53 us -> 8.93 us  [the longest x1 5.81 us: products(): pl.pallas_call(functools.partial(product_kernel, full), out_shape=pltpu.V...]
    convert_element_type x1, other arithmetic: 1.13 us -> 0.04 us  [reduced(): partial = lax.cond(general, lambda: full_products(wire, which), lambda: p...]
  transfers between devices with their start and end apart: 1 -> 1, of which waited for: 0 -> 0; matrix products, arithmetic and copies ran while one was open for 1% -> 1% of each run, Pallas kernels for 13% -> 16%
where the time goes in v5:
time: 105 us
  blocking collectives  74.1 us (71%)
  Pallas kernels  25.7 us (24%)
  between operations  2.08 us (2%)
  starting transfers between devices  1.91 us (2%)
    all_to_all x1, blocking collectives, reduced(): lax.all_to_all(partial, 'panel', split_axis=0, concat_axis=0, tiled=True)  45.2 us
    all_to_all x1, blocking collectives, both_cores(): mine = lax.all_to_all(sent, CHIPS, split_axis=0, concat_axis=0, tiled=True)  28.9 us
    pallas_call x1, Pallas kernels, body(): pl.pallas_call(tables_kernel, out_shape=[shaped((LIST,), i32), shaped((CO...  11.2 us
    pallas_call x1, Pallas kernels, products(): pl.pallas_call(functools.partial(product_kernel, full), out_shape=pltpu.V...  5.81 us
    pallas_call x1, Pallas kernels, body(): pl.pallas_call(own_product_kernel, out_shape=[shaped((half_rows, 128), f3...  3.12 us
    pallas_call x1, Pallas kernels, weights(): pl.pallas_call(functools.partial(pack_rows_kernel, turn), out_shape=shape...  2.22 us
  transfers between devices with their start and end apart: 1, of which 0 were waited for; matrix products, arithmetic and copies ran while one was open for 1% of the time, Pallas kernels for 16%

profile of v5, /device:TPU:2, one launch (start us, length us, event | category | flops | bytes accessed | tf_op | source)
XLA Modules:
  0.0 104.5 jit_solution(4602097834602286954)
XLA Ops:
  0.0 0.0 copy-start.5
  0.0 0.0 copy-start.6
  0.0 0.0 copy-start.4
  0.0 1.8 %send.1 = bf16[16,136,128]{2,1,0:T(8,128)(2,1)S(1)} custom-call(bf16[50,1024]{1,0:T(8,128)(2,1)} %t_ref.1, s32[16]{0:T(128)} %cd_ref.5, s32[40]{0:T(128)} %occ_ref.3), custom_call_target="tpu_custom_call" | custom-call | tf_op jit(solution)/shard_map/send/pallas_call | solution.py:372
  1.8 0.0 copy-start.3
  1.8 28.9 %all_to_all.45 = bf16[16,136,128]{2,1,0:T(8,128)(2,1)S(1)} all-to-all(bf16[16,136,128]{2,1,0:T(8,128)(2,1)S(1)} %send.1), channel_id=1, replica_groups=mesh['blk_0'=2,'blk_1'=8,'blk_2'=2,'panel'=32] {'blk_0','blk_1'}, dimensions={0} | all-to-all | bytes 1114112 | tf_op jit(solution)/shard_map/all_to_all | solution.py:347
  30.7 1.9 %collective-permute-start.6 = (bf16[2176,128]{1,0:T(8,128)(2,1)S(1)}, bf16[2176,128]{1,0:T(8,128)(2,1)}, u32[]{:S(2)}, u32[]{:S(2)}) collective-permute-start(bf16[2176,128]{1,0:T(8,128)(2,1)S(1)} %bitcast.24), channel_id=1, source_target_pairs={{0,32},{32,0},{1,33},{33,1},{2,34},{34,2},{3,35},{35,3},{4,36},{36... | collective-permute-start | bytes 1671176 | tf_op jit(solution)/shard_map/ppermute | solution.py:349
  32.7 0.0 copy-done.5
  32.7 0.0 copy-done.6
  32.7 11.2 %tables.1 = (s32[2304]{0:T(1024)S(1)}, s32[1664]{0:T(1024)S(1)}, s32[16]{0:T(128)S(1)}) custom-call(s32[16]{0:T(128)S(1)} %copy-done.5, s32[40]{0:T(128)S(1)} %copy-done.6), custom_call_target="tpu_custom_call" | custom-call | tf_op jit(solution)/shard_map/tables/pallas_call | solution.py:383
  43.9 0.7 fusion
  46.6 0.0 copy-done.4
  46.6 2.2 %shard_map.58.weight_ref = bf16[256,512]{1,0:T(8,128)(2,1)} custom-call(bf16[256,1024]{1,0:T(8,128)(2,1)} %v_ref.1, s32[4]{0:T(128)S(1)} %copy-done.4, s32[16]{0:T(128)S(1)} %copy-done.5), custom_call_target="tpu_custom_call" | custom-call | tf_op jit(solution)/shard_map/pallas_call | solution.py:363
  48.8 3.1 %own_product.1 = (f32[2176,128]{1,0:T(8,128)}, f32[2176,128]{1,0:T(8,128)}) custom-call(bf16[2176,128]{1,0:T(8,128)(2,1)S(1)} %bitcast.25, bf16[256,512]{1,0:T(8,128)(2,1)} %shard_map.58.weight_ref), custom_call_target="tpu_custom_call" | custom-call | tf_op jit(solution)/shard_map/own_product/pallas_call | solution.py:397
  52.0 0.0 collective-permute-done.6
  52.0 0.0 copy-done.3
  52.0 52.6 %conditional.4 = (f32[8,1600]{1,0:T(8,128)}) conditional(s32[]{:T(128)} %clamp.3, (pred[]{:T(512)}, f32[2176,128]{1,0:T(8,128)}, f32[2176,128]{1,0:T(8,128)}, bf16[2176,128]{1,0:T(8,128)(2,1)}, bf16[256,512]{1,0:T(8,128)(2,1)}, /*index=5*/s32[4]{0:T(128)S(1)}, s32[2304]{0:T(1024)S(1)}, s32[16]{0:T(128)S(1)}, ...), branch_computations={%region_0.0_spmd, %region_3.0_spmd, %region_6.11_spmd} | conditional | flops 340492 | bytes 18099554 | solution.py:466
  52.0 5.8 %conditional.1 = (f32[32,8,640]{2,1,0:T(8,128)S(1)}) conditional(s32[]{:T(128)} %convert_element_type.25, (f32[2176,128]{1,0:T(8,128)}, f32[2176,128]{1,0:T(8,128)}, bf16[2176,128]{1,0:T(8,128)(2,1)}, bf16[256,512]{1,0:T(8,128)(2,1)}, s32[4]{0:T(128)S(1)}, /*index=5*/s32[2304]{0:T(1024)S(1)}, s32[16]{0:T(128)S(1)}) %tuple.27, ...), branch_computations={%region_4.0_spmd, %region_5.0_spmd} | conditional | bytes 14943724 | solution.py:440
  52.0 5.8 %branch_0_fun.4 = f32[32,8,640]{2,1,0:T(8,128)S(1)} custom-call(s32[1]{0:T(128)} %constant.16.clone.round_ref, f32[2176,128]{1,0:T(8,128)} %get-tuple-element.277.refs_0_, f32[2176,128]{1,0:T(8,128)} %get-tuple-element.278.refs_1_, bf16[2176,128]{1,0:T(8,128)(2,1)} %get-tuple-element.279.refs_2_, bf16[256,512]{1,0:T(8,128)(2,1)} %get-tuple-element.280.refs_3_, ...), custom_call_target="tpu_custom_call" | custom-call | tf_op jit(solution)/shard_map/cond/branch_1_fun/cond/branch_0_fun/pallas_call | solution.py:409
  57.8 45.2 %all_to_all.44 = f16[32,8,640]{2,1,0:T(8,128)(2,1)S(1)} all-to-all(f16[32,8,640]{2,1,0:T(8,128)(2,1)S(1)} %convert_element_type.26), channel_id=1, replica_groups=mesh['blk_0'=2,'blk_1'=8,'blk_2'=2,'panel'=32] {'panel'}, dimensions={0} | all-to-all | bytes 655360 | tf_op jit(solution)/shard_map/cond/branch_1_fun/all_to_all | solution.py:445
  103.1 1.5 %finish.4 = f32[8,1600]{1,0:T(8,128)} custom-call(s32[1]{0:T(128)} %constant.18.clone.round_ref, f32[32,8,640]{2,1,0:T(8,128)S(1)} %convert_element_type.27.got_ref, s32[4]{0:T(128)S(1)} %get-tuple-element.296.ab_ref, s32[16]{0:T(128)S(1)} %get-tuple-element.298.kept_ref, s32[1,1664]{1,0:T(1,128)S(1)} %get-tuple-element.303.code_ref), custom_call_target="tpu_custom_call" | custom-call | tf_op jit(solution)/shard_map/cond/branch_1_fun/finish/pallas_call | solution.py:446
  (3 shorter events, 0.1 us)
Async XLA Ops:
  0.0 32.7 %copy-start.5 = (s32[16]{0:T(128)S(1)}, s32[16]{0:T(128)}, u32[]{:S(2)}) copy-start(s32[16]{0:T(128)} %cd_ref.5) | copy-start | bytes 196
  0.0 32.7 %copy-start.6 = (s32[40]{0:T(128)S(1)}, s32[40]{0:T(128)}, u32[]{:S(2)}) copy-start(s32[40]{0:T(128)} %occ_ref.3) | copy-start | bytes 484
  0.0 46.6 %copy-start.4 = (s32[4]{0:T(128)S(1)}, s32[4]{0:T(128)}, u32[]{:S(2)}) copy-start(s32[4]{0:T(128)} %ab_ref.1) | copy-start | bytes 52
  1.8 50.2 %copy-start.3 = (bf16[50,1024]{1,0:T(8,128)(2,1)S(1)}, bf16[50,1024]{1,0:T(8,128)(2,1)}, u32[]{:S(2)}) copy-start(bf16[50,1024]{1,0:T(8,128)(2,1)} %t_ref.1) | copy-start | bytes 307204
  30.7 21.2 %collective-permute-start.6 = (bf16[2176,128]{1,0:T(8,128)(2,1)S(1)}, bf16[2176,128]{1,0:T(8,128)(2,1)}, u32[]{:S(2)}, u32[]{:S(2)}) collective-permute-start(bf16[2176,128]{1,0:T(8,128)(2,1)S(1)} %bitcast.24), channel_id=1, source_target_pairs={{0,32},{32,0},{1,33},{33,1},{2,34},{34,2},{3,35},{35,3},{4,36},{36... | collective-permute-start | bytes 1671176 | tf_op jit(solution)/shard_map/ppermute | solution.py:349

commit v6 on v4

--- a/solution.py
+++ b/solution.py
@@ -22,12 +22,12 @@
 WIDE = 8
 NARROW = 2
 PARTS = WIDE // NARROW
-ROWS = 136
+ROWS = 144
 FULL = 56
-WIRES = (512, 640)
+WIRES = (512, 640, 896)
 CODES = 1664
 NOWHERE = 1 << 24
-LIST = 2304
+LIST = 2560
 KEPT = 16
 
 SMEM = pl.BlockSpec(memory_space=pltpu.SMEM)
@@ -372,7 +372,7 @@
         rows = 2 * SOURCES * (FULL if full else ROWS)
         return pl.pallas_call(
             functools.partial(product_kernel, full),
-            out_shape=shaped((32, 8, wire), f32),
+            out_shape=pltpu.VMEM((32, 8, wire), f32),
             in_specs=[SMEM] + [VMEM] * len(operands) + [SMEM] * 3,
             out_specs=VMEM,
             scratch_shapes=[

time: 103 us -> 104 us (level)
  local copies, waits for them, and re-layouts: 0.65 us -> 2.35 us
  other arithmetic: 1.17 us -> 0.08 us
    cond x0 -> x6, local copies, waits for them, and re-layouts: none -> 1.13 us
    convert_element_type x1, other arithmetic: 1.13 us -> 0.04 us  [reduced(): partial = lax.cond(general, lambda: full_products(wire, which), lambda: p...]
where the time goes in v6:
time: 104 us
  blocking collectives  74.4 us (72%)
  Pallas kernels  22 us (21%)
  between operations  2.62 us (3%)
  local copies, waits for them, and re-layouts  2.35 us (2%)
  starting transfers between devices  2.04 us (2%)
    all_to_all x1, blocking collectives, reduced(): lax.all_to_all(partial, 'panel', split_axis=0, concat_axis=0, tiled=True)  45.2 us
    all_to_all x1, blocking collectives, both_cores(): mine = lax.all_to_all(sent, CHIPS, split_axis=0, concat_axis=0, tiled=True)  29.3 us
    pallas_call x1, Pallas kernels, body(): pl.pallas_call(tables_kernel, out_shape=[shaped((LIST,), i32), shaped((CO...  11.5 us
    pallas_call x1, Pallas kernels, products(): pl.pallas_call(functools.partial(product_kernel, full), out_shape=pltpu.V...  5.71 us
  transfers between devices with their start and end apart: 1, of which 0 were waited for; matrix products, arithmetic and copies ran while one was open for 1% of the time, Pallas kernels for 13%

profile of v6, /device:TPU:2, one launch (start us, length us, event | category | flops | bytes accessed | tf_op | source)
XLA Modules:
  0.0 103.6 jit_solution(9192869392648335518)
XLA Ops:
  0.0 1.8 %send.1 = bf16[16,144,128]{2,1,0:T(8,128)(2,1)S(1)} custom-call(bf16[50,1024]{1,0:T(8,128)(2,1)} %t_ref.1, s32[16]{0:T(128)} %cd_ref.5, s32[40]{0:T(128)} %occ_ref.3), custom_call_target="tpu_custom_call" | custom-call | tf_op jit(solution)/shard_map/send/pallas_call | solution.py:347
  1.8 29.3 %all_to_all.58 = bf16[16,144,128]{2,1,0:T(8,128)(2,1)} all-to-all(bf16[16,144,128]{2,1,0:T(8,128)(2,1)S(1)} %send.1), channel_id=1, replica_groups=mesh['blk_0'=2,'blk_1'=8,'blk_2'=2,'panel'=32] {'blk_0','blk_1'}, dimensions={0} | all-to-all | bytes 1179648 | tf_op jit(solution)/shard_map/all_to_all | solution.py:322
  31.0 2.0 %collective-permute-start.8 = (bf16[2304,128]{1,0:T(8,128)(2,1)}, bf16[2304,128]{1,0:T(8,128)(2,1)}, u32[]{:S(2)}, u32[]{:S(2)}) collective-permute-start(bf16[2304,128]{1,0:T(8,128)(2,1)} %bitcast.11), channel_id=1, source_target_pairs={{0,32},{32,0},{1,33},{33,1},{2,34},{34,2},{3,35},{35,3},{4,36},{36... | collective-permute-start | bytes 1769480 | tf_op jit(solution)/shard_map/ppermute | solution.py:324
  33.1 0.0 copy-done.34
  33.1 0.0 copy-done.45
  33.1 11.5 %tables.1 = (s32[2560]{0:T(1024)S(1)}, s32[1664]{0:T(1024)S(1)}, s32[16]{0:T(128)S(1)}) custom-call(s32[16]{0:T(128)S(1)} %copy-done.34, s32[40]{0:T(128)S(1)} %copy-done.45), custom_call_target="tpu_custom_call" | custom-call | tf_op jit(solution)/shard_map/tables/pallas_call | solution.py:358
  44.6 0.6 reshape.33
  45.2 0.6 fusion
  47.7 0.0 copy-start.13
  48.3 0.0 copy-done.13
  48.3 0.0 copy-start.10
  48.3 1.5 %shard_map.59 = bf16[256,512]{1,0:T(8,128)(2,1)S(1)} custom-call(bf16[256,1024]{1,0:T(8,128)(2,1)} %v_ref.1, s32[4]{0:T(128)S(1)} %copy-done.13, s32[16]{0:T(128)S(1)} %copy-done.34), custom_call_target="tpu_custom_call" | custom-call | tf_op jit(solution)/shard_map/pallas_call | solution.py:338
  49.9 0.0 collective-permute-done.8
  49.9 0.0 copy-done.10
  49.9 53.6 %conditional.5 = (f32[8,1600]{1,0:T(8,128)}) conditional(s32[]{:T(128)} %clamp.3, (pred[]{:T(512)}, bf16[2304,128]{1,0:T(8,128)(2,1)}, bf16[2304,128]{1,0:T(8,128)(2,1)}, bf16[256,512]{1,0:T(8,128)(2,1)S(1)}, s32[4]{0:T(128)S(1)}, /*index=5*/s32[2560]{0:T(1024)S(1)}, s32[16]{0:T(128)S(1)}, ...), branch_computations={%region_0.0_spmd, %region_3.0_spmd, %region_6.0_spmd, %region_9.14... | conditional | flops 471564 | bytes 27466678 | solution.py:429
  49.9 0.0 copy-start.18
  50.0 0.5 copy-done.18
  50.4 5.7 %conditional.1 = (f32[32,8,640]{2,1,0:T(8,128)S(1)}) conditional(s32[]{:T(128)} %convert_element_type.33, (bf16[2304,128]{1,0:T(8,128)(2,1)}, bf16[2304,128]{1,0:T(8,128)(2,1)}, bf16[256,512]{1,0:T(8,128)(2,1)S(1)}, s32[4]{0:T(128)S(1)}, s32[2560]{0:T(1024)S(1)}, /*index=5*/s32[16]{0:T(128)S(1)}) %tuple.33, (bf16[50,1024]{1,0:T(8,128)(2,1)S(1)}, ...), branch_computations={%region_4.0_spmd, %region_5.0_spmd} | conditional | bytes 17041684 | solution.py:403
  50.4 5.7 %branch_0_fun.5 = f32[32,8,640]{2,1,0:T(8,128)S(1)} custom-call(s32[1]{0:T(128)} %constant.14.clone.round_ref, bf16[2304,128]{1,0:T(8,128)(2,1)} %get-tuple-element.313.refs_0_, bf16[2304,128]{1,0:T(8,128)(2,1)} %get-tuple-element.314.refs_1_, bf16[256,512]{1,0:T(8,128)(2,1)S(1)} %get-tuple-element.315.refs_2_, s32[4]{0:T(128)S(1)} %get-tuple-element.316.refs_3_, ...), custom_call_target="tpu_custom_call" | custom-call | tf_op jit(solution)/shard_map/cond/branch_1_fun/cond/branch_0_fun/pallas_call | solution.py:373
  56.2 45.2 %all_to_all.56 = f16[32,8,640]{2,1,0:T(8,128)(2,1)S(1)} all-to-all(f16[32,8,640]{2,1,0:T(8,128)(2,1)S(1)} %convert_element_type.34), channel_id=1, replica_groups=mesh['blk_0'=2,'blk_1'=8,'blk_2'=2,'panel'=32] {'panel'}, dimensions={0} | all-to-all | bytes 655360 | tf_op jit(solution)/shard_map/cond/branch_1_fun/all_to_all | solution.py:408
  101.4 0.0 copy-start.19
  101.5 0.6 copy-done.31
  102.1 0.0 copy-done.19
  102.1 1.5 %finish.5 = f32[8,1600]{1,0:T(8,128)} custom-call(s32[1]{0:T(128)} %constant.18.clone.round_ref, f32[32,8,640]{2,1,0:T(8,128)S(1)} %convert_element_type.35.got_ref, s32[4]{0:T(128)S(1)} %copy-done.19, s32[16]{0:T(128)S(1)} %get-tuple-element.332.kept_ref, s32[1,1664]{1,0:T(1,128)S(1)} %copy-done.31), custom_call_target="tpu_custom_call" | custom-call | tf_op jit(solution)/shard_map/cond/branch_1_fun/finish/pallas_call | solution.py:409
  (5 shorter events, 0.1 us)
Async XLA Ops:
  31.0 2.1 %copy-start.34 = (s32[16]{0:T(128)S(1)}, s32[16]{0:T(128)}, u32[]{:S(2)}) copy-start(s32[16]{0:T(128)} %cd_ref.5) | copy-start | bytes 196
  31.0 2.1 %copy-start.45 = (s32[40]{0:T(128)S(1)}, s32[40]{0:T(128)}, u32[]{:S(2)}) copy-start(s32[40]{0:T(128)} %occ_ref.3) | copy-start | bytes 484
  31.0 18.9 %collective-permute-start.8 = (bf16[2304,128]{1,0:T(8,128)(2,1)}, bf16[2304,128]{1,0:T(8,128)(2,1)}, u32[]{:S(2)}, u32[]{:S(2)}) collective-permute-start(bf16[2304,128]{1,0:T(8,128)(2,1)} %bitcast.11), channel_id=1, source_target_pairs={{0,32},{32,0},{1,33},{33,1},{2,34},{34,2},{3,35},{35,3},{4,36},{36... | collective-permute-start | bytes 1769480 | tf_op jit(solution)/shard_map/ppermute | solution.py:324
  47.7 0.7 copy-start.13
  48.3 1.6 %copy-start.10 = (bf16[50,1024]{1,0:T(8,128)(2,1)S(1)}, bf16[50,1024]{1,0:T(8,128)(2,1)}, u32[]{:S(2)}) copy-start(bf16[50,1024]{1,0:T(8,128)(2,1)} %t_ref.1) | copy-start | bytes 307204
  49.9 0.5 copy-start.18
  101.4 0.7 copy-start.31
  101.4 0.6 copy-start.19

commit v7 on v6

v7 whole, which is shorter than its diff:
```python
import functools

import jax
import jax.numpy as jnp
from jax import lax
from jax.experimental import pallas as pl
from jax.experimental.pallas import tpu as pltpu
from jax.sharding import Mesh
from jax.sharding import PartitionSpec as P


TW = 64
IRREPS = 8
OCC = 40
IJ = 1600
BLK = ("blk_0", "blk_1", "blk_2")
BLK_PANEL = ("blk_0", "blk_1", "blk_2", "panel")
CHIPS = ("blk_0", "blk_1")

PAIRS = 50
SOURCES = 16
WIDE = 8
NARROW = 2
PARTS = WIDE // NARROW
ROWS = 144
FULL = 56
WIRES = (256, 384, 512)
LIST = 1408
KEPT = 16

SMEM = pl.BlockSpec(memory_space=pltpu.SMEM)
VMEM = pl.BlockSpec(memory_space=pltpu.VMEM)
NT = (((1,), (1,)), ((), ()))
GRANT = pltpu.CompilerParams(vmem_limit_bytes=24 << 20)
LARGE = pltpu.CompilerParams(vmem_limit_bytes=40 << 20)


def places(cd_ref):
    irreps = [cd_ref[t] for t in range(16)]
    ranks = []
    for t in range(16):
        rank = jnp.int32(0)
        for earlier in range(t):
            rank += jnp.where(irreps[earlier] == irreps[t], 1, 0)
        ranks.append(rank)
    return irreps, ranks


def fill_chooser(choose, ranks, turn):
    width = WIDE * TW
    row = lax.broadcasted_iota(jnp.int32, (TW, width), 0)
    col = lax.broadcasted_iota(jnp.int32, (TW, width), 1)
    place = jnp.where(col % TW == row, col // TW + turn * WIDE, -1)
    for t in range(16):
        hit = jnp.where(place == ranks[t], 1.0, 0.0)
        choose[t * TW : (t + 1) * TW, :] = hit.astype(jnp.bfloat16)


def column_irreps(irreps):
    lane = lax.broadcasted_iota(jnp.int32, (1, 16 * TW), 1) // TW
    found = jnp.zeros((1, 16 * TW), jnp.int32)
    for t in range(16):
        found = jnp.where(lane == t, irreps[t], found)
    return found


def pack(values, row_irrep, col_irrep, choose):
    kept = jnp.where(row_irrep == col_irrep, values.astype(jnp.float32), 0.0)
    return jnp.dot(
        kept.astype(jnp.bfloat16), choose[...], preferred_element_type=jnp.float32
    ).astype(jnp.bfloat16)


def my_pairs(occ_ref):
    blk = lax.axis_index("blk_0") * 16 + lax.axis_index("blk_1") * 2 + lax.axis_index("blk_2")
    upper = blk * 5 // 4
    at = blk % 4 * 10
    left = [occ_ref[upper], occ_ref[jnp.minimum(upper + 1, OCC - 1)]]
    row = lax.broadcasted_iota(jnp.int32, (PAIRS, 1), 0)
    column = jnp.zeros((PAIRS, 1), jnp.int32)
    irreps = []
    for m in range(PAIRS):
        later = at + m >= OCC
        right = occ_ref[at + m - jnp.where(later, OCC, 0)]
        irreps.append(jnp.bitwise_xor(jnp.where(later, left[1], left[0]), right))
        column = jnp.where(row == m, irreps[m], column)
    return irreps, column


def count_rows(irreps, need):
    for g in range(IRREPS):
        tiles = jnp.int32(0)
        for irrep in irreps:
            tiles += jnp.where(irrep == g, 1, 0)
        need[g] = (tiles + NARROW - 1) // NARROW


def send_kernel(t_ref, cd_ref, occ_ref, out_ref, choose, need):
    irreps, ranks = places(cd_ref)
    fill_chooser(choose, ranks, 0)
    count_rows(irreps, need)
    pairs, row_irrep = my_pairs(occ_ref)
    packed = pack(t_ref[...], row_irrep, column_irreps(irreps), choose)
    lane = lax.broadcasted_iota(jnp.int32, (1, PAIRS), 1)
    first = jnp.zeros((1, PAIRS), jnp.int32)
    count = jnp.zeros((1, PAIRS), jnp.int32)
    row = jnp.int32(0)
    for m in range(PAIRS):
        rows = need[pairs[m]]
        first = jnp.where(lane == m, row, first)
        count = jnp.where(lane == m, rows, count)
        row += rows
    place = lax.broadcasted_iota(jnp.int32, (ROWS, PAIRS), 0)
    width = NARROW * TW
    spread = None
    for part in range(PARTS):
        at = jnp.where(count > part, first + part, -1)
        move = jnp.where(place == at, 1.0, 0.0).astype(jnp.bfloat16)
        moved = jnp.dot(
            move, packed[:, part * width : (part + 1) * width], preferred_element_type=jnp.float32
        )
        spread = moved if spread is None else spread + moved
    spread = spread.astype(jnp.bfloat16)
    for s in range(SOURCES):
        out_ref[s] = spread


def send_full_kernel(turn, t_ref, cd_ref, occ_ref, out_ref, choose):
    irreps, ranks = places(cd_ref)
    fill_chooser(choose, ranks, turn)
    _, row_irrep = my_pairs(occ_ref)
    packed = pack(t_ref[...], row_irrep, column_irreps(irreps), choose)
    for s in range(SOURCES):
        out_ref[s, :PAIRS, :] = packed
        out_ref[s, PAIRS:, :] = jnp.zeros((FULL - PAIRS, WIDE * TW), jnp.bfloat16)


def pack_rows_kernel(turn, v_ref, ab_ref, cd_ref, out_ref, choose):
    irreps, ranks = places(cd_ref)
    fill_chooser(choose, ranks, turn)
    row = lax.broadcasted_iota(jnp.int32, (4 * TW, 1), 0) // TW
    row_irrep = jnp.zeros((4 * TW, 1), jnp.int32)
    for i in range(4):
        row_irrep = jnp.where(row == i, ab_ref[i], row_irrep)
    out_ref[...] = pack(v_ref[...], row_irrep, column_irreps(irreps), choose)


def list_kernel(cd_ref, occ_ref, counts_ref, list_ref, kept_ref, count, need):
    core = lax.axis_index("blk_2")
    irreps, _ = places(cd_ref)
    count_rows(irreps, need)
    start = jnp.int32(0)
    for g in range(IRREPS):
        kept_ref[g] = start
        count[g] = start
        start += counts_ref[core * IRREPS + g]
    for k in range(IRREPS, KEPT):
        kept_ref[k] = start

    for mine in range(2):

        @pl.when(core == mine)
        def _():
            @pl.loop(0, 8)
            def _(part):
                for chip in range(2):
                    row = (part * 2 + chip) * ROWS
                    last = row + ROWS - 1
                    for m in range(PAIRS):
                        i, j = divmod((chip * 2 + mine) * PAIRS + m, OCC)
                        if m == 0 or j == 0:
                            left = occ_ref[part * 5 + i]
                        irrep = jnp.bitwise_xor(left, occ_ref[j])
                        at = count[irrep]
                        count[irrep] = at + 1
                        list_ref[at] = jnp.minimum(row, last)
                        row += need[irrep]

    @pl.loop(0, (LIST - IJ // 2) // 16)
    def _(k):
        for u in range(16):
            list_ref[IJ // 2 + k * 16 + u] = 0


def full_list_kernel(occ_ref, kept_ref, list_ref, count):
    core = lax.axis_index("blk_2")
    for g in range(IRREPS):
        count[g] = kept_ref[g]

    @pl.loop(0, OCC)
    def _(i):
        left = occ_ref[i]

        @pl.loop(0, OCC)
        def _(j):
            pair = i * OCC + j
            source = pair // PAIRS

            @pl.when((source & 1) == core)
            def _():
                irrep = jnp.bitwise_xor(left, occ_ref[j])
                at = count[irrep]
                count[irrep] = at + 1
                list_ref[at] = (source >> 1) * FULL + pair - source * PAIRS

    @pl.loop(IJ // 2, LIST)
    def _(k):
        list_ref[k] = 0


def times(held, weight):
    return lax.dot_general(held, weight, NT, preferred_element_type=jnp.float32)


def joined_rows(held_ref):
    held = held_ref[...].astype(jnp.float32)
    count = held.shape[0]
    rows = [held] + [pltpu.roll(held, count - part, 0) for part in range(1, PARTS)]
    return jnp.concatenate([r.astype(jnp.bfloat16) for r in rows], axis=1)


def product_kernel(full, round_ref, *refs):
    turns = 2 if full else 1
    held, weights, refs = refs[:turns], refs[turns : 3 * turns], refs[3 * turns :]
    *ab_refs, list_ref, kept_ref, out_ref = refs[:5]
    *products, dense, both = refs[5:]
    wire = dense.shape[0]
    cols = wire - 1
    rows = [ref[...] for ref in held] if full else [joined_rows(held[0])]
    for core in range(2):
        total = None
        for turn in range(turns):
            part = times(rows[turn], weights[2 * turn + core][...])
            total = part if total is None else total + part
        for q in range(2):
            products[2 * core + q][...] = total[:, q * 128 : (q + 1) * 128]
    lower = lax.broadcasted_iota(jnp.int32, (1, 128), 1) < TW
    skip = round_ref[0] * cols
    for q in range(4):
        product = products[q]
        dense[...] = jnp.zeros_like(dense)
        irreps = [ab_refs[q // 2][2 * (q % 2) + i] for i in range(2)]
        starts = [jnp.minimum(kept_ref[g] + skip, IJ // 2) for g in irreps]
        counts = [kept_ref[g + 1] - kept_ref[g] - skip for g in irreps]
        most = jnp.clip(jnp.maximum(counts[0], counts[1]), 0, cols)

        @pl.loop(0, (most + 7) // 8)
        def _(block):
            base = block * 8
            for u in range(8):
                at = [list_ref[start + base + u] for start in starts]
                picked = [product[pl.ds(a, 1), :] for a in at]
                dense[pl.ds(base + u, 1), :] = jnp.where(lower, picked[0], picked[1])

        both[q * 128 : (q + 1) * 128, :] = dense[...].T
    largest = jnp.max(jnp.max(jnp.abs(both[...]), axis=1, keepdims=True), axis=0, keepdims=True)
    power = 14.0 - jnp.floor(jnp.log2(jnp.maximum(largest, 1e-30)))
    lane = lax.broadcasted_iota(jnp.int32, (4 * TW, wire), 1)
    for core in range(2):
        scaled = both[core * 4 * TW : (core + 1) * 4 * TW, :] * jnp.exp2(power)
        sent = jnp.where(lane == cols, power, scaled).reshape(32, 8, wire)
        out_ref[:, core * 8 : (core + 1) * 8, :] = sent


def sum_kernel(got_ref, mine_ref, partner_ref):
    cols = got_ref.shape[2] - 1
    total = None
    for s in range(32):
        got = got_ref[s]
        got = got * jnp.exp2(-got[:, cols:])
        total = got if total is None else total + got
    mine_ref[...] = total[:8]
    partner_ref[...] = total[8:]


def finish_kernel(round_ref, mine_ref, partner_ref, ab_ref, pairs_ref, out_ref):
    core = lax.axis_index("blk_2")
    irrep = ab_ref[lax.axis_index("panel") // 8]
    wire = mine_ref.shape[1]
    cols = wire - 1
    pairs = pairs_ref[...]
    hits = [pairs == irrep + core * IRREPS, pairs == irrep + (1 - core) * IRREPS]
    count = jnp.where(hits[0], 1, jnp.where(hits[1], 1 << 16, 0))
    row = lax.broadcasted_iota(jnp.int32, pairs.shape, 0)
    lane = lax.broadcasted_iota(jnp.int32, pairs.shape, 1)
    for step in (1, 2, 4, 8, 16, 32, 64):
        count += jnp.where(lane >= step, pltpu.roll(count, step, 1), 0)
    whole = jnp.broadcast_to(count[:, 127:], pairs.shape)
    above = whole
    for step in (1, 2, 4, 8):
        above += jnp.where(row >= step, pltpu.roll(above, step, 0), 0)
    count += above - whole
    skip = round_ref[0] * cols + 1
    places_of = []
    for hit, found in zip(hits, (count & 0xFFFF, count >> 16)):
        place = jnp.where(hit, found - skip, -1)
        places_of.append(jnp.where(place < cols, place, -1))
    sources = [mine_ref[...], partner_ref[...]]
    for block in range(13):
        spread = jnp.zeros((8, 128), jnp.float32)
        for place, source in zip(places_of, sources):
            at = jnp.broadcast_to(place[block : block + 1, :], (8, 128))
            for k in range(wire // 128):
                moved = jnp.take_along_axis(source[:, k * 128 : (k + 1) * 128], at & 127, axis=1)
                spread = jnp.where(at >> 7 == k, moved, spread)
        held = min(128, IJ - block * 128)
        out_ref[:, block * 128 : block * 128 + held] = spread[:, :held]


def shaped(shape, dtype):
    return jax.ShapeDtypeStruct(shape, dtype)


def body(integrals, amplitudes, ab_irrep, cd_irrep, occ_irrep):
    bf16, f32, i32 = jnp.bfloat16, jnp.float32, jnp.int32
    width = WIDE * TW
    chooser = pltpu.VMEM((16 * TW, width), bf16)
    numbers = pltpu.SMEM((IRREPS,), i32)

    def over_chips(sent):
        got = lax.all_to_all(sent, CHIPS, split_axis=0, concat_axis=0, tiled=True)
        return got.reshape(sent.shape[0] * sent.shape[1], sent.shape[2])

    def swapped(array):
        return lax.ppermute(array, "blk_2", [(0, 1), (1, 0)])

    def gathered_full(turn):
        sent = pl.pallas_call(
            functools.partial(send_full_kernel, turn),
            out_shape=shaped((SOURCES, FULL, width), bf16),
            in_specs=[VMEM, SMEM, SMEM],
            out_specs=VMEM,
            scratch_shapes=[chooser],
            compiler_params=GRANT,
        )(amplitudes, cd_irrep, occ_irrep)
        return over_chips(sent)

    def weights(turn):
        mine = pl.pallas_call(
            functools.partial(pack_rows_kernel, turn),
            out_shape=shaped((4 * TW, width), bf16),
            in_specs=[VMEM, SMEM, SMEM],
            out_specs=VMEM,
            scratch_shapes=[chooser],
            compiler_params=GRANT,
        )(integrals, ab_irrep, cd_irrep)
        return [mine, swapped(mine)]

    sent = pl.pallas_call(
        send_kernel,
        out_shape=shaped((SOURCES, ROWS, NARROW * TW), bf16),
        in_specs=[VMEM, SMEM, SMEM],
        out_specs=VMEM,
        scratch_shapes=[chooser, numbers],
        compiler_params=GRANT,
        name="send",
    )(amplitudes, cd_irrep, occ_irrep)
    held = over_chips(sent)

    irrep = jnp.bitwise_xor(occ_irrep[:, None], occ_irrep[None, :]).reshape(32, PAIRS)
    kinds = irrep + jnp.arange(32, dtype=i32)[:, None] % 2 * IRREPS
    numbered = jnp.arange(2 * IRREPS, dtype=i32)
    counts = jnp.sum((kinds == numbered[:, None, None]).astype(i32), axis=(1, 2))
    tiles = jnp.sum((cd_irrep == numbered[:IRREPS, None]).astype(i32), axis=1)
    need = (tiles + NARROW - 1) // NARROW
    alike = irrep == numbered[:IRREPS, None, None]
    rows = jnp.sum(jnp.where(alike, need[:, None, None], 0), axis=(0, 2))
    general = jnp.logical_or(jnp.max(rows) > ROWS, jnp.max(tiles) > WIDE)
    most = jnp.max(counts)
    pairs = jnp.pad(kinds.reshape(IJ), (0, 2048 - IJ), constant_values=2 * IRREPS)
    pairs = pairs.reshape(16, 128)

    first_weights = weights(0)
    irreps = [ab_irrep, swapped(ab_irrep)]

    pair_list, kept = pl.pallas_call(
        list_kernel,
        out_shape=[shaped((LIST,), i32), shaped((KEPT,), i32)],
        in_specs=[SMEM] * 3,
        out_specs=[SMEM] * 2,
        scratch_shapes=[numbers] * 2,
        compiler_params=GRANT,
        name="list",
    )(cd_irrep, occ_irrep, counts)

    def products(full, wire, which, operands, rows_list):
        rows = SOURCES * (FULL if full else ROWS)
        return pl.pallas_call(
            functools.partial(product_kernel, full),
            out_shape=pltpu.VMEM((32, 16, wire), f32),
            in_specs=[SMEM] + [VMEM] * len(operands) + [SMEM] * 4,
            out_specs=VMEM,
            scratch_shapes=[pltpu.VMEM((rows, 128), f32)] * 4
            + [pltpu.VMEM((wire, 128), f32), pltpu.VMEM((8 * TW, wire), f32)],
            compiler_params=LARGE,
        )(which, *operands, *irreps, rows_list, kept)

    def full_products(wire, which):
        rows_list = pl.pallas_call(
            full_list_kernel,
            out_shape=shaped((LIST,), i32),
            in_specs=[SMEM] * 2,
            out_specs=SMEM,
            scratch_shapes=[numbers],
            compiler_params=GRANT,
            name="full_list",
        )(occ_irrep, kept)
        operands = [gathered_full(0), gathered_full(1), *first_weights, *weights(1)]
        return products(True, wire, which, operands, rows_list)

    def reduced(wire, which):
        partial = lax.cond(
            general,
            lambda: full_products(wire, which),
            lambda: products(False, wire, which, [held, *first_weights], pair_list),
        ).astype(jnp.float16)
        arrived = lax.all_to_all(partial, "panel", split_axis=0, concat_axis=0, tiled=True)
        mine, partners = pl.pallas_call(
            sum_kernel,
            out_shape=[shaped((8, wire), f32)] * 2,
            in_specs=[VMEM],
            out_specs=[VMEM] * 2,
            compiler_params=GRANT,
            name="sum",
        )(arrived.astype(f32))
        return pl.pallas_call(
            finish_kernel,
            out_shape=shaped((8, IJ), f32),
            in_specs=[SMEM, VMEM, VMEM, SMEM, VMEM],
            out_specs=VMEM,
            compiler_params=GRANT,
            name="finish",
        )(which, mine, swapped(partners), ab_irrep, pairs)

    zero = jnp.zeros((1,), i32)

    def all_rounds():
        cols = WIRES[-1] - 1

        def add_round(number, total):
            which = jnp.full((1,), number, i32)
            return total + reduced(WIRES[-1], which)

        return lax.fori_loop(0, (most + cols - 1) // cols, add_round, jnp.zeros((8, IJ), f32))

    branches = [functools.partial(reduced, wire, zero) for wire in WIRES]
    chosen = sum((most >= wire).astype(i32) for wire in WIRES)
    return lax.switch(chosen, [*branches, all_rounds])


def solution(mesh):
    split = Mesh(
        mesh.devices.reshape(2, 8, 2, mesh.shape["panel"]), ("blk_0", "blk_1", "blk_2", "panel")
    )
    return jax.shard_map(
        body,
        mesh=split,
        in_specs=(P(BLK, "panel"), P(BLK, "panel"), P(BLK), P("panel"), P()),
        out_specs=P(BLK_PANEL, None),
        check_vma=False,
    )
```

time: 104 us -> 95.8 us (0.921)
  the two profiles are of different devices: /device:TPU:2 before, /device:TPU:1 now
where the time goes in v7:
time: 95.8 us; the launch traced here: 95.4 us
  blocking collectives  35.1 us (37%)
  starting transfers between devices  28.9 us (30%)
  Pallas kernels  18.3 us (19%)
  waiting for transfers between devices  5.68 us (6%)
  between operations  3.33 us (3%)
  other arithmetic  3.02 us (3%)
  local copies, waits for them, and re-layouts  1 us (1%)
    all_to_all x1, blocking collectives, reduced(): lax.all_to_all(partial, 'panel', split_axis=0, concat_axis=0, tiled=True)  35.1 us
    ppermute x3, starting transfers between devices, swapped(): return lax.ppermute(array, 'blk_2', [(0, 1), (1, 0)])  24.6 us
    pallas_call x1, Pallas kernels, products(): pl.pallas_call(functools.partial(product_kernel, full), out_shape=pltpu.V...  5.91 us
    pallas_call x1, Pallas kernels, body(): pl.pallas_call(list_kernel, out_shape=[shaped((LIST,), i32), shaped((KEPT...  5.83 us
    all_to_all x1, waiting for transfers between devices, over_chips(): got = lax.all_to_all(sent, CHIPS, split_axis=0, concat_axis=0, tiled=True)  4.86 us
    all_to_all x1, starting transfers between devices, over_chips(): got = lax.all_to_all(sent, CHIPS, split_axis=0, concat_axis=0, tiled=True)  4.24 us
    pallas_call x1, Pallas kernels, weights(): pl.pallas_call(functools.partial(pack_rows_kernel, turn), out_shape=shape...  2.22 us
    pallas_call x1, Pallas kernels, body(): pl.pallas_call(send_kernel, out_shape=shaped((SOURCES, ROWS, NARROW * TW)...  2.22 us
  transfers between devices with their start and end apart: 4, of which 2 were waited for; matrix products, arithmetic and copies ran while one was open for 3% of the time, Pallas kernels for 8%

profile of v7, /device:TPU:1, one launch (start us, length us, event | category | flops | bytes accessed | tf_op | source)
XLA Modules:
  0.0 95.4 jit_solution(14484228960174023772)
XLA Ops:
  0.0 16.1 %collective-permute-start.9 = (s32[4]{0:T(128)}, s32[4]{0:T(128)S(1)}, u32[]{:S(2)}, u32[]{:S(2)}) collective-permute-start(s32[4]{0:T(128)} %ab_ref.1), channel_id=1, source_target_pairs={{0,32},{32,0},{1,33},{33,1},{2,34},{34,2},{3,35},{35,3},{4,36},{36... | collective-permute-start | bytes 56 | tf_op jit(solution)/shard_map/ppermute | solution.py:325
  16.2 2.2 %shard_map.59 = bf16[256,512]{1,0:T(8,128)(2,1)} custom-call(bf16[256,1024]{1,0:T(8,128)(2,1)} %v_ref.1, s32[4]{0:T(128)} %ab_ref.1, s32[16]{0:T(128)} %cd_ref.5), custom_call_target="tpu_custom_call" | custom-call | tf_op jit(solution)/shard_map/pallas_call | solution.py:339
  18.4 1.9 %collective-permute-start.8 = (bf16[256,512]{1,0:T(8,128)(2,1)}, bf16[256,512]{1,0:T(8,128)(2,1)}, u32[]{:S(2)}, u32[]{:S(2)}) collective-permute-start(bf16[256,512]{1,0:T(8,128)(2,1)} %shard_map.59), channel_id=1, source_target_pairs={{0,32},{32,0},{1,33},{33,1},{2,34},{34,2},{3,35},{35,3},{4,36},{36... | collective-permute-start | bytes 786440 | tf_op jit(solution)/shard_map/ppermute | solution.py:325
  20.3 2.2 %send.1 = bf16[16,144,128]{2,1,0:T(8,128)(2,1)} custom-call(bf16[50,1024]{1,0:T(8,128)(2,1)S(1)} %copy-done.2, s32[16]{0:T(128)S(1)} %copy-done.5, s32[40]{0:T(128)S(1)} %copy-done.4), custom_call_target="tpu_custom_call" | custom-call | tf_op jit(solution)/shard_map/send/pallas_call | solution.py:349
  22.5 4.2 %all-to-all-start.12 = ((bf16[16,144,128]{2,1,0:T(8,128)(2,1)}), bf16[16,144,128]{2,1,0:T(8,128)(2,1)}, u32[]{:S(2)}, u32[]{:S(2)}) async-start(bf16[16,144,128]{2,1,0:T(8,128)(2,1)} %send.1), calls=%async_computation.12 | async-start | bytes 1179648 | tf_op jit(solution)/shard_map/all_to_all | solution.py:321
  27.0 0.2 convert_reduce_fusion.1
  27.1 0.6 fusion.1
  27.9 0.4 convert_reduce_fusion.counts_ref
  28.2 0.1 xor.32
  28.3 5.8 %list.1 = (s32[1408]{0:T(1024)S(1)}, s32[16]{0:T(128)S(1)}) custom-call(s32[16]{0:T(128)S(1)} %copy-done.5, s32[40]{0:T(128)S(1)} %copy-done.4, s32[16]{0:T(128)S(1)} %convert_reduce_fusion.counts_ref), custom_call_target="tpu_custom_call" | custom-call | tf_op jit(solution)/shard_map/list/pallas_call | solution.py:376
  34.2 0.7 reduce_max.27
  34.8 0.2 select_reduce_fusion
  35.0 0.7 reduce_max.28
  35.8 0.1 add.70
  39.1 4.9 %all-to-all-done.12 = bf16[16,144,128]{2,1,0:T(8,128)(2,1)} async-done(((bf16[16,144,128]{2,1,0:T(8,128)(2,1)}), bf16[16,144,128]{2,1,0:T(8,128)(2,1)}, u32[]{:S(2)}, u32[]{:S(2)}) %all-to-all-start.12) | async-done | bytes 589856 | tf_op jit(solution)/shard_map/all_to_all | solution.py:321
  44.0 0.7 copy-done.3
  44.7 50.7 %conditional.5 = (f32[8,1600]{1,0:T(8,128)}) conditional(s32[]{:T(128)} %clamp.3, (pred[]{:T(512)}, bf16[2304,128]{1,0:T(8,128)(2,1)}, bf16[256,512]{1,0:T(8,128)(2,1)}, bf16[256,512]{1,0:T(8,128)(2,1)}, s32[4]{0:T(128)S(1)}, /*index=5*/s32[4]{0:T(128)S(1)}, s32[1408]{0:T(1024)S(1)}, s32[16]{0:T(128)S(1)}, ...), branch_computations={%region_6.9_spmd, %region_9.12_spmd, %region_12.15_spmd, %region_1... | conditional | flops 537100 | bytes 13118488 | solution.py:448
  44.7 5.9 %conditional.1 = (f32[32,16,384]{2,1,0:T(8,128)S(1)}) conditional(s32[]{:T(128)} %convert_element_type.37, (bf16[2304,128]{1,0:T(8,128)(2,1)}, bf16[256,512]{1,0:T(8,128)(2,1)}, bf16[256,512]{1,0:T(8,128)(2,1)}, s32[4]{0:T(128)S(1)}, s32[4]{0:T(128)S(1)}, /*index=5*/s32[1408]{0:T(1024)S(1)}, s32[16]{0:T(128)S(1)}) %tuple.33, ...), branch_computations={%region_10.10_spmd, %region_11.11_spmd} | conditional | bytes 6553712 | solution.py:412
  44.7 5.9 %branch_0_fun.5 = f32[32,16,384]{2,1,0:T(8,128)S(1)} custom-call(s32[1]{0:T(128)} %constant.42.clone.round_ref, bf16[2304,128]{1,0:T(8,128)(2,1)} %get-tuple-element.355.refs_0_, bf16[256,512]{1,0:T(8,128)(2,1)} %get-tuple-element.356.refs_1_, bf16[256,512]{1,0:T(8,128)(2,1)} %get-tuple-element.357.refs_2_, s32[4]{0:T(128)S(1)} %get-tuple-element.358.refs_3_, ...), custom_call_target="tpu_custom_call" | custom-call | tf_op jit(solution)/shard_map/cond/branch_1_fun/cond/branch_0_fun/pallas_call | solution.py:388
  50.6 35.1 %all_to_all.56 = f16[32,16,384]{2,1,0:T(8,128)(2,1)S(1)} all-to-all(f16[32,16,384]{2,1,0:T(8,128)(2,1)S(1)} %convert_element_type.38), channel_id=1, replica_groups=mesh['blk_0'=2,'blk_1'=8,'blk_2'=2,'panel'=32] {'panel'}, dimensions={0} | all-to-all | bytes 786432 | tf_op jit(solution)/shard_map/cond/branch_1_fun/all_to_all | solution.py:417
  85.8 0.1 sum.5
  86.0 6.6 %collective-permute-start.3 = (f32[8,384]{1,0:T(8,128)S(1)}, f32[8,384]{1,0:T(8,128)S(1)}, u32[]{:S(2)}, u32[]{:S(2)}) collective-permute-start(f32[8,384]{1,0:T(8,128)S(1)} %get-tuple-element.384), channel_id=1, source_target_pairs={{0,32},{32,0},{1,33},{33,1},{2,34},{34,2},{3,35},{35,3},{4,36},{36... | collective-permute-start | bytes 36872 | tf_op jit(solution)/shard_map/cond/branch_1_fun/ppermute | solution.py:325
  92.5 0.8 collective-permute-done.3.partner_ref
  93.3 2.0 %finish.5 = f32[8,1600]{1,0:T(8,128)} custom-call(s32[1]{0:T(128)} %constant.44.clone.round_ref, f32[8,384]{1,0:T(8,128)S(1)} %get-tuple-element.383.mine_ref, f32[8,384]{1,0:T(8,128)S(1)} %collective-permute-done.3.partner_ref, s32[4]{0:T(128)S(1)} %get-tuple-element.375.ab_ref, s32[16,128]{1,0:T(8,128)S(1)} %get-tuple-element.385.pairs_ref), custom_call_target="tpu_custom_call" | custom-call | tf_op jit(solution)/shard_map/cond/branch_1_fun/finish/pallas_call | solution.py:426
  (19 shorter events, 0.4 us)
Async XLA Ops:
  0.0 20.3 %copy-start.5 = (s32[16]{0:T(128)S(1)}, s32[16]{0:T(128)}, u32[]{:S(2)}) copy-start(s32[16]{0:T(128)} %cd_ref.5) | copy-start | bytes 196
  0.0 20.3 %copy-start.4 = (s32[40]{0:T(128)S(1)}, s32[40]{0:T(128)}, u32[]{:S(2)}) copy-start(s32[40]{0:T(128)} %occ_ref.3) | copy-start | bytes 484
  0.0 20.3 %copy-start.2 = (bf16[50,1024]{1,0:T(8,128)(2,1)S(1)}, bf16[50,1024]{1,0:T(8,128)(2,1)}, u32[]{:S(2)}) copy-start(bf16[50,1024]{1,0:T(8,128)(2,1)} %t_ref.1) | copy-start | bytes 307204
  0.0 39.1 %collective-permute-start.9 = (s32[4]{0:T(128)}, s32[4]{0:T(128)S(1)}, u32[]{:S(2)}, u32[]{:S(2)}) collective-permute-start(s32[4]{0:T(128)} %ab_ref.1), channel_id=1, source_target_pairs={{0,32},{32,0},{1,33},{33,1},{2,34},{34,2},{3,35},{35,3},{4,36},{36... | collective-permute-start | bytes 56 | tf_op jit(solution)/shard_map/ppermute | solution.py:325
  18.4 20.7 %collective-permute-start.8 = (bf16[256,512]{1,0:T(8,128)(2,1)}, bf16[256,512]{1,0:T(8,128)(2,1)}, u32[]{:S(2)}, u32[]{:S(2)}) collective-permute-start(bf16[256,512]{1,0:T(8,128)(2,1)} %shard_map.59), channel_id=1, source_target_pairs={{0,32},{32,0},{1,33},{33,1},{2,34},{34,2},{3,35},{35,3},{4,36},{36... | collective-permute-start | bytes 786440 | tf_op jit(solution)/shard_map/ppermute | solution.py:325
  22.5 21.4 %all-to-all-start.12 = ((bf16[16,144,128]{2,1,0:T(8,128)(2,1)}), bf16[16,144,128]{2,1,0:T(8,128)(2,1)}, u32[]{:S(2)}, u32[]{:S(2)}) async-start(bf16[16,144,128]{2,1,0:T(8,128)(2,1)} %send.1), calls=%async_computation.12 | async-start | bytes 1179648 | tf_op jit(solution)/shard_map/all_to_all | solution.py:321
  44.0 0.7 copy-start.3
  86.0 7.4 %collective-permute-start.3 = (f32[8,384]{1,0:T(8,128)S(1)}, f32[8,384]{1,0:T(8,128)S(1)}, u32[]{:S(2)}, u32[]{:S(2)}) collective-permute-start(f32[8,384]{1,0:T(8,128)S(1)} %get-tuple-element.384), channel_id=1, source_target_pairs={{0,32},{32,0},{1,33},{33,1},{2,34},{34,2},{3,35},{35,3},{4,36},{36... | collective-permute-start | bytes 36872 | tf_op jit(solution)/shard_map/cond/branch_1_fun/ppermute | solution.py:325

commit v8 on v7

--- a/solution.py
+++ b/solution.py
@@ -2,6 +2,7 @@
 
 import jax
 import jax.numpy as jnp
+import numpy as np
 from jax import lax
 from jax.experimental import pallas as pl
 from jax.experimental.pallas import tpu as pltpu
@@ -24,9 +25,10 @@
 PARTS = WIDE // NARROW
 ROWS = 144
 FULL = 56
-WIRES = (256, 384, 512)
-LIST = 1408
-KEPT = 16
+WIRES = (256, 384)
+LONG = 512
+KEPT = 24
+LIST = KEPT + 1384
 
 SMEM = pl.BlockSpec(memory_space=pltpu.SMEM)
 VMEM = pl.BlockSpec(memory_space=pltpu.VMEM)
@@ -135,27 +137,45 @@
         out_ref[s, PAIRS:, :] = jnp.zeros((FULL - PAIRS, WIDE * TW), jnp.bfloat16)
 
 
-def pack_rows_kernel(turn, v_ref, ab_ref, cd_ref, out_ref, choose):
+def pack_rows_kernel(turn, first, v_ref, ab_ref, cd_ref, out_ref, tiles_ref, choose):
     irreps, ranks = places(cd_ref)
     fill_chooser(choose, ranks, turn)
     row = lax.broadcasted_iota(jnp.int32, (4 * TW, 1), 0) // TW
     row_irrep = jnp.zeros((4 * TW, 1), jnp.int32)
     for i in range(4):
-        row_irrep = jnp.where(row == i, ab_ref[i], row_irrep)
+        row_irrep = jnp.where(row == i, ab_ref[first + i], row_irrep)
+        tiles_ref[i] = ab_ref[first + i]
     out_ref[...] = pack(v_ref[...], row_irrep, column_irreps(irreps), choose)
 
 
-def list_kernel(cd_ref, occ_ref, counts_ref, list_ref, kept_ref, count, need):
+def list_kernel(cd_ref, occ_ref, counts_ref, rows_ref, ab_ref, theirs_ref, list_ref, chosen_ref, count, need):
     core = lax.axis_index("blk_2")
     irreps, _ = places(cd_ref)
     count_rows(irreps, need)
-    start = jnp.int32(0)
+    start = jnp.int32(KEPT)
     for g in range(IRREPS):
-        kept_ref[g] = start
+        list_ref[g] = start
         count[g] = start
         start += counts_ref[core * IRREPS + g]
-    for k in range(IRREPS, KEPT):
-        kept_ref[k] = start
+    for k in range(IRREPS, 16):
+        list_ref[k] = start
+    for k in range(4):
+        list_ref[16 + k] = ab_ref[k]
+        list_ref[20 + k] = theirs_ref[k]
+    tiles, longest, most = jnp.int32(0), jnp.int32(0), jnp.int32(0)
+    for g in range(IRREPS):
+        tiles = jnp.maximum(tiles, need[g])
+    for k in range(32):
+        longest = jnp.maximum(longest, rows_ref[k])
+    for k in range(2 * IRREPS):
+        most = jnp.maximum(most, counts_ref[k])
+    chosen = jnp.int32(0)
+    for wire in WIRES:
+        chosen += jnp.where(most >= wire, 1, 0)
+    chosen_ref[0] = chosen
+    chosen_ref[1] = jnp.where(jnp.logical_or(tiles > PARTS, longest > ROWS), 1, 0)
+    chosen_ref[2] = most
+    chosen_ref[3] = 0
 
     for mine in range(2):
 
@@ -176,16 +196,18 @@
                         list_ref[at] = jnp.minimum(row, last)
                         row += need[irrep]
 
-    @pl.loop(0, (LIST - IJ // 2) // 16)
+    @pl.loop(0, (LIST - KEPT - IJ // 2) // 8)
     def _(k):
-        for u in range(16):
-            list_ref[IJ // 2 + k * 16 + u] = 0
-
-
-def full_list_kernel(occ_ref, kept_ref, list_ref, count):
+        for u in range(8):
+            list_ref[KEPT + IJ // 2 + k * 8 + u] = 0
+
+
+def full_list_kernel(occ_ref, starts_ref, list_ref, count):
     core = lax.axis_index("blk_2")
     for g in range(IRREPS):
-        count[g] = kept_ref[g]
+        count[g] = starts_ref[g]
+    for k in range(KEPT):
+        list_ref[k] = starts_ref[k]
 
     @pl.loop(0, OCC)
     def _(i):
@@ -203,7 +225,7 @@
                 count[irrep] = at + 1
                 list_ref[at] = (source >> 1) * FULL + pair - source * PAIRS
 
-    @pl.loop(IJ // 2, LIST)
+    @pl.loop(KEPT + IJ // 2, LIST)
     def _(k):
         list_ref[k] = 0
 
@@ -222,8 +244,7 @@
 def product_kernel(full, round_ref, *refs):
     turns = 2 if full else 1
     held, weights, refs = refs[:turns], refs[turns : 3 * turns], refs[3 * turns :]
-    *ab_refs, list_ref, kept_ref, out_ref = refs[:5]
-    *products, dense, both = refs[5:]
+    list_ref, out_ref, *products, dense, both = refs
     wire = dense.shape[0]
     cols = wire - 1
     rows = [ref[...] for ref in held] if full else [joined_rows(held[0])]
@@ -239,9 +260,9 @@
     for q in range(4):
         product = products[q]
         dense[...] = jnp.zeros_like(dense)
-        irreps = [ab_refs[q // 2][2 * (q % 2) + i] for i in range(2)]
-        starts = [jnp.minimum(kept_ref[g] + skip, IJ // 2) for g in irreps]
-        counts = [kept_ref[g + 1] - kept_ref[g] - skip for g in irreps]
+        irreps = [list_ref[16 + 2 * q + i] for i in range(2)]
+        starts = [jnp.minimum(list_ref[g] + skip, KEPT + IJ // 2) for g in irreps]
+        counts = [list_ref[g + 1] - list_ref[g] - skip for g in irreps]
         most = jnp.clip(jnp.maximum(counts[0], counts[1]), 0, cols)
 
         @pl.loop(0, (most + 7) // 8)
@@ -273,11 +294,9 @@
     partner_ref[...] = total[8:]
 
 
-def finish_kernel(round_ref, mine_ref, partner_ref, ab_ref, pairs_ref, out_ref):
+def places_kernel(cols, round_ref, list_ref, pairs_ref, *place_refs):
     core = lax.axis_index("blk_2")
-    irrep = ab_ref[lax.axis_index("panel") // 8]
-    wire = mine_ref.shape[1]
-    cols = wire - 1
+    irrep = list_ref[16 + lax.axis_index("panel") // 8]
     pairs = pairs_ref[...]
     hits = [pairs == irrep + core * IRREPS, pairs == irrep + (1 - core) * IRREPS]
     count = jnp.where(hits[0], 1, jnp.where(hits[1], 1 << 16, 0))
@@ -291,15 +310,18 @@
         above += jnp.where(row >= step, pltpu.roll(above, step, 0), 0)
     count += above - whole
     skip = round_ref[0] * cols + 1
-    places_of = []
-    for hit, found in zip(hits, (count & 0xFFFF, count >> 16)):
+    for hit, found, place_ref in zip(hits, (count & 0xFFFF, count >> 16), place_refs):
         place = jnp.where(hit, found - skip, -1)
-        places_of.append(jnp.where(place < cols, place, -1))
+        place_ref[...] = jnp.where(place < cols, place, -1)
+
+
+def finish_kernel(mine_ref, partner_ref, mine_place_ref, partner_place_ref, out_ref):
+    wire = mine_ref.shape[1]
     sources = [mine_ref[...], partner_ref[...]]
     for block in range(13):
         spread = jnp.zeros((8, 128), jnp.float32)
-        for place, source in zip(places_of, sources):
-            at = jnp.broadcast_to(place[block : block + 1, :], (8, 128))
+        for place_ref, source in zip((mine_place_ref, partner_place_ref), sources):
+            at = jnp.broadcast_to(place_ref[block : block + 1, :], (8, 128))
             for k in range(wire // 128):
                 moved = jnp.take_along_axis(source[:, k * 128 : (k + 1) * 128], at & 127, axis=1)
                 spread = jnp.where(at >> 7 == k, moved, spread)
@@ -335,16 +357,16 @@
         )(amplitudes, cd_irrep, occ_irrep)
         return over_chips(sent)
 
-    def weights(turn):
-        mine = pl.pallas_call(
-            functools.partial(pack_rows_kernel, turn),
-            out_shape=shaped((4 * TW, width), bf16),
+    def weights(turn, first, irreps):
+        mine, tiles = pl.pallas_call(
+            functools.partial(pack_rows_kernel, turn, first),
+            out_shape=[shaped((4 * TW, width), bf16), shaped((4,), i32)],
             in_specs=[VMEM, SMEM, SMEM],
-            out_specs=VMEM,
+            out_specs=[VMEM, SMEM],
             scratch_shapes=[chooser],
             compiler_params=GRANT,
-        )(integrals, ab_irrep, cd_irrep)
-        return [mine, swapped(mine)]
+        )(integrals, irreps, cd_irrep)
+        return [mine, swapped(mine)], tiles
 
     sent = pl.pallas_call(
         send_kernel,
@@ -357,43 +379,51 @@
     )(amplitudes, cd_irrep, occ_irrep)
     held = over_chips(sent)
 
-    irrep = jnp.bitwise_xor(occ_irrep[:, None], occ_irrep[None, :]).reshape(32, PAIRS)
-    kinds = irrep + jnp.arange(32, dtype=i32)[:, None] % 2 * IRREPS
-    numbered = jnp.arange(2 * IRREPS, dtype=i32)
-    counts = jnp.sum((kinds == numbered[:, None, None]).astype(i32), axis=(1, 2))
+    number = np.arange(16 * 128, dtype=np.int32).reshape(16, 128)
+    real, source = number < IJ, number // PAIRS
+
+    def orbital_irrep(which):
+        orbital = lax.broadcasted_iota(i32, (OCC, 16, 128), 0)
+        hit = orbital == jnp.asarray(which)[None]
+        return jnp.sum(jnp.where(hit, occ_irrep[:, None, None], 0), axis=0)
+
+    irrep = jnp.bitwise_xor(orbital_irrep(number // OCC), orbital_irrep(number % OCC))
+    kinds = jnp.asarray(np.where(real, source % 2 * IRREPS, 4 * IRREPS), dtype=i32)
+    pairs = irrep + kinds
+    numbered = np.arange(2 * IRREPS, dtype=np.int32)
+    counts = jnp.sum((pairs == numbered[:, None, None]).astype(i32), axis=(1, 2))
     tiles = jnp.sum((cd_irrep == numbered[:IRREPS, None]).astype(i32), axis=1)
     need = (tiles + NARROW - 1) // NARROW
     alike = irrep == numbered[:IRREPS, None, None]
-    rows = jnp.sum(jnp.where(alike, need[:, None, None], 0), axis=(0, 2))
-    general = jnp.logical_or(jnp.max(rows) > ROWS, jnp.max(tiles) > WIDE)
-    most = jnp.max(counts)
-    pairs = jnp.pad(kinds.reshape(IJ), (0, 2048 - IJ), constant_values=2 * IRREPS)
-    pairs = pairs.reshape(16, 128)
-
-    first_weights = weights(0)
-    irreps = [ab_irrep, swapped(ab_irrep)]
-
-    pair_list, kept = pl.pallas_call(
+    taken = jnp.sum(jnp.where(alike, need[:, None, None], 0), axis=0)
+    theirs = jnp.asarray(source)[None] == lax.broadcasted_iota(i32, (32, 16, 128), 0)
+    rows = jnp.sum(jnp.where(theirs, taken, 0), axis=(1, 2))
+
+    first_weights, my_irrep = weights(0, 0, ab_irrep)
+    their_irrep = swapped(my_irrep)
+
+    pair_list, choices = pl.pallas_call(
         list_kernel,
-        out_shape=[shaped((LIST,), i32), shaped((KEPT,), i32)],
-        in_specs=[SMEM] * 3,
+        out_shape=[shaped((LIST,), i32), shaped((4,), i32)],
+        in_specs=[SMEM] * 6,
         out_specs=[SMEM] * 2,
         scratch_shapes=[numbers] * 2,
         compiler_params=GRANT,
         name="list",
-    )(cd_irrep, occ_irrep, counts)
+    )(cd_irrep, occ_irrep, counts, rows, ab_irrep, their_irrep)
+    chosen, general, most = choices[0], choices[1] > 0, choices[2]
 
     def products(full, wire, which, operands, rows_list):
         rows = SOURCES * (FULL if full else ROWS)
         return pl.pallas_call(
             functools.partial(product_kernel, full),
             out_shape=pltpu.VMEM((32, 16, wire), f32),
-            in_specs=[SMEM] + [VMEM] * len(operands) + [SMEM] * 4,
+            in_specs=[SMEM] + [VMEM] * len(operands) + [SMEM],
             out_specs=VMEM,
             scratch_shapes=[pltpu.VMEM((rows, 128), f32)] * 4
             + [pltpu.VMEM((wire, 128), f32), pltpu.VMEM((8 * TW, wire), f32)],
             compiler_params=LARGE,
-        )(which, *operands, *irreps, rows_list, kept)
+        )(which, *operands, rows_list)
 
     def full_products(wire, which):
         rows_list = pl.pallas_call(
@@ -404,8 +434,8 @@
             scratch_shapes=[numbers],
             compiler_params=GRANT,
             name="full_list",
-        )(occ_irrep, kept)
-        operands = [gathered_full(0), gathered_full(1), *first_weights, *weights(1)]
+        )(occ_irrep, pair_list)
+        operands = [gathered_full(0), gathered_full(1), *first_weights, *weights(1, 16, pair_list)[0]]
         return products(True, wire, which, operands, rows_list)
 
     def reduced(wire, which):
@@ -423,28 +453,36 @@
             compiler_params=GRANT,
             name="sum",
         )(arrived.astype(f32))
+        spots = pl.pallas_call(
+            functools.partial(places_kernel, wire - 1),
+            out_shape=[shaped((16, 128), i32)] * 2,
+            in_specs=[SMEM, SMEM, VMEM],
+            out_specs=[VMEM] * 2,
+            compiler_params=GRANT,
+            name="places",
+        )(which, pair_list, pairs)
+        theirs = swapped(partners)
         return pl.pallas_call(
             finish_kernel,
             out_shape=shaped((8, IJ), f32),
-            in_specs=[SMEM, VMEM, VMEM, SMEM, VMEM],
+            in_specs=[VMEM] * 4,
             out_specs=VMEM,
             compiler_params=GRANT,
             name="finish",
-        )(which, mine, swapped(partners), ab_irrep, pairs)
+        )(mine, theirs, *spots)
 
     zero = jnp.zeros((1,), i32)
 
     def all_rounds():
-        cols = WIRES[-1] - 1
+        cols = LONG - 1
 
         def add_round(number, total):
             which = jnp.full((1,), number, i32)
-            return total + reduced(WIRES[-1], which)
+            return total + reduced(LONG, which)
 
         return lax.fori_loop(0, (most + cols - 1) // cols, add_round, jnp.zeros((8, IJ), f32))
 
     branches = [functools.partial(reduced, wire, zero) for wire in WIRES]
-    chosen = sum((most >= wire).astype(i32) for wire in WIRES)
     return lax.switch(chosen, [*branches, all_rounds])
 
 

time: 95.8 us -> 95.2 us (level)
  between operations: 3.33 us -> 1.37 us
  other arithmetic: 3.02 us -> 1.5 us
  waiting for transfers between devices: 5.68 us -> 6.96 us
  local copies, waits for them, and re-layouts: 1 us -> 2.13 us
    all_to_all x1, waiting for transfers between devices: 4.86 us -> 6.95 us  [over_chips(): got = lax.all_to_all(sent, CHIPS, split_axis=0, concat_axis=0, tiled=True)]
    reduce_max x3 -> x0, other arithmetic: 2 us -> none  [the longest x2 1.34 us: body(): general = jnp.logical_or(jnp.max(rows) > ROWS, jnp.max(tiles) > WIDE)]
    pallas_call x3 -> x4, Pallas kernels: 10 us -> 10.4 us  [the longest x1 6.1 us: body(): pl.pallas_call(list_kernel, out_shape=[shaped((LIST,), i32), shaped((4,),...]
  transfers between devices with their start and end apart: 4 -> 4, of which waited for: 2 -> 1; matrix products, arithmetic and copies ran while one was open for 3% -> 2% of each run, Pallas kernels for 8% -> 8%
where the time goes in v8:
time: 95.2 us; the launch traced here: 94.7 us
  blocking collectives  35.1 us (37%)
  starting transfers between devices  28.9 us (30%)
  Pallas kernels  18.7 us (20%)
  waiting for transfers between devices  6.96 us (7%)
  local copies, waits for them, and re-layouts  2.13 us (2%)
  other arithmetic  1.5 us (2%)
  between operations  1.37 us (1%)
    all_to_all x1, blocking collectives, reduced(): lax.all_to_all(partial, 'panel', split_axis=0, concat_axis=0, tiled=True)  35.1 us
    ppermute x3, starting transfers between devices, swapped(): return lax.ppermute(array, 'blk_2', [(0, 1), (1, 0)])  24.5 us
    all_to_all x1, waiting for transfers between devices, over_chips(): got = lax.all_to_all(sent, CHIPS, split_axis=0, concat_axis=0, tiled=True)  6.95 us
    pallas_call x1, Pallas kernels, body(): pl.pallas_call(list_kernel, out_shape=[shaped((LIST,), i32), shaped((4,),...  6.1 us
    pallas_call x1, Pallas kernels, products(): pl.pallas_call(functools.partial(product_kernel, full), out_shape=pltpu.V...  5.9 us
    all_to_all x1, starting transfers between devices, over_chips(): got = lax.all_to_all(sent, CHIPS, split_axis=0, concat_axis=0, tiled=True)  4.39 us
    pallas_call x1, Pallas kernels, weights(): pl.pallas_call(functools.partial(pack_rows_kernel, turn, first), out_shap...  2.24 us
    pallas_call x1, Pallas kernels, body(): pl.pallas_call(send_kernel, out_shape=shaped((SOURCES, ROWS, NARROW * TW)...  2.22 us
  transfers between devices with their start and end apart: 4, of which 1 were waited for; matrix products, arithmetic and copies ran while one was open for 2% of the time, Pallas kernels for 8%

profile of v8, /device:TPU:1, one launch (start us, length us, event | category | flops | bytes accessed | tf_op | source)
XLA Modules:
  0.0 94.7 jit_solution(15281641695519218389)
XLA Ops:
  0.0 0.7 copy-done
  0.7 2.2 %shard_map.121 = (bf16[256,512]{1,0:T(8,128)(2,1)}, s32[4]{0:T(128)S(1)}) custom-call(bf16[256,1024]{1,0:T(8,128)(2,1)} %v_ref.1, s32[4]{0:T(128)S(1)} %copy-done, s32[16]{0:T(128)} %cd_ref.5), custom_call_target="tpu_custom_call" | custom-call | tf_op jit(solution)/shard_map/pallas_call | solution.py:361
  2.9 16.0 %collective-permute-start.6 = (s32[4]{0:T(128)S(1)}, s32[4]{0:T(128)S(1)}, u32[]{:S(2)}, u32[]{:S(2)}) collective-permute-start(s32[4]{0:T(128)S(1)} %get-tuple-element.305), channel_id=1, source_target_pairs={{0,32},{32,0},{1,33},{33,1},{2,34},{34,2},{3,35},{35,3},{4,36},{36... | collective-permute-start | bytes 56 | tf_op jit(solution)/shard_map/ppermute | solution.py:347
  19.0 1.9 %collective-permute-start.7 = (bf16[256,512]{1,0:T(8,128)(2,1)}, bf16[256,512]{1,0:T(8,128)(2,1)}, u32[]{:S(2)}, u32[]{:S(2)}) collective-permute-start(bf16[256,512]{1,0:T(8,128)(2,1)} %get-tuple-element.307), channel_id=1, source_target_pairs={{0,32},{32,0},{1,33},{33,1},{2,34},{34,2},{3,35},{35,3},{4,36},{36... | collective-permute-start | bytes 786440 | tf_op jit(solution)/shard_map/ppermute | solution.py:347
  20.9 2.2 %send.1 = bf16[16,144,128]{2,1,0:T(8,128)(2,1)} custom-call(bf16[50,1024]{1,0:T(8,128)(2,1)S(1)} %copy-done.7, s32[16]{0:T(128)S(1)} %copy-done.9, s32[40]{0:T(128)S(1)} %copy-done.8), custom_call_target="tpu_custom_call" | custom-call | tf_op jit(solution)/shard_map/send/pallas_call | solution.py:371
  23.1 4.4 %all-to-all-start.9 = ((bf16[16,144,128]{2,1,0:T(8,128)(2,1)}), bf16[16,144,128]{2,1,0:T(8,128)(2,1)}, u32[]{:S(2)}, u32[]{:S(2)}) async-start(bf16[16,144,128]{2,1,0:T(8,128)(2,1)} %send.1), calls=%async_computation.9 | async-start | bytes 1179648 | tf_op jit(solution)/shard_map/all_to_all | solution.py:343
  27.5 0.1 convert_reduce_fusion.1
  27.7 0.1 select_reduce_fusion
  27.8 0.5 copy-done.10
  28.4 0.1 select_reduce_fusion.3
  28.5 0.4 convert_reduce_fusion.counts_ref
  28.8 0.3 copy-done.11
  29.2 0.7 select_reduce_fusion.2.rows_ref
  29.8 6.1 %list.1 = (s32[1408]{0:T(1024)S(1)}, s32[4]{0:T(128)S(1)}) custom-call(s32[16]{0:T(128)S(1)} %copy-done.9, s32[40]{0:T(128)S(1)} %copy-done.8, s32[16]{0:T(128)S(1)} %convert_reduce_fusion.counts_ref, s32[32]{0:T(128)S(1)} %select_reduce_fusion.2.rows_ref, s32[4]{0:T(128)S(1)} %copy-done.1, s32[4]{0:T(128)S(1)} %collective-permute-done.6.theirs_ref), custom_call_target="tpu_custom_call" | custom-call | tf_op jit(solution)/shard_map/list/pallas_call | solution.py:405
  36.0 0.6 fusion.1
  37.8 7.0 %all-to-all-done.9 = bf16[16,144,128]{2,1,0:T(8,128)(2,1)} async-done(((bf16[16,144,128]{2,1,0:T(8,128)(2,1)}), bf16[16,144,128]{2,1,0:T(8,128)(2,1)}, u32[]{:S(2)}, u32[]{:S(2)}) %all-to-all-start.9) | async-done | bytes 589856 | tf_op jit(solution)/shard_map/all_to_all | solution.py:343
  44.7 49.9 %conditional.4 = (f32[8,1600]{1,0:T(8,128)}) conditional(s32[]{:T(128)} %bitcast.9, (pred[]{:T(512)}, bf16[2304,128]{1,0:T(8,128)(2,1)}, bf16[256,512]{1,0:T(8,128)(2,1)}, bf16[256,512]{1,0:T(8,128)(2,1)}, s32[1408]{0:T(1024)S(1)}, /*index=5*/bf16[50,1024]{1,0:T(8,128)(2,1)S(1)}, s32[16]{0:T(128)S(1)}, s32[40]{0:T(128)S(1)}, ...), branch_computations={%region_6.9_spmd, %region_9.12_spmd, %region_12.17_spmd} | conditional | flops 537100 | bytes 19407582 | solution.py:486
  44.7 5.9 %conditional.1 = (f32[32,16,384]{2,1,0:T(8,128)S(1)}) conditional(s32[]{:T(128)} %convert_element_type.25, (bf16[2304,128]{1,0:T(8,128)(2,1)}, bf16[256,512]{1,0:T(8,128)(2,1)}, bf16[256,512]{1,0:T(8,128)(2,1)}, s32[1408]{0:T(1024)S(1)}) %tuple.27, (bf16[50,1024]{1,0:T(8,128)(2,1)S(1)}, s32[16]{0:T(128)S(1)}, s32[40]{0:T(128)S(1)}, ...), branch_computations={%region_10.10_spmd, %region_11.11_spmd} | conditional | bytes 6553712 | solution.py:442
  44.7 5.9 %branch_0_fun.4 = f32[32,16,384]{2,1,0:T(8,128)S(1)} custom-call(s32[1]{0:T(128)} %constant.60.clone.round_ref, bf16[2304,128]{1,0:T(8,128)(2,1)} %get-tuple-element.230.refs_0_, bf16[256,512]{1,0:T(8,128)(2,1)} %get-tuple-element.231.refs_1_, bf16[256,512]{1,0:T(8,128)(2,1)} %get-tuple-element.232.refs_2_, s32[1408]{0:T(1024)S(1)} %get-tuple-element.233.refs_3_), custom_call_target="tpu_custom_call" | custom-call | tf_op jit(solution)/shard_map/cond/branch_1_fun/cond/branch_0_fun/pallas_call | solution.py:418
  50.7 35.1 %all_to_all.44 = f16[32,16,384]{2,1,0:T(8,128)(2,1)S(1)} all-to-all(f16[32,16,384]{2,1,0:T(8,128)(2,1)S(1)} %convert_element_type.26), channel_id=1, replica_groups=mesh['blk_0'=2,'blk_1'=8,'blk_2'=2,'panel'=32] {'panel'}, dimensions={0} | all-to-all | bytes 786432 | tf_op jit(solution)/shard_map/cond/branch_1_fun/all_to_all | solution.py:447
  85.9 0.1 sum.4
  86.0 6.6 %collective-permute-start.3 = (f32[8,384]{1,0:T(8,128)S(1)}, f32[8,384]{1,0:T(8,128)S(1)}, u32[]{:S(2)}, u32[]{:S(2)}) collective-permute-start(f32[8,384]{1,0:T(8,128)S(1)} %get-tuple-element.252), channel_id=1, source_target_pairs={{0,32},{32,0},{1,33},{33,1},{2,34},{34,2},{3,35},{35,3},{4,36},{36... | collective-permute-start | bytes 36872 | tf_op jit(solution)/shard_map/cond/branch_1_fun/ppermute | solution.py:347
  92.6 1.2 %places.4 = (s32[16,128]{1,0:T(8,128)S(1)}, s32[16,128]{1,0:T(8,128)S(1)}) custom-call(s32[1]{0:T(128)} %constant.62.clone.round_ref, s32[1408]{0:T(1024)S(1)} %get-tuple-element.246.list_ref, s32[16,128]{1,0:T(8,128)S(1)} %get-tuple-element.253.pairs_ref), custom_call_target="tpu_custom_call" | custom-call | tf_op jit(solution)/shard_map/cond/branch_1_fun/places/pallas_call | solution.py:456
  93.8 0.9 finish.4
  (24 shorter events, 0.2 us)
Async XLA Ops:
  0.0 0.7 copy-start
  0.7 20.2 %copy-start.7 = (bf16[50,1024]{1,0:T(8,128)(2,1)S(1)}, bf16[50,1024]{1,0:T(8,128)(2,1)}, u32[]{:S(2)}) copy-start(bf16[50,1024]{1,0:T(8,128)(2,1)} %t_ref.1) | copy-start | bytes 307204
  2.9 18.0 %copy-start.8 = (s32[40]{0:T(128)S(1)}, s32[40]{0:T(128)}, u32[]{:S(2)}) copy-start(s32[40]{0:T(128)} %occ_ref.3) | copy-start | bytes 484
  2.9 18.0 %copy-start.9 = (s32[16]{0:T(128)S(1)}, s32[16]{0:T(128)}, u32[]{:S(2)}) copy-start(s32[16]{0:T(128)} %cd_ref.5) | copy-start | bytes 196
  2.9 26.9 %collective-permute-start.6 = (s32[4]{0:T(128)S(1)}, s32[4]{0:T(128)S(1)}, u32[]{:S(2)}, u32[]{:S(2)}) collective-permute-start(s32[4]{0:T(128)S(1)} %get-tuple-element.305), channel_id=1, source_target_pairs={{0,32},{32,0},{1,33},{33,1},{2,34},{34,2},{3,35},{35,3},{4,36},{36... | collective-permute-start | bytes 56 | tf_op jit(solution)/shard_map/ppermute | solution.py:347
  19.0 18.8 %collective-permute-start.7 = (bf16[256,512]{1,0:T(8,128)(2,1)}, bf16[256,512]{1,0:T(8,128)(2,1)}, u32[]{:S(2)}, u32[]{:S(2)}) collective-permute-start(bf16[256,512]{1,0:T(8,128)(2,1)} %get-tuple-element.307), channel_id=1, source_target_pairs={{0,32},{32,0},{1,33},{33,1},{2,34},{34,2},{3,35},{35,3},{4,36},{36... | collective-permute-start | bytes 786440 | tf_op jit(solution)/shard_map/ppermute | solution.py:347
  23.1 4.5 %copy-start.12 = (s32[16,128]{1,0:T(8,128)S(1)}, s32[16,128]{1,0:T(8,128)}, u32[]{:S(2)}) copy-start(s32[16,128]{1,0:T(8,128)} %constant.76.clone) | copy-start | bytes 24580
  23.1 4.5 %copy-start.13 = (s32[16,128]{1,0:T(8,128)S(1)}, s32[16,128]{1,0:T(8,128)}, u32[]{:S(2)}) copy-start(s32[16,128]{1,0:T(8,128)} %constant.77.clone) | copy-start | bytes 24580
  23.1 21.6 %copy-start.2 = (bf16[256,1024]{1,0:T(8,128)(2,1)S(1)}, bf16[256,1024]{1,0:T(8,128)(2,1)}, u32[]{:S(2)}) copy-start(bf16[256,1024]{1,0:T(8,128)(2,1)} %v_ref.1) | copy-start | bytes 1572868
  23.1 21.6 %all-to-all-start.9 = ((bf16[16,144,128]{2,1,0:T(8,128)(2,1)}), bf16[16,144,128]{2,1,0:T(8,128)(2,1)}, u32[]{:S(2)}, u32[]{:S(2)}) async-start(bf16[16,144,128]{2,1,0:T(8,128)(2,1)} %send.1), calls=%async_computation.9 | async-start | bytes 1179648 | tf_op jit(solution)/shard_map/all_to_all | solution.py:343
  27.7 0.7 copy-start.10
  28.5 0.7 copy-start.11
  29.2 0.7 copy-start.1
  86.0 7.8 %collective-permute-start.3 = (f32[8,384]{1,0:T(8,128)S(1)}, f32[8,384]{1,0:T(8,128)S(1)}, u32[]{:S(2)}, u32[]{:S(2)}) collective-permute-start(f32[8,384]{1,0:T(8,128)S(1)} %get-tuple-element.252), channel_id=1, source_target_pairs={{0,32},{32,0},{1,33},{33,1},{2,34},{34,2},{3,35},{35,3},{4,36},{36... | collective-permute-start | bytes 36872 | tf_op jit(solution)/shard_map/cond/branch_1_fun/ppermute | solution.py:347

commit v9 on v8

--- a/solution.py
+++ b/solution.py
@@ -137,18 +137,22 @@
         out_ref[s, PAIRS:, :] = jnp.zeros((FULL - PAIRS, WIDE * TW), jnp.bfloat16)
 
 
-def pack_rows_kernel(turn, first, v_ref, ab_ref, cd_ref, out_ref, tiles_ref, choose):
+def pack_rows_kernel(turn, first, v_ref, ab_ref, cd_ref, out_ref, choose):
     irreps, ranks = places(cd_ref)
     fill_chooser(choose, ranks, turn)
     row = lax.broadcasted_iota(jnp.int32, (4 * TW, 1), 0) // TW
     row_irrep = jnp.zeros((4 * TW, 1), jnp.int32)
     for i in range(4):
         row_irrep = jnp.where(row == i, ab_ref[first + i], row_irrep)
-        tiles_ref[i] = ab_ref[first + i]
-    out_ref[...] = pack(v_ref[...], row_irrep, column_irreps(irreps), choose)
-
-
-def list_kernel(cd_ref, occ_ref, counts_ref, rows_ref, ab_ref, theirs_ref, list_ref, chosen_ref, count, need):
+    lane = lax.broadcasted_iota(jnp.int32, (8, WIDE * TW), 1) // 128
+    told = jnp.zeros((8, WIDE * TW), jnp.int32)
+    for i in range(4):
+        told = jnp.where(lane == i, ab_ref[first + i], told)
+    out_ref[4 * TW :, :] = told.astype(jnp.float32).astype(jnp.bfloat16)
+    out_ref[: 4 * TW, :] = pack(v_ref[...], row_irrep, column_irreps(irreps), choose)
+
+
+def list_kernel(cd_ref, occ_ref, counts_ref, rows_ref, ab_ref, list_ref, chosen_ref, count, need):
     core = lax.axis_index("blk_2")
     irreps, _ = places(cd_ref)
     count_rows(irreps, need)
@@ -161,7 +165,7 @@
         list_ref[k] = start
     for k in range(4):
         list_ref[16 + k] = ab_ref[k]
-        list_ref[20 + k] = theirs_ref[k]
+        list_ref[20 + k] = 0
     tiles, longest, most = jnp.int32(0), jnp.int32(0), jnp.int32(0)
     for g in range(IRREPS):
         tiles = jnp.maximum(tiles, need[g])
@@ -251,16 +255,19 @@
     for core in range(2):
         total = None
         for turn in range(turns):
-            part = times(rows[turn], weights[2 * turn + core][...])
+            part = times(rows[turn], weights[2 * turn + core][: 4 * TW, :])
             total = part if total is None else total + part
         for q in range(2):
             products[2 * core + q][...] = total[:, q * 128 : (q + 1) * 128]
     lower = lax.broadcasted_iota(jnp.int32, (1, 128), 1) < TW
     skip = round_ref[0] * cols
+    told = weights[1][4 * TW :, :].astype(jnp.float32)
+    tile_irreps = [list_ref[16 + i] for i in range(4)]
+    tile_irreps += [jnp.max(told[:, i * 128 : (i + 1) * 128]).astype(jnp.int32) for i in range(4)]
     for q in range(4):
         product = products[q]
         dense[...] = jnp.zeros_like(dense)
-        irreps = [list_ref[16 + 2 * q + i] for i in range(2)]
+        irreps = tile_irreps[2 * q : 2 * q + 2]
         starts = [jnp.minimum(list_ref[g] + skip, KEPT + IJ // 2) for g in irreps]
         counts = [list_ref[g + 1] - list_ref[g] - skip for g in irreps]
         most = jnp.clip(jnp.maximum(counts[0], counts[1]), 0, cols)
@@ -358,15 +365,15 @@
         return over_chips(sent)
 
     def weights(turn, first, irreps):
-        mine, tiles = pl.pallas_call(
+        mine = pl.pallas_call(
             functools.partial(pack_rows_kernel, turn, first),
-            out_shape=[shaped((4 * TW, width), bf16), shaped((4,), i32)],
+            out_shape=shaped((4 * TW + 8, width), bf16),
             in_specs=[VMEM, SMEM, SMEM],
-            out_specs=[VMEM, SMEM],
+            out_specs=VMEM,
             scratch_shapes=[chooser],
             compiler_params=GRANT,
         )(integrals, irreps, cd_irrep)
-        return [mine, swapped(mine)], tiles
+        return [mine, swapped(mine)]
 
     sent = pl.pallas_call(
         send_kernel,
@@ -399,18 +406,17 @@
     theirs = jnp.asarray(source)[None] == lax.broadcasted_iota(i32, (32, 16, 128), 0)
     rows = jnp.sum(jnp.where(theirs, taken, 0), axis=(1, 2))
 
-    first_weights, my_irrep = weights(0, 0, ab_irrep)
-    their_irrep = swapped(my_irrep)
+    first_weights = weights(0, 0, ab_irrep)
 
     pair_list, choices = pl.pallas_call(
         list_kernel,
         out_shape=[shaped((LIST,), i32), shaped((4,), i32)],
-        in_specs=[SMEM] * 6,
+        in_specs=[SMEM] * 5,
         out_specs=[SMEM] * 2,
         scratch_shapes=[numbers] * 2,
         compiler_params=GRANT,
         name="list",
-    )(cd_irrep, occ_irrep, counts, rows, ab_irrep, their_irrep)
+    )(cd_irrep, occ_irrep, counts, rows, ab_irrep)
     chosen, general, most = choices[0], choices[1] > 0, choices[2]
 
     def products(full, wire, which, operands, rows_list):
@@ -435,7 +441,7 @@
             compiler_params=GRANT,
             name="full_list",
         )(occ_irrep, pair_list)
-        operands = [gathered_full(0), gathered_full(1), *first_weights, *weights(1, 16, pair_list)[0]]
+        operands = [gathered_full(0), gathered_full(1), *first_weights, *weights(1, 16, pair_list)]
         return products(True, wire, which, operands, rows_list)
 
     def reduced(wire, which):

time: 95.2 us -> 93.4 us (0.981)
  starting transfers between devices: 28.9 us -> 26.1 us
    ppermute x3 -> x2, starting transfers between devices: 24.5 us -> 21.8 us  [swapped(): return lax.ppermute(array, 'blk_2', [(0, 1), (1, 0)])]
  transfers between devices with their start and end apart: 4 -> 3, of which waited for: 1 -> 1; matrix products, arithmetic and copies ran while one was open for 2% -> 2% of each run, Pallas kernels for 8% -> 8%
where the time goes in v9:
time: 93.4 us; the launch traced here: 92.9 us
  blocking collectives  35.5 us (38%)
  starting transfers between devices  26.1 us (28%)
  Pallas kernels  18.7 us (20%)
  waiting for transfers between devices  7.46 us (8%)
  local copies, waits for them, and re-layouts  2.13 us (2%)
  other arithmetic  1.5 us (2%)
  between operations  1.38 us (1%)
    all_to_all x1, blocking collectives, reduced(): lax.all_to_all(partial, 'panel', split_axis=0, concat_axis=0, tiled=True)  35.5 us
    ppermute x2, starting transfers between devices, swapped(): return lax.ppermute(array, 'blk_2', [(0, 1), (1, 0)])  21.8 us
    all_to_all x1, waiting for transfers between devices, over_chips(): got = lax.all_to_all(sent, CHIPS, split_axis=0, concat_axis=0, tiled=True)  7.45 us
    pallas_call x1, Pallas kernels, body(): pl.pallas_call(list_kernel, out_shape=[shaped((LIST,), i32), shaped((4,),...  6.1 us
    pallas_call x1, Pallas kernels, products(): pl.pallas_call(functools.partial(product_kernel, full), out_shape=pltpu.V...  5.91 us
    all_to_all x1, starting transfers between devices, over_chips(): got = lax.all_to_all(sent, CHIPS, split_axis=0, concat_axis=0, tiled=True)  4.39 us
    pallas_call x1, Pallas kernels, weights(): pl.pallas_call(functools.partial(pack_rows_kernel, turn, first), out_shap...  2.24 us
    pallas_call x1, Pallas kernels, body(): pl.pallas_call(send_kernel, out_shape=shaped((SOURCES, ROWS, NARROW * TW)...  2.23 us
  transfers between devices with their start and end apart: 3, of which 1 were waited for; matrix products, arithmetic and copies ran while one was open for 2% of the time, Pallas kernels for 8%

profile of v9, /device:TPU:1, one launch (start us, length us, event | category | flops | bytes accessed | tf_op | source)
XLA Modules:
  0.0 92.9 jit_solution(11427245940805959713)
XLA Ops:
  0.0 0.7 copy-done
  0.7 2.2 %shard_map.121 = bf16[264,512]{1,0:T(8,128)(2,1)} custom-call(bf16[256,1024]{1,0:T(8,128)(2,1)} %v_ref.1, s32[4]{0:T(128)S(1)} %copy-done, s32[16]{0:T(128)} %cd_ref.5), custom_call_target="tpu_custom_call" | custom-call | tf_op jit(solution)/shard_map/pallas_call | solution.py:368
  2.9 16.0 %collective-permute-start.6 = (bf16[264,512]{1,0:T(8,128)(2,1)}, bf16[264,512]{1,0:T(8,128)(2,1)}, u32[]{:S(2)}, u32[]{:S(2)}) collective-permute-start(bf16[264,512]{1,0:T(8,128)(2,1)} %shard_map.121), channel_id=1, source_target_pairs={{0,32},{32,0},{1,33},{33,1},{2,34},{34,2},{3,35},{35,3},{4,36},{36... | collective-permute-start | bytes 811016 | tf_op jit(solution)/shard_map/ppermute | solution.py:354
  19.0 2.2 %send.1 = bf16[16,144,128]{2,1,0:T(8,128)(2,1)} custom-call(bf16[50,1024]{1,0:T(8,128)(2,1)S(1)} %copy-done.7, s32[16]{0:T(128)S(1)} %copy-done.19, s32[40]{0:T(128)S(1)} %copy-done.12), custom_call_target="tpu_custom_call" | custom-call | tf_op jit(solution)/shard_map/send/pallas_call | solution.py:378
  21.2 4.4 %all-to-all-start.9 = ((bf16[16,144,128]{2,1,0:T(8,128)(2,1)}), bf16[16,144,128]{2,1,0:T(8,128)(2,1)}, u32[]{:S(2)}, u32[]{:S(2)}) async-start(bf16[16,144,128]{2,1,0:T(8,128)(2,1)} %send.1), calls=%async_computation.9 | async-start | bytes 1179648 | tf_op jit(solution)/shard_map/all_to_all | solution.py:350
  25.6 0.1 convert_reduce_fusion.1
  25.7 0.1 select_reduce_fusion
  25.9 0.5 copy-done.26
  26.4 0.1 select_reduce_fusion.3
  26.5 0.4 convert_reduce_fusion.counts_ref
  26.9 0.1 copy-done.8
  27.0 0.2 copy-done.27
  27.2 0.7 select_reduce_fusion.2.rows_ref
  27.9 6.1 %list.1 = (s32[1408]{0:T(1024)S(1)}, s32[4]{0:T(128)S(1)}) custom-call(s32[16]{0:T(128)S(1)} %copy-done.19, s32[40]{0:T(128)S(1)} %copy-done.12, s32[16]{0:T(128)S(1)} %convert_reduce_fusion.counts_ref, s32[32]{0:T(128)S(1)} %select_reduce_fusion.2.rows_ref, s32[4]{0:T(128)S(1)} %copy-done.1), custom_call_target="tpu_custom_call" | custom-call | tf_op jit(solution)/shard_map/list/pallas_call | solution.py:411
  34.0 0.6 fusion.1
  35.9 7.5 %all-to-all-done.9 = bf16[16,144,128]{2,1,0:T(8,128)(2,1)} async-done(((bf16[16,144,128]{2,1,0:T(8,128)(2,1)}), bf16[16,144,128]{2,1,0:T(8,128)(2,1)}, u32[]{:S(2)}, u32[]{:S(2)}) %all-to-all-start.9) | async-done | bytes 589856 | tf_op jit(solution)/shard_map/all_to_all | solution.py:350
  43.3 49.6 %conditional.4 = (f32[8,1600]{1,0:T(8,128)}) conditional(s32[]{:T(128)} %bitcast.9, (pred[]{:T(512)}, bf16[2304,128]{1,0:T(8,128)(2,1)}, bf16[264,512]{1,0:T(8,128)(2,1)}, bf16[264,512]{1,0:T(8,128)(2,1)}, s32[1408]{0:T(1024)S(1)}, /*index=5*/bf16[50,1024]{1,0:T(8,128)(2,1)S(1)}, s32[16]{0:T(128)S(1)}, s32[40]{0:T(128)S(1)}, ...), branch_computations={%region_6.9_spmd, %region_9.12_spmd, %region_12.17_spmd} | conditional | flops 537100 | bytes 19476954 | solution.py:492
  43.3 5.9 %conditional.1 = (f32[32,16,384]{2,1,0:T(8,128)S(1)}) conditional(s32[]{:T(128)} %convert_element_type.25, (bf16[2304,128]{1,0:T(8,128)(2,1)}, bf16[264,512]{1,0:T(8,128)(2,1)}, bf16[264,512]{1,0:T(8,128)(2,1)}, s32[1408]{0:T(1024)S(1)}) %tuple.27, (bf16[50,1024]{1,0:T(8,128)(2,1)S(1)}, s32[16]{0:T(128)S(1)}, s32[40]{0:T(128)S(1)}, ...), branch_computations={%region_10.10_spmd, %region_11.11_spmd} | conditional | bytes 6587048 | solution.py:448
  43.3 5.9 %branch_0_fun.4 = f32[32,16,384]{2,1,0:T(8,128)S(1)} custom-call(s32[1]{0:T(128)} %constant.60.clone.round_ref, bf16[2304,128]{1,0:T(8,128)(2,1)} %get-tuple-element.229.refs_0_, bf16[264,512]{1,0:T(8,128)(2,1)} %get-tuple-element.230.refs_1_, bf16[264,512]{1,0:T(8,128)(2,1)} %get-tuple-element.231.refs_2_, s32[1408]{0:T(1024)S(1)} %get-tuple-element.232.refs_3_), custom_call_target="tpu_custom_call" | custom-call | tf_op jit(solution)/shard_map/cond/branch_1_fun/cond/branch_0_fun/pallas_call | solution.py:424
  49.3 35.5 %all_to_all.44 = f16[32,16,384]{2,1,0:T(8,128)(2,1)S(1)} all-to-all(f16[32,16,384]{2,1,0:T(8,128)(2,1)S(1)} %convert_element_type.26), channel_id=1, replica_groups=mesh['blk_0'=2,'blk_1'=8,'blk_2'=2,'panel'=32] {'panel'}, dimensions={0} | all-to-all | bytes 786432 | tf_op jit(solution)/shard_map/cond/branch_1_fun/all_to_all | solution.py:453
  84.9 0.1 sum.4
  85.0 5.8 %collective-permute-start.3 = (f32[8,384]{1,0:T(8,128)S(1)}, f32[8,384]{1,0:T(8,128)S(1)}, u32[]{:S(2)}, u32[]{:S(2)}) collective-permute-start(f32[8,384]{1,0:T(8,128)S(1)} %get-tuple-element.250), channel_id=1, source_target_pairs={{0,32},{32,0},{1,33},{33,1},{2,34},{34,2},{3,35},{35,3},{4,36},{36... | collective-permute-start | bytes 36872 | tf_op jit(solution)/shard_map/cond/branch_1_fun/ppermute | solution.py:354
  90.8 1.2 %places.4 = (s32[16,128]{1,0:T(8,128)S(1)}, s32[16,128]{1,0:T(8,128)S(1)}) custom-call(s32[1]{0:T(128)} %constant.62.clone.round_ref, s32[1408]{0:T(1024)S(1)} %get-tuple-element.244.list_ref, s32[16,128]{1,0:T(8,128)S(1)} %copy-done.10), custom_call_target="tpu_custom_call" | custom-call | tf_op jit(solution)/shard_map/cond/branch_1_fun/places/pallas_call | solution.py:462
  92.0 0.9 finish.4
  (26 shorter events, 0.2 us)
Async XLA Ops:
  0.0 0.7 copy-start
  0.7 18.3 %copy-start.7 = (bf16[50,1024]{1,0:T(8,128)(2,1)S(1)}, bf16[50,1024]{1,0:T(8,128)(2,1)}, u32[]{:S(2)}) copy-start(bf16[50,1024]{1,0:T(8,128)(2,1)} %t_ref.1) | copy-start | bytes 307204
  0.7 18.3 %copy-start.12 = (s32[40]{0:T(128)S(1)}, s32[40]{0:T(128)}, u32[]{:S(2)}) copy-start(s32[40]{0:T(128)} %occ_ref.3) | copy-start | bytes 484
  0.7 18.3 %copy-start.19 = (s32[16]{0:T(128)S(1)}, s32[16]{0:T(128)}, u32[]{:S(2)}) copy-start(s32[16]{0:T(128)} %cd_ref.5) | copy-start | bytes 196
  2.9 32.9 %collective-permute-start.6 = (bf16[264,512]{1,0:T(8,128)(2,1)}, bf16[264,512]{1,0:T(8,128)(2,1)}, u32[]{:S(2)}, u32[]{:S(2)}) collective-permute-start(bf16[264,512]{1,0:T(8,128)(2,1)} %shard_map.121), channel_id=1, source_target_pairs={{0,32},{32,0},{1,33},{33,1},{2,34},{34,2},{3,35},{35,3},{4,36},{36... | collective-permute-start | bytes 811016 | tf_op jit(solution)/shard_map/ppermute | solution.py:354
  21.2 4.5 %copy-start.28 = (s32[16,128]{1,0:T(8,128)S(1)}, s32[16,128]{1,0:T(8,128)}, u32[]{:S(2)}) copy-start(s32[16,128]{1,0:T(8,128)} %constant.76.clone) | copy-start | bytes 24580
  21.2 4.5 %copy-start.29 = (s32[16,128]{1,0:T(8,128)S(1)}, s32[16,128]{1,0:T(8,128)}, u32[]{:S(2)}) copy-start(s32[16,128]{1,0:T(8,128)} %constant.77.clone) | copy-start | bytes 24580
  21.2 22.1 %copy-start.2 = (bf16[256,1024]{1,0:T(8,128)(2,1)S(1)}, bf16[256,1024]{1,0:T(8,128)(2,1)}, u32[]{:S(2)}) copy-start(bf16[256,1024]{1,0:T(8,128)(2,1)} %v_ref.1) | copy-start | bytes 1572868
  21.2 22.1 %all-to-all-start.9 = ((bf16[16,144,128]{2,1,0:T(8,128)(2,1)}), bf16[16,144,128]{2,1,0:T(8,128)(2,1)}, u32[]{:S(2)}, u32[]{:S(2)}) async-start(bf16[16,144,128]{2,1,0:T(8,128)(2,1)} %send.1), calls=%async_computation.9 | async-start | bytes 1179648 | tf_op jit(solution)/shard_map/all_to_all | solution.py:350
  25.7 0.7 copy-start.26
  26.4 0.6 copy-start.8
  26.5 0.7 copy-start.27
  27.2 0.7 copy-start.1
  84.9 5.9 %copy-start.10 = (s32[16,128]{1,0:T(8,128)S(1)}, s32[16,128]{1,0:T(8,128)}, u32[]{:S(2)}) copy-start(s32[16,128]{1,0:T(8,128)} %get-tuple-element.251.pairs_ref) | copy-start | bytes 24580 | tf_op jit(solution)/shard_map/cond
  85.0 7.0 %collective-permute-start.3 = (f32[8,384]{1,0:T(8,128)S(1)}, f32[8,384]{1,0:T(8,128)S(1)}, u32[]{:S(2)}, u32[]{:S(2)}) collective-permute-start(f32[8,384]{1,0:T(8,128)S(1)} %get-tuple-element.250), channel_id=1, source_target_pairs={{0,32},{32,0},{1,33},{33,1},{2,34},{34,2},{3,35},{35,3},{4,36},{36... | collective-permute-start | bytes 36872 | tf_op jit(solution)/shard_map/cond/branch_1_fun/ppermute | solution.py:354

commit v10 on v9

--- a/solution.py
+++ b/solution.py
@@ -272,10 +272,10 @@
         counts = [list_ref[g + 1] - list_ref[g] - skip for g in irreps]
         most = jnp.clip(jnp.maximum(counts[0], counts[1]), 0, cols)
 
-        @pl.loop(0, (most + 7) // 8)
+        @pl.loop(0, (most + 15) // 16)
         def _(block):
-            base = block * 8
-            for u in range(8):
+            base = block * 16
+            for u in range(16):
                 at = [list_ref[start + base + u] for start in starts]
                 picked = [product[pl.ds(a, 1), :] for a in at]
                 dense[pl.ds(base + u, 1), :] = jnp.where(lower, picked[0], picked[1])

time: 93.4 us -> 95.5 us (1.022)
  loops' own time: 0.08 us -> 2.29 us
    another operation x1, loops' own time: 0.01 us -> 1.75 us  [reduced(): lax.cond(general, lambda: full_products(wire, which), lambda: products(Fa...]
where the time goes in v10:
time: 95.5 us; the launch traced here: 95 us
  blocking collectives  35.5 us (37%)
  starting transfers between devices  26.1 us (27%)
  Pallas kernels  18.4 us (19%)
  waiting for transfers between devices  7.46 us (8%)
  loops' own time  2.29 us (2%)
  local copies, waits for them, and re-layouts  2.13 us (2%)
  between operations  1.56 us (2%)
  other arithmetic  1.5 us (2%)
    all_to_all x1, blocking collectives, reduced(): lax.all_to_all(partial, 'panel', split_axis=0, concat_axis=0, tiled=True)  35.5 us
    ppermute x2, starting transfers between devices, swapped(): return lax.ppermute(array, 'blk_2', [(0, 1), (1, 0)])  21.8 us
    all_to_all x1, waiting for transfers between devices, over_chips(): got = lax.all_to_all(sent, CHIPS, split_axis=0, concat_axis=0, tiled=True)  7.45 us
    pallas_call x1, Pallas kernels, body(): pl.pallas_call(list_kernel, out_shape=[shaped((LIST,), i32), shaped((4,),...  6.1 us
    pallas_call x1, Pallas kernels, products(): pl.pallas_call(functools.partial(product_kernel, full), out_shape=pltpu.V...  5.59 us
    all_to_all x1, starting transfers between devices, over_chips(): got = lax.all_to_all(sent, CHIPS, split_axis=0, concat_axis=0, tiled=True)  4.39 us
    pallas_call x1, Pallas kernels, weights(): pl.pallas_call(functools.partial(pack_rows_kernel, turn, first), out_shap...  2.24 us
    pallas_call x1, Pallas kernels, body(): pl.pallas_call(send_kernel, out_shape=shaped((SOURCES, ROWS, NARROW * TW)...  2.23 us
  transfers between devices with their start and end apart: 3, of which 1 were waited for; matrix products, arithmetic and copies ran while one was open for 2% of the time, Pallas kernels for 8%

profile of v10, /device:TPU:1, one launch (start us, length us, event | category | flops | bytes accessed | tf_op | source)
XLA Modules:
  0.0 95.0 jit_solution(3925099463145347595)
XLA Ops:
  0.0 0.7 copy-done
  0.7 2.2 %shard_map.121 = bf16[264,512]{1,0:T(8,128)(2,1)} custom-call(bf16[256,1024]{1,0:T(8,128)(2,1)} %v_ref.1, s32[4]{0:T(128)S(1)} %copy-done, s32[16]{0:T(128)} %cd_ref.5), custom_call_target="tpu_custom_call" | custom-call | tf_op jit(solution)/shard_map/pallas_call | solution.py:368
  2.9 16.0 %collective-permute-start.6 = (bf16[264,512]{1,0:T(8,128)(2,1)}, bf16[264,512]{1,0:T(8,128)(2,1)}, u32[]{:S(2)}, u32[]{:S(2)}) collective-permute-start(bf16[264,512]{1,0:T(8,128)(2,1)} %shard_map.121), channel_id=1, source_target_pairs={{0,32},{32,0},{1,33},{33,1},{2,34},{34,2},{3,35},{35,3},{4,36},{36... | collective-permute-start | bytes 811016 | tf_op jit(solution)/shard_map/ppermute | solution.py:354
  19.0 2.2 %send.1 = bf16[16,144,128]{2,1,0:T(8,128)(2,1)} custom-call(bf16[50,1024]{1,0:T(8,128)(2,1)S(1)} %copy-done.7, s32[16]{0:T(128)S(1)} %copy-done.19, s32[40]{0:T(128)S(1)} %copy-done.12), custom_call_target="tpu_custom_call" | custom-call | tf_op jit(solution)/shard_map/send/pallas_call | solution.py:378
  21.2 4.4 %all-to-all-start.9 = ((bf16[16,144,128]{2,1,0:T(8,128)(2,1)}), bf16[16,144,128]{2,1,0:T(8,128)(2,1)}, u32[]{:S(2)}, u32[]{:S(2)}) async-start(bf16[16,144,128]{2,1,0:T(8,128)(2,1)} %send.1), calls=%async_computation.9 | async-start | bytes 1179648 | tf_op jit(solution)/shard_map/all_to_all | solution.py:350
  25.6 0.1 convert_reduce_fusion.1
  25.7 0.1 select_reduce_fusion
  25.9 0.5 copy-done.26
  26.4 0.1 select_reduce_fusion.3
  26.5 0.4 convert_reduce_fusion.counts_ref
  26.9 0.1 copy-done.8
  27.0 0.2 copy-done.27
  27.2 0.7 select_reduce_fusion.2.rows_ref
  27.9 6.1 %list.1 = (s32[1408]{0:T(1024)S(1)}, s32[4]{0:T(128)S(1)}) custom-call(s32[16]{0:T(128)S(1)} %copy-done.19, s32[40]{0:T(128)S(1)} %copy-done.12, s32[16]{0:T(128)S(1)} %convert_reduce_fusion.counts_ref, s32[32]{0:T(128)S(1)} %select_reduce_fusion.2.rows_ref, s32[4]{0:T(128)S(1)} %copy-done.1), custom_call_target="tpu_custom_call" | custom-call | tf_op jit(solution)/shard_map/list/pallas_call | solution.py:411
  34.0 0.6 fusion.1
  35.9 7.5 %all-to-all-done.9 = bf16[16,144,128]{2,1,0:T(8,128)(2,1)} async-done(((bf16[16,144,128]{2,1,0:T(8,128)(2,1)}), bf16[16,144,128]{2,1,0:T(8,128)(2,1)}, u32[]{:S(2)}, u32[]{:S(2)}) %all-to-all-start.9) | async-done | bytes 589856 | tf_op jit(solution)/shard_map/all_to_all | solution.py:350
  43.3 51.5 %conditional.4 = (f32[8,1600]{1,0:T(8,128)}) conditional(s32[]{:T(128)} %bitcast.9, (pred[]{:T(512)}, bf16[2304,128]{1,0:T(8,128)(2,1)}, bf16[264,512]{1,0:T(8,128)(2,1)}, bf16[264,512]{1,0:T(8,128)(2,1)}, s32[1408]{0:T(1024)S(1)}, /*index=5*/bf16[50,1024]{1,0:T(8,128)(2,1)S(1)}, s32[16]{0:T(128)S(1)}, s32[40]{0:T(128)S(1)}, ...), branch_computations={%region_6.9_spmd, %region_9.12_spmd, %region_12.17_spmd} | conditional | flops 537100 | bytes 19476954 | solution.py:492
  43.3 7.3 %conditional.1 = (f32[32,16,384]{2,1,0:T(8,128)S(1)}) conditional(s32[]{:T(128)} %convert_element_type.25, (bf16[2304,128]{1,0:T(8,128)(2,1)}, bf16[264,512]{1,0:T(8,128)(2,1)}, bf16[264,512]{1,0:T(8,128)(2,1)}, s32[1408]{0:T(1024)S(1)}) %tuple.27, (bf16[50,1024]{1,0:T(8,128)(2,1)S(1)}, s32[16]{0:T(128)S(1)}, s32[40]{0:T(128)S(1)}, ...), branch_computations={%region_10.10_spmd, %region_11.11_spmd} | conditional | bytes 6587048 | solution.py:448
  43.3 5.6 %branch_0_fun.4 = f32[32,16,384]{2,1,0:T(8,128)S(1)} custom-call(s32[1]{0:T(128)} %constant.60.clone.round_ref, bf16[2304,128]{1,0:T(8,128)(2,1)} %get-tuple-element.229.refs_0_, bf16[264,512]{1,0:T(8,128)(2,1)} %get-tuple-element.230.refs_1_, bf16[264,512]{1,0:T(8,128)(2,1)} %get-tuple-element.231.refs_2_, s32[1408]{0:T(1024)S(1)} %get-tuple-element.232.refs_3_), custom_call_target="tpu_custom_call" | custom-call | tf_op jit(solution)/shard_map/cond/branch_1_fun/cond/branch_0_fun/pallas_call | solution.py:424
  50.7 35.5 %all_to_all.44 = f16[32,16,384]{2,1,0:T(8,128)(2,1)S(1)} all-to-all(f16[32,16,384]{2,1,0:T(8,128)(2,1)S(1)} %convert_element_type.26), channel_id=1, replica_groups=mesh['blk_0'=2,'blk_1'=8,'blk_2'=2,'panel'=32] {'panel'}, dimensions={0} | all-to-all | bytes 786432 | tf_op jit(solution)/shard_map/cond/branch_1_fun/all_to_all | solution.py:453
  86.3 0.1 sum.4
  86.4 5.8 %collective-permute-start.3 = (f32[8,384]{1,0:T(8,128)S(1)}, f32[8,384]{1,0:T(8,128)S(1)}, u32[]{:S(2)}, u32[]{:S(2)}) collective-permute-start(f32[8,384]{1,0:T(8,128)S(1)} %get-tuple-element.250), channel_id=1, source_target_pairs={{0,32},{32,0},{1,33},{33,1},{2,34},{34,2},{3,35},{35,3},{4,36},{36... | collective-permute-start | bytes 36872 | tf_op jit(solution)/shard_map/cond/branch_1_fun/ppermute | solution.py:354
  92.2 1.2 %places.4 = (s32[16,128]{1,0:T(8,128)S(1)}, s32[16,128]{1,0:T(8,128)S(1)}) custom-call(s32[1]{0:T(128)} %constant.62.clone.round_ref, s32[1408]{0:T(1024)S(1)} %get-tuple-element.244.list_ref, s32[16,128]{1,0:T(8,128)S(1)} %copy-done.10), custom_call_target="tpu_custom_call" | custom-call | tf_op jit(solution)/shard_map/cond/branch_1_fun/places/pallas_call | solution.py:462
  93.4 0.9 finish.4
  (26 shorter events, 0.2 us)
Async XLA Ops:
  0.0 0.7 copy-start
  0.7 18.3 %copy-start.7 = (bf16[50,1024]{1,0:T(8,128)(2,1)S(1)}, bf16[50,1024]{1,0:T(8,128)(2,1)}, u32[]{:S(2)}) copy-start(bf16[50,1024]{1,0:T(8,128)(2,1)} %t_ref.1) | copy-start | bytes 307204
  0.7 18.3 %copy-start.12 = (s32[40]{0:T(128)S(1)}, s32[40]{0:T(128)}, u32[]{:S(2)}) copy-start(s32[40]{0:T(128)} %occ_ref.3) | copy-start | bytes 484
  0.7 18.3 %copy-start.19 = (s32[16]{0:T(128)S(1)}, s32[16]{0:T(128)}, u32[]{:S(2)}) copy-start(s32[16]{0:T(128)} %cd_ref.5) | copy-start | bytes 196
  2.9 32.9 %collective-permute-start.6 = (bf16[264,512]{1,0:T(8,128)(2,1)}, bf16[264,512]{1,0:T(8,128)(2,1)}, u32[]{:S(2)}, u32[]{:S(2)}) collective-permute-start(bf16[264,512]{1,0:T(8,128)(2,1)} %shard_map.121), channel_id=1, source_target_pairs={{0,32},{32,0},{1,33},{33,1},{2,34},{34,2},{3,35},{35,3},{4,36},{36... | collective-permute-start | bytes 811016 | tf_op jit(solution)/shard_map/ppermute | solution.py:354
  21.2 4.5 %copy-start.28 = (s32[16,128]{1,0:T(8,128)S(1)}, s32[16,128]{1,0:T(8,128)}, u32[]{:S(2)}) copy-start(s32[16,128]{1,0:T(8,128)} %constant.76.clone) | copy-start | bytes 24580
  21.2 4.5 %copy-start.29 = (s32[16,128]{1,0:T(8,128)S(1)}, s32[16,128]{1,0:T(8,128)}, u32[]{:S(2)}) copy-start(s32[16,128]{1,0:T(8,128)} %constant.77.clone) | copy-start | bytes 24580
  21.2 22.1 %copy-start.2 = (bf16[256,1024]{1,0:T(8,128)(2,1)S(1)}, bf16[256,1024]{1,0:T(8,128)(2,1)}, u32[]{:S(2)}) copy-start(bf16[256,1024]{1,0:T(8,128)(2,1)} %v_ref.1) | copy-start | bytes 1572868
  21.2 22.1 %all-to-all-start.9 = ((bf16[16,144,128]{2,1,0:T(8,128)(2,1)}), bf16[16,144,128]{2,1,0:T(8,128)(2,1)}, u32[]{:S(2)}, u32[]{:S(2)}) async-start(bf16[16,144,128]{2,1,0:T(8,128)(2,1)} %send.1), calls=%async_computation.9 | async-start | bytes 1179648 | tf_op jit(solution)/shard_map/all_to_all | solution.py:350
  25.7 0.7 copy-start.26
  26.4 0.6 copy-start.8
  26.5 0.7 copy-start.27
  27.2 0.7 copy-start.1
  86.3 5.9 %copy-start.10 = (s32[16,128]{1,0:T(8,128)S(1)}, s32[16,128]{1,0:T(8,128)}, u32[]{:S(2)}) copy-start(s32[16,128]{1,0:T(8,128)} %get-tuple-element.251.pairs_ref) | copy-start | bytes 24580 | tf_op jit(solution)/shard_map/cond
  86.4 7.0 %collective-permute-start.3 = (f32[8,384]{1,0:T(8,128)S(1)}, f32[8,384]{1,0:T(8,128)S(1)}, u32[]{:S(2)}, u32[]{:S(2)}) collective-permute-start(f32[8,384]{1,0:T(8,128)S(1)} %get-tuple-element.250), channel_id=1, source_target_pairs={{0,32},{32,0},{1,33},{33,1},{2,34},{34,2},{3,35},{35,3},{4,36},{36... | collective-permute-start | bytes 36872 | tf_op jit(solution)/shard_map/cond/branch_1_fun/ppermute | solution.py:354

commit v11 on v9

--- a/solution.py
+++ b/solution.py
@@ -444,7 +444,20 @@
         operands = [gathered_full(0), gathered_full(1), *first_weights, *weights(1, 16, pair_list)]
         return products(True, wire, which, operands, rows_list)
 
-    def reduced(wire, which):
+    def places_of(cols, which):
+        return pl.pallas_call(
+            functools.partial(places_kernel, cols),
+            out_shape=[shaped((16, 128), i32)] * 2,
+            in_specs=[SMEM, SMEM, VMEM],
+            out_specs=[VMEM] * 2,
+            compiler_params=GRANT,
+            name="places",
+        )(which, pair_list, pairs)
+
+    zero = jnp.zeros((1,), i32)
+    first_spots = places_of(IJ, zero)
+
+    def reduced(wire, which, spots=None):
         partial = lax.cond(
             general,
             lambda: full_products(wire, which),
@@ -459,14 +472,8 @@
             compiler_params=GRANT,
             name="sum",
         )(arrived.astype(f32))
-        spots = pl.pallas_call(
-            functools.partial(places_kernel, wire - 1),
-            out_shape=[shaped((16, 128), i32)] * 2,
-            in_specs=[SMEM, SMEM, VMEM],
-            out_specs=[VMEM] * 2,
-            compiler_params=GRANT,
-            name="places",
-        )(which, pair_list, pairs)
+        if spots is None:
+            spots = places_of(wire - 1, which)
         theirs = swapped(partners)
         return pl.pallas_call(
             finish_kernel,
@@ -477,8 +484,6 @@
             name="finish",
         )(mine, theirs, *spots)
 
-    zero = jnp.zeros((1,), i32)
-
     def all_rounds():
         cols = LONG - 1
 
@@ -488,7 +493,7 @@
 
         return lax.fori_loop(0, (most + cols - 1) // cols, add_round, jnp.zeros((8, IJ), f32))
 
-    branches = [functools.partial(reduced, wire, zero) for wire in WIRES]
+    branches = [functools.partial(reduced, wire, zero, first_spots) for wire in WIRES]
     return lax.switch(chosen, [*branches, all_rounds])
 
 

time: 93.4 us -> 93 us (level)
  waiting for transfers between devices: 7.46 us -> 6.44 us
    all_to_all x1, waiting for transfers between devices: 7.45 us -> 5.62 us  [over_chips(): got = lax.all_to_all(sent, CHIPS, split_axis=0, concat_axis=0, tiled=True)]
  transfers between devices with their start and end apart: 3 -> 3, of which waited for: 1 -> 2; matrix products, arithmetic and copies ran while one was open for 2% -> 2% of each run, Pallas kernels for 8% -> 9%
where the time goes in v11:
time: 93 us; the launch traced here: 92.5 us
  blocking collectives  35.5 us (38%)
  starting transfers between devices  26.1 us (28%)
  Pallas kernels  19.3 us (21%)
  waiting for transfers between devices  6.44 us (7%)
  local copies, waits for them, and re-layouts  2.13 us (2%)
  other arithmetic  1.5 us (2%)
  between operations  1.39 us (1%)
    all_to_all x1, blocking collectives, reduced(): lax.all_to_all(partial, 'panel', split_axis=0, concat_axis=0, tiled=True)  35.5 us
    ppermute x2, starting transfers between devices, swapped(): return lax.ppermute(array, 'blk_2', [(0, 1), (1, 0)])  21.7 us
    pallas_call x1, Pallas kernels, body(): pl.pallas_call(list_kernel, out_shape=[shaped((LIST,), i32), shaped((4,),...  6.1 us
    pallas_call x1, Pallas kernels, products(): pl.pallas_call(functools.partial(product_kernel, full), out_shape=pltpu.V...  5.92 us
    all_to_all x1, waiting for transfers between devices, over_chips(): got = lax.all_to_all(sent, CHIPS, split_axis=0, concat_axis=0, tiled=True)  5.62 us
    all_to_all x1, starting transfers between devices, over_chips(): got = lax.all_to_all(sent, CHIPS, split_axis=0, concat_axis=0, tiled=True)  4.38 us
    pallas_call x1, Pallas kernels, weights(): pl.pallas_call(functools.partial(pack_rows_kernel, turn, first), out_shap...  2.25 us
    pallas_call x1, Pallas kernels, body(): pl.pallas_call(send_kernel, out_shape=shaped((SOURCES, ROWS, NARROW * TW)...  2.23 us
  transfers between devices with their start and end apart: 3, of which 2 were waited for; matrix products, arithmetic and copies ran while one was open for 2% of the time, Pallas kernels for 9%

profile of v11, /device:TPU:1, one launch (start us, length us, event | category | flops | bytes accessed | tf_op | source)
XLA Modules:
  0.0 92.5 jit_solution(2760254922118436933)
XLA Ops:
  0.0 0.7 copy-done
  0.7 2.3 %shard_map.121 = bf16[264,512]{1,0:T(8,128)(2,1)} custom-call(bf16[256,1024]{1,0:T(8,128)(2,1)} %v_ref.1, s32[4]{0:T(128)S(1)} %copy-done, s32[16]{0:T(128)} %cd_ref.5), custom_call_target="tpu_custom_call" | custom-call | tf_op jit(solution)/shard_map/pallas_call | solution.py:368
  2.9 16.0 %collective-permute-start.6 = (bf16[264,512]{1,0:T(8,128)(2,1)}, bf16[264,512]{1,0:T(8,128)(2,1)}, u32[]{:S(2)}, u32[]{:S(2)}) collective-permute-start(bf16[264,512]{1,0:T(8,128)(2,1)} %shard_map.121), channel_id=1, source_target_pairs={{0,32},{32,0},{1,33},{33,1},{2,34},{34,2},{3,35},{35,3},{4,36},{36... | collective-permute-start | bytes 811016 | tf_op jit(solution)/shard_map/ppermute | solution.py:354
  19.0 2.2 %send.1 = bf16[16,144,128]{2,1,0:T(8,128)(2,1)} custom-call(bf16[50,1024]{1,0:T(8,128)(2,1)S(1)} %copy-done.7, s32[16]{0:T(128)S(1)} %copy-done.17, s32[40]{0:T(128)S(1)} %copy-done.10), custom_call_target="tpu_custom_call" | custom-call | tf_op jit(solution)/shard_map/send/pallas_call | solution.py:378
  21.2 4.4 %all-to-all-start.9 = ((bf16[16,144,128]{2,1,0:T(8,128)(2,1)}), bf16[16,144,128]{2,1,0:T(8,128)(2,1)}, u32[]{:S(2)}, u32[]{:S(2)}) async-start(bf16[16,144,128]{2,1,0:T(8,128)(2,1)} %send.1), calls=%async_computation.9 | async-start | bytes 1179648 | tf_op jit(solution)/shard_map/all_to_all | solution.py:350
  25.6 0.1 convert_reduce_fusion.1
  25.7 0.1 select_reduce_fusion
  25.9 0.5 copy-done.28
  26.4 0.1 select_reduce_fusion.3
  26.5 0.4 convert_reduce_fusion.counts_ref
  26.9 0.3 copy-done.29
  27.2 0.7 select_reduce_fusion.2.rows_ref
  27.9 6.1 %list.1 = (s32[1408]{0:T(1024)S(1)}, s32[4]{0:T(128)S(1)}) custom-call(s32[16]{0:T(128)S(1)} %copy-done.17, s32[40]{0:T(128)S(1)} %copy-done.10, s32[16]{0:T(128)S(1)} %convert_reduce_fusion.counts_ref, s32[32]{0:T(128)S(1)} %select_reduce_fusion.2.rows_ref, s32[4]{0:T(128)S(1)} %copy-done.1), custom_call_target="tpu_custom_call" | custom-call | tf_op jit(solution)/shard_map/list/pallas_call | solution.py:411
  34.0 1.8 %places.2 = (s32[16,128]{1,0:T(8,128)}, s32[16,128]{1,0:T(8,128)}) custom-call(s32[1]{0:T(128)} %constant.68.clone.1.round_ref, s32[1408]{0:T(1024)S(1)} %get-tuple-element.305.list_ref, s32[16,128]{1,0:T(8,128)S(1)} %get-tuple-element.337.pairs_ref), custom_call_target="tpu_custom_call" | custom-call | tf_op jit(solution)/shard_map/places/pallas_call | solution.py:448
  35.8 0.6 fusion.1
  37.7 5.6 %all-to-all-done.9 = bf16[16,144,128]{2,1,0:T(8,128)(2,1)} async-done(((bf16[16,144,128]{2,1,0:T(8,128)(2,1)}), bf16[16,144,128]{2,1,0:T(8,128)(2,1)}, u32[]{:S(2)}, u32[]{:S(2)}) %all-to-all-start.9) | async-done | bytes 589856 | tf_op jit(solution)/shard_map/all_to_all | solution.py:350
  43.3 49.2 %conditional.4 = (f32[8,1600]{1,0:T(8,128)}) conditional(s32[]{:T(128)} %bitcast.9, (pred[]{:T(512)}, bf16[2304,128]{1,0:T(8,128)(2,1)}, bf16[264,512]{1,0:T(8,128)(2,1)}, bf16[264,512]{1,0:T(8,128)(2,1)}, s32[1408]{0:T(1024)S(1)}, /*index=5*/bf16[50,1024]{1,0:T(8,128)(2,1)S(1)}, s32[16]{0:T(128)S(1)}, s32[40]{0:T(128)S(1)}, ...), branch_computations={%region_6.9_spmd, %region_9.12_spmd, %region_12.17_spmd} | conditional | flops 537100 | bytes 19476954 | solution.py:497
  43.3 5.9 %conditional.1 = (f32[32,16,384]{2,1,0:T(8,128)S(1)}) conditional(s32[]{:T(128)} %convert_element_type.25, (bf16[2304,128]{1,0:T(8,128)(2,1)}, bf16[264,512]{1,0:T(8,128)(2,1)}, bf16[264,512]{1,0:T(8,128)(2,1)}, s32[1408]{0:T(1024)S(1)}) %tuple.27, (bf16[50,1024]{1,0:T(8,128)(2,1)S(1)}, s32[16]{0:T(128)S(1)}, s32[40]{0:T(128)S(1)}, ...), branch_computations={%region_10.10_spmd, %region_11.11_spmd} | conditional | bytes 6587048 | solution.py:461
  43.3 5.9 %branch_0_fun.4 = f32[32,16,384]{2,1,0:T(8,128)S(1)} custom-call(s32[1]{0:T(128)} %constant.58.clone.round_ref, bf16[2304,128]{1,0:T(8,128)(2,1)} %get-tuple-element.232.refs_0_, bf16[264,512]{1,0:T(8,128)(2,1)} %get-tuple-element.233.refs_1_, bf16[264,512]{1,0:T(8,128)(2,1)} %get-tuple-element.234.refs_2_, s32[1408]{0:T(1024)S(1)} %get-tuple-element.235.refs_3_), custom_call_target="tpu_custom_call" | custom-call | tf_op jit(solution)/shard_map/cond/branch_1_fun/cond/branch_0_fun/pallas_call | solution.py:424
  49.3 35.5 %all_to_all.44 = f16[32,16,384]{2,1,0:T(8,128)(2,1)S(1)} all-to-all(f16[32,16,384]{2,1,0:T(8,128)(2,1)S(1)} %convert_element_type.26), channel_id=1, replica_groups=mesh['blk_0'=2,'blk_1'=8,'blk_2'=2,'panel'=32] {'panel'}, dimensions={0} | all-to-all | bytes 786432 | tf_op jit(solution)/shard_map/cond/branch_1_fun/all_to_all | solution.py:466
  84.9 0.1 sum.4
  85.1 5.7 %collective-permute-start.3 = (f32[8,384]{1,0:T(8,128)S(1)}, f32[8,384]{1,0:T(8,128)S(1)}, u32[]{:S(2)}, u32[]{:S(2)}) collective-permute-start(f32[8,384]{1,0:T(8,128)S(1)} %get-tuple-element.253), channel_id=1, source_target_pairs={{0,32},{32,0},{1,33},{33,1},{2,34},{34,2},{3,35},{35,3},{4,36},{36... | collective-permute-start | bytes 36872 | tf_op jit(solution)/shard_map/cond/branch_1_fun/ppermute | solution.py:354
  90.8 0.8 collective-permute-done.3.partner_ref
  91.6 0.9 finish.4
  (28 shorter events, 0.2 us)
Async XLA Ops:
  0.0 0.7 copy-start
  0.7 18.3 %copy-start.7 = (bf16[50,1024]{1,0:T(8,128)(2,1)S(1)}, bf16[50,1024]{1,0:T(8,128)(2,1)}, u32[]{:S(2)}) copy-start(bf16[50,1024]{1,0:T(8,128)(2,1)} %t_ref.1) | copy-start | bytes 307204
  0.7 18.3 %copy-start.10 = (s32[40]{0:T(128)S(1)}, s32[40]{0:T(128)}, u32[]{:S(2)}) copy-start(s32[40]{0:T(128)} %occ_ref.3) | copy-start | bytes 484
  0.7 18.3 %copy-start.17 = (s32[16]{0:T(128)S(1)}, s32[16]{0:T(128)}, u32[]{:S(2)}) copy-start(s32[16]{0:T(128)} %cd_ref.5) | copy-start | bytes 196
  2.9 34.8 %collective-permute-start.6 = (bf16[264,512]{1,0:T(8,128)(2,1)}, bf16[264,512]{1,0:T(8,128)(2,1)}, u32[]{:S(2)}, u32[]{:S(2)}) collective-permute-start(bf16[264,512]{1,0:T(8,128)(2,1)} %shard_map.121), channel_id=1, source_target_pairs={{0,32},{32,0},{1,33},{33,1},{2,34},{34,2},{3,35},{35,3},{4,36},{36... | collective-permute-start | bytes 811016 | tf_op jit(solution)/shard_map/ppermute | solution.py:354
  21.2 4.5 %copy-start.30 = (s32[16,128]{1,0:T(8,128)S(1)}, s32[16,128]{1,0:T(8,128)}, u32[]{:S(2)}) copy-start(s32[16,128]{1,0:T(8,128)} %constant.73.clone) | copy-start | bytes 24580
  21.2 4.5 %copy-start.31 = (s32[16,128]{1,0:T(8,128)S(1)}, s32[16,128]{1,0:T(8,128)}, u32[]{:S(2)}) copy-start(s32[16,128]{1,0:T(8,128)} %constant.74.clone) | copy-start | bytes 24580
  21.2 22.1 %copy-start.2 = (bf16[256,1024]{1,0:T(8,128)(2,1)S(1)}, bf16[256,1024]{1,0:T(8,128)(2,1)}, u32[]{:S(2)}) copy-start(bf16[256,1024]{1,0:T(8,128)(2,1)} %v_ref.1) | copy-start | bytes 1572868
  21.2 22.1 %all-to-all-start.9 = ((bf16[16,144,128]{2,1,0:T(8,128)(2,1)}), bf16[16,144,128]{2,1,0:T(8,128)(2,1)}, u32[]{:S(2)}, u32[]{:S(2)}) async-start(bf16[16,144,128]{2,1,0:T(8,128)(2,1)} %send.1), calls=%async_computation.9 | async-start | bytes 1179648 | tf_op jit(solution)/shard_map/all_to_all | solution.py:350
  25.7 0.7 copy-start.28
  26.4 7.6 %copy-start.8 = (s32[16,128]{1,0:T(8,128)}, s32[16,128]{1,0:T(8,128)S(1)}, u32[]{:S(2)}) copy-start(s32[16,128]{1,0:T(8,128)S(1)} %get-tuple-element.337.pairs_ref) | copy-start | bytes 24580
  26.5 0.7 copy-start.29
  27.2 0.7 copy-start.1
  84.9 6.7 %copy-start.25 = (s32[16,128]{1,0:T(8,128)S(1)}, s32[16,128]{1,0:T(8,128)}, u32[]{:S(2)}) copy-start(s32[16,128]{1,0:T(8,128)} %get-tuple-element.254.mine_place_ref) | copy-start | bytes 24580 | tf_op jit(solution)/shard_map/cond
  84.9 6.7 %copy-start.27 = (s32[16,128]{1,0:T(8,128)S(1)}, s32[16,128]{1,0:T(8,128)}, u32[]{:S(2)}) copy-start(s32[16,128]{1,0:T(8,128)} %get-tuple-element.255.partner_place_ref) | copy-start | bytes 24580 | tf_op jit(solution)/shard_map/cond
  85.1 6.6 %collective-permute-start.3 = (f32[8,384]{1,0:T(8,128)S(1)}, f32[8,384]{1,0:T(8,128)S(1)}, u32[]{:S(2)}, u32[]{:S(2)}) collective-permute-start(f32[8,384]{1,0:T(8,128)S(1)} %get-tuple-element.253), channel_id=1, source_target_pairs={{0,32},{32,0},{1,33},{33,1},{2,34},{34,2},{3,35},{35,3},{4,36},{36... | collective-permute-start | bytes 36872 | tf_op jit(solution)/shard_map/cond/branch_1_fun/ppermute | solution.py:354

commit v12 on v9

--- a/solution.py
+++ b/solution.py
@@ -252,13 +252,13 @@
     wire = dense.shape[0]
     cols = wire - 1
     rows = [ref[...] for ref in held] if full else [joined_rows(held[0])]
-    for core in range(2):
-        total = None
-        for turn in range(turns):
-            part = times(rows[turn], weights[2 * turn + core][: 4 * TW, :])
-            total = part if total is None else total + part
-        for q in range(2):
-            products[2 * core + q][...] = total[:, q * 128 : (q + 1) * 128]
+    total = None
+    for turn in range(turns):
+        both_cores = [weights[2 * turn + core][: 4 * TW, :] for core in range(2)]
+        part = times(rows[turn], jnp.concatenate(both_cores, axis=0))
+        total = part if total is None else total + part
+    for q in range(4):
+        products[q][...] = total[:, q * 128 : (q + 1) * 128]
     lower = lax.broadcasted_iota(jnp.int32, (1, 128), 1) < TW
     skip = round_ref[0] * cols
     told = weights[1][4 * TW :, :].astype(jnp.float32)

time: 93.4 us -> 93.4 us (level)
  no operation moved by 1% of the time
where the time goes in v12:
time: 93.4 us; the launch traced here: 92.9 us
  blocking collectives  35.5 us (38%)
  starting transfers between devices  26.1 us (28%)
  Pallas kernels  18.7 us (20%)
  waiting for transfers between devices  7.46 us (8%)
  local copies, waits for them, and re-layouts  2.13 us (2%)
  other arithmetic  1.5 us (2%)
  between operations  1.38 us (1%)
    all_to_all x1, blocking collectives, reduced(): lax.all_to_all(partial, 'panel', split_axis=0, concat_axis=0, tiled=True)  35.5 us
    ppermute x2, starting transfers between devices, swapped(): return lax.ppermute(array, 'blk_2', [(0, 1), (1, 0)])  21.8 us
    all_to_all x1, waiting for transfers between devices, over_chips(): got = lax.all_to_all(sent, CHIPS, split_axis=0, concat_axis=0, tiled=True)  7.45 us
    pallas_call x1, Pallas kernels, body(): pl.pallas_call(list_kernel, out_shape=[shaped((LIST,), i32), shaped((4,),...  6.1 us
    pallas_call x1, Pallas kernels, products(): pl.pallas_call(functools.partial(product_kernel, full), out_shape=pltpu.V...  5.91 us
    all_to_all x1, starting transfers between devices, over_chips(): got = lax.all_to_all(sent, CHIPS, split_axis=0, concat_axis=0, tiled=True)  4.39 us
    pallas_call x1, Pallas kernels, weights(): pl.pallas_call(functools.partial(pack_rows_kernel, turn, first), out_shap...  2.24 us
    pallas_call x1, Pallas kernels, body(): pl.pallas_call(send_kernel, out_shape=shaped((SOURCES, ROWS, NARROW * TW)...  2.23 us
  transfers between devices with their start and end apart: 3, of which 1 were waited for; matrix products, arithmetic and copies ran while one was open for 2% of the time, Pallas kernels for 8%

profile of v12, /device:TPU:1, one launch (start us, length us, event | category | flops | bytes accessed | tf_op | source)
XLA Modules:
  0.0 92.9 jit_solution(11427245940805959713)
XLA Ops:
  0.0 0.7 copy-done
  0.7 2.2 %shard_map.121 = bf16[264,512]{1,0:T(8,128)(2,1)} custom-call(bf16[256,1024]{1,0:T(8,128)(2,1)} %v_ref.1, s32[4]{0:T(128)S(1)} %copy-done, s32[16]{0:T(128)} %cd_ref.5), custom_call_target="tpu_custom_call" | custom-call | tf_op jit(solution)/shard_map/pallas_call | solution.py:368
  2.9 16.0 %collective-permute-start.6 = (bf16[264,512]{1,0:T(8,128)(2,1)}, bf16[264,512]{1,0:T(8,128)(2,1)}, u32[]{:S(2)}, u32[]{:S(2)}) collective-permute-start(bf16[264,512]{1,0:T(8,128)(2,1)} %shard_map.121), channel_id=1, source_target_pairs={{0,32},{32,0},{1,33},{33,1},{2,34},{34,2},{3,35},{35,3},{4,36},{36... | collective-permute-start | bytes 811016 | tf_op jit(solution)/shard_map/ppermute | solution.py:354
  19.0 2.2 %send.1 = bf16[16,144,128]{2,1,0:T(8,128)(2,1)} custom-call(bf16[50,1024]{1,0:T(8,128)(2,1)S(1)} %copy-done.7, s32[16]{0:T(128)S(1)} %copy-done.19, s32[40]{0:T(128)S(1)} %copy-done.12), custom_call_target="tpu_custom_call" | custom-call | tf_op jit(solution)/shard_map/send/pallas_call | solution.py:378
  21.2 4.4 %all-to-all-start.9 = ((bf16[16,144,128]{2,1,0:T(8,128)(2,1)}), bf16[16,144,128]{2,1,0:T(8,128)(2,1)}, u32[]{:S(2)}, u32[]{:S(2)}) async-start(bf16[16,144,128]{2,1,0:T(8,128)(2,1)} %send.1), calls=%async_computation.9 | async-start | bytes 1179648 | tf_op jit(solution)/shard_map/all_to_all | solution.py:350
  25.6 0.1 convert_reduce_fusion.1
  25.7 0.1 select_reduce_fusion
  25.9 0.5 copy-done.26
  26.4 0.1 select_reduce_fusion.3
  26.5 0.4 convert_reduce_fusion.counts_ref
  26.9 0.1 copy-done.8
  27.0 0.2 copy-done.27
  27.2 0.7 select_reduce_fusion.2.rows_ref
  27.9 6.1 %list.1 = (s32[1408]{0:T(1024)S(1)}, s32[4]{0:T(128)S(1)}) custom-call(s32[16]{0:T(128)S(1)} %copy-done.19, s32[40]{0:T(128)S(1)} %copy-done.12, s32[16]{0:T(128)S(1)} %convert_reduce_fusion.counts_ref, s32[32]{0:T(128)S(1)} %select_reduce_fusion.2.rows_ref, s32[4]{0:T(128)S(1)} %copy-done.1), custom_call_target="tpu_custom_call" | custom-call | tf_op jit(solution)/shard_map/list/pallas_call | solution.py:411
  34.0 0.6 fusion.1
  35.9 7.5 %all-to-all-done.9 = bf16[16,144,128]{2,1,0:T(8,128)(2,1)} async-done(((bf16[16,144,128]{2,1,0:T(8,128)(2,1)}), bf16[16,144,128]{2,1,0:T(8,128)(2,1)}, u32[]{:S(2)}, u32[]{:S(2)}) %all-to-all-start.9) | async-done | bytes 589856 | tf_op jit(solution)/shard_map/all_to_all | solution.py:350
  43.3 49.6 %conditional.4 = (f32[8,1600]{1,0:T(8,128)}) conditional(s32[]{:T(128)} %bitcast.9, (pred[]{:T(512)}, bf16[2304,128]{1,0:T(8,128)(2,1)}, bf16[264,512]{1,0:T(8,128)(2,1)}, bf16[264,512]{1,0:T(8,128)(2,1)}, s32[1408]{0:T(1024)S(1)}, /*index=5*/bf16[50,1024]{1,0:T(8,128)(2,1)S(1)}, s32[16]{0:T(128)S(1)}, s32[40]{0:T(128)S(1)}, ...), branch_computations={%region_6.9_spmd, %region_9.12_spmd, %region_12.17_spmd} | conditional | flops 537100 | bytes 19476954 | solution.py:492
  43.3 5.9 %conditional.1 = (f32[32,16,384]{2,1,0:T(8,128)S(1)}) conditional(s32[]{:T(128)} %convert_element_type.25, (bf16[2304,128]{1,0:T(8,128)(2,1)}, bf16[264,512]{1,0:T(8,128)(2,1)}, bf16[264,512]{1,0:T(8,128)(2,1)}, s32[1408]{0:T(1024)S(1)}) %tuple.27, (bf16[50,1024]{1,0:T(8,128)(2,1)S(1)}, s32[16]{0:T(128)S(1)}, s32[40]{0:T(128)S(1)}, ...), branch_computations={%region_10.10_spmd, %region_11.11_spmd} | conditional | bytes 6587048 | solution.py:448
  43.3 5.9 %branch_0_fun.4 = f32[32,16,384]{2,1,0:T(8,128)S(1)} custom-call(s32[1]{0:T(128)} %constant.60.clone.round_ref, bf16[2304,128]{1,0:T(8,128)(2,1)} %get-tuple-element.229.refs_0_, bf16[264,512]{1,0:T(8,128)(2,1)} %get-tuple-element.230.refs_1_, bf16[264,512]{1,0:T(8,128)(2,1)} %get-tuple-element.231.refs_2_, s32[1408]{0:T(1024)S(1)} %get-tuple-element.232.refs_3_), custom_call_target="tpu_custom_call" | custom-call | tf_op jit(solution)/shard_map/cond/branch_1_fun/cond/branch_0_fun/pallas_call | solution.py:424
  49.3 35.5 %all_to_all.44 = f16[32,16,384]{2,1,0:T(8,128)(2,1)S(1)} all-to-all(f16[32,16,384]{2,1,0:T(8,128)(2,1)S(1)} %convert_element_type.26), channel_id=1, replica_groups=mesh['blk_0'=2,'blk_1'=8,'blk_2'=2,'panel'=32] {'panel'}, dimensions={0} | all-to-all | bytes 786432 | tf_op jit(solution)/shard_map/cond/branch_1_fun/all_to_all | solution.py:453
  84.9 0.1 sum.4
  85.0 5.8 %collective-permute-start.3 = (f32[8,384]{1,0:T(8,128)S(1)}, f32[8,384]{1,0:T(8,128)S(1)}, u32[]{:S(2)}, u32[]{:S(2)}) collective-permute-start(f32[8,384]{1,0:T(8,128)S(1)} %get-tuple-element.250), channel_id=1, source_target_pairs={{0,32},{32,0},{1,33},{33,1},{2,34},{34,2},{3,35},{35,3},{4,36},{36... | collective-permute-start | bytes 36872 | tf_op jit(solution)/shard_map/cond/branch_1_fun/ppermute | solution.py:354
  90.8 1.2 %places.4 = (s32[16,128]{1,0:T(8,128)S(1)}, s32[16,128]{1,0:T(8,128)S(1)}) custom-call(s32[1]{0:T(128)} %constant.62.clone.round_ref, s32[1408]{0:T(1024)S(1)} %get-tuple-element.244.list_ref, s32[16,128]{1,0:T(8,128)S(1)} %copy-done.10), custom_call_target="tpu_custom_call" | custom-call | tf_op jit(solution)/shard_map/cond/branch_1_fun/places/pallas_call | solution.py:462
  92.0 0.9 finish.4
  (26 shorter events, 0.2 us)
Async XLA Ops:
  0.0 0.7 copy-start
  0.7 18.3 %copy-start.7 = (bf16[50,1024]{1,0:T(8,128)(2,1)S(1)}, bf16[50,1024]{1,0:T(8,128)(2,1)}, u32[]{:S(2)}) copy-start(bf16[50,1024]{1,0:T(8,128)(2,1)} %t_ref.1) | copy-start | bytes 307204
  0.7 18.3 %copy-start.12 = (s32[40]{0:T(128)S(1)}, s32[40]{0:T(128)}, u32[]{:S(2)}) copy-start(s32[40]{0:T(128)} %occ_ref.3) | copy-start | bytes 484
  0.7 18.3 %copy-start.19 = (s32[16]{0:T(128)S(1)}, s32[16]{0:T(128)}, u32[]{:S(2)}) copy-start(s32[16]{0:T(128)} %cd_ref.5) | copy-start | bytes 196
  2.9 32.9 %collective-permute-start.6 = (bf16[264,512]{1,0:T(8,128)(2,1)}, bf16[264,512]{1,0:T(8,128)(2,1)}, u32[]{:S(2)}, u32[]{:S(2)}) collective-permute-start(bf16[264,512]{1,0:T(8,128)(2,1)} %shard_map.121), channel_id=1, source_target_pairs={{0,32},{32,0},{1,33},{33,1},{2,34},{34,2},{3,35},{35,3},{4,36},{36... | collective-permute-start | bytes 811016 | tf_op jit(solution)/shard_map/ppermute | solution.py:354
  21.2 4.5 %copy-start.28 = (s32[16,128]{1,0:T(8,128)S(1)}, s32[16,128]{1,0:T(8,128)}, u32[]{:S(2)}) copy-start(s32[16,128]{1,0:T(8,128)} %constant.76.clone) | copy-start | bytes 24580
  21.2 4.5 %copy-start.29 = (s32[16,128]{1,0:T(8,128)S(1)}, s32[16,128]{1,0:T(8,128)}, u32[]{:S(2)}) copy-start(s32[16,128]{1,0:T(8,128)} %constant.77.clone) | copy-start | bytes 24580
  21.2 22.1 %copy-start.2 = (bf16[256,1024]{1,0:T(8,128)(2,1)S(1)}, bf16[256,1024]{1,0:T(8,128)(2,1)}, u32[]{:S(2)}) copy-start(bf16[256,1024]{1,0:T(8,128)(2,1)} %v_ref.1) | copy-start | bytes 1572868
  21.2 22.1 %all-to-all-start.9 = ((bf16[16,144,128]{2,1,0:T(8,128)(2,1)}), bf16[16,144,128]{2,1,0:T(8,128)(2,1)}, u32[]{:S(2)}, u32[]{:S(2)}) async-start(bf16[16,144,128]{2,1,0:T(8,128)(2,1)} %send.1), calls=%async_computation.9 | async-start | bytes 1179648 | tf_op jit(solution)/shard_map/all_to_all | solution.py:350
  25.7 0.7 copy-start.26
  26.4 0.6 copy-start.8
  26.5 0.7 copy-start.27
  27.2 0.7 copy-start.1
  84.9 5.9 %copy-start.10 = (s32[16,128]{1,0:T(8,128)S(1)}, s32[16,128]{1,0:T(8,128)}, u32[]{:S(2)}) copy-start(s32[16,128]{1,0:T(8,128)} %get-tuple-element.251.pairs_ref) | copy-start | bytes 24580 | tf_op jit(solution)/shard_map/cond
  85.0 7.0 %collective-permute-start.3 = (f32[8,384]{1,0:T(8,128)S(1)}, f32[8,384]{1,0:T(8,128)S(1)}, u32[]{:S(2)}, u32[]{:S(2)}) collective-permute-start(f32[8,384]{1,0:T(8,128)S(1)} %get-tuple-element.250), channel_id=1, source_target_pairs={{0,32},{32,0},{1,33},{33,1},{2,34},{34,2},{3,35},{35,3},{4,36},{36... | collective-permute-start | bytes 36872 | tf_op jit(solution)/shard_map/cond/branch_1_fun/ppermute | solution.py:354
